TPU v7x, 512 devices: a whole 4x8x8 slice. The times are simulated.
512 devices in a mesh: tok: 8 (over z), row: 8 (over y_hi, core), col: 8 (over x, y_lo).
Axes of the slice: x: 4, y: 8 (y_hi: 4, y_lo: 2; y = y_hi * 2 + y_lo), z: 8, core: 2. Of those that a mesh axis runs over, the one named last changes fastest.
Arguments:
- activations: bfloat16 [2048, 8192], P('tok', 'row'), may hold values from -8 to 8
- gradients: bfloat16 [2048, 8192], P('tok', 'col'), may hold values from -8 to 8
- act_basis: bfloat16 [8192, 8192], P('row', ('tok', 'col')), may hold values from -1 to 1
- grad_basis: bfloat16 [8192, 8192], P('col', 'row'), may hold values from -1 to 1
- eigen_noise: float32 [8192, 8192], P('row', ('tok', 'col')), may hold values from -6 to 6
Outputs:
- scales: float32 [8192, 8192], P('row', ('tok', 'col'))
- output_shift: bfloat16 [2048, 8192], P('tok', 'col')
All inputs are finite; a program needn't handle non-finite values.
Results may differ from a plain program's by a relative error of at most 0.0064.
Values may be sent and summed in bfloat16 or wider, within the bound.
No kernel may reach another device: no remote copies, remote signals or barrier semaphores. Data moves between devices by JAX's collectives and lax.ppermute only.
A program may use at most 64 MiB of HBM per device.

v0:
```python
import jax
import jax.numpy as jnp
from jax import lax
from jax.sharding import Mesh, PartitionSpec as P

damping = 0.1
narrow = jnp.bfloat16
wide = jnp.float32
row = ("yh", "core")
col = ("x", "yl")


def contract(former, latter, former_dim, latter_dim):
    return lax.dot_general(
        former,
        latter,
        (((former_dim,), (latter_dim,)), ((), ())),
        preferred_element_type=wide,
    )


def exchange(blocks, axes):
    return lax.all_to_all(blocks, axes, 0, 0, tiled=True)


def spread(block, axes):
    members = lax.axis_size(axes)
    copies = jnp.broadcast_to(block[None], (members, *block.shape))
    return exchange(copies.reshape(members * block.shape[0], *block.shape[1:]), axes)


def scatter_sum(partial, axes):
    members = lax.axis_size(axes)
    parts = exchange(partial.astype(narrow), axes)
    parts = parts.reshape(members, parts.shape[0] // members, *parts.shape[1:])
    return jnp.sum(parts.astype(wide), axis=0)


def pick(blocks, index, axis):
    return lax.dynamic_index_in_dim(blocks, index, axis, keepdims=False)


def shifted(block, axis, step):
    members = lax.axis_size(axis)
    return lax.ppermute(block, axis, [(i, (i + step) % members) for i in range(members)])


def pair_sum(partial, axis):
    half = partial.reshape(4, 2, partial.shape[0] // 8, partial.shape[1])
    mine = lax.axis_index(axis)
    theirs = shifted(pick(half, 1 - mine, 1).astype(narrow), axis, 1)
    return pick(half, mine, 1) + theirs.astype(wide)


def ring_sum(halves, axis):
    mine = lax.axis_index(axis)
    sent = halves.astype(narrow)
    total = pick(halves, mine, 0)
    for step in range(1, 4):
        total = total + shifted(pick(sent, (mine + step) % 4, 0), axis, step).astype(wide)
    return total


def gather_by_permutes(block, axis):
    members = lax.axis_size(axis)
    mine = lax.axis_index(axis)
    behind = [block] + [shifted(block, axis, step) for step in range(1, members)]
    placed = [lax.select_n((mine - place) % members, *behind) for place in range(members)]
    return lax.optimization_barrier(jnp.concatenate(placed, axis=0))


def plan(activations, gradients, act_basis, grad_basis, eigen_noise):
    token_count = activations.shape[0] * lax.axis_size("tok")
    slab = activations.shape[0] // lax.axis_size("x")

    own_rows = lax.dynamic_slice_in_dim(activations, lax.axis_index("x") * slab, slab, 0)
    act_rows = spread(own_rows, "tok")
    basis_t = gather_by_permutes(act_basis.T, "x")

    grad_part = contract(gradients, grad_basis, 1, 0)
    grad_half = ring_sum(grad_part.reshape(4, slab, grad_part.shape[1]), "x")
    grad_proj = grad_half + shifted(grad_half.astype(narrow), "yl", 1).astype(wide)
    grad_sq = (grad_proj * grad_proj).astype(narrow)

    act_halves = pair_sum(contract(act_rows, basis_t, 1, 1), "core")
    act_proj = ring_sum(act_halves, "yh")
    grad_sq = spread(grad_sq, "tok")
    act_half = lax.all_gather(act_proj.astype(narrow), row, axis=0, tiled=True)
    act_wide = act_half.astype(wide)
    act_sq = (act_wide * act_wide).astype(narrow)

    scales_t = scatter_sum(contract(act_sq, grad_sq, 0, 0), "x") / token_count
    scaled_t = (eigen_noise.T * lax.rsqrt(token_count * (scales_t + damping))).astype(narrow)
    widened_t = spread(scaled_t, "x")

    hidden = scatter_sum(contract(act_half, widened_t, 1, 0), ("tok", "yl")).astype(narrow)
    hidden = spread(hidden, col)
    halves = pair_sum(contract(hidden, grad_basis, 1, 1), "core")
    shift = scatter_sum(halves, "yh")[0].astype(narrow)
    output_shift = lax.all_gather(shift, row, axis=0, tiled=True)
    return (scales_t.T, output_shift)


def solution(mesh):
    fine = Mesh(mesh.devices.reshape(8, 4, 2, 4, 2), ("tok", "yh", "core", "x", "yl"))
    in_specs = (
        P("tok", row),
        P("tok", col),
        P(row, ("tok", *col)),
        P(col, row),
        P(row, ("tok", *col)),
    )
    out_specs = (P(row, ("tok", *col)), P("tok", col))
    return jax.shard_map(plan, mesh=fine, in_specs=in_specs, out_specs=out_specs, check_vma=False)
```

profile of v0, /device:TPU:1, one launch (start us, length us, event | category | flops | bytes accessed | tf_op | source)
XLA Modules:
  0.0 229.5 jit_solution(10306752577301314140)
XLA Ops:
  0.6 0.0 copy-start
  0.7 1.1 constant_dynamic-slice_fusion
  1.7 1.1 broadcast_in_dim.8
  2.8 10.9 %all-to-all-start = ((bf16[8,64,1024]{2,1,0:T(8,128)(2,1)}), bf16[8,64,1024]{2,1,0:T(8,128)(2,1)}, u32[]{:S(2)}, u32[]{:S(2)}) async-start(bf16[8,64,1024]{2,1,0:T(8,128)(2,1)} %broadcast_in_dim.8), calls=%async_computation | async-start | bytes 2097152 | tf_op jit(solution)/shard_map/all_to_all | solution.py:23
  13.7 1.7 fusion.15
  15.4 0.9 convert_element_type.90
  16.3 1.8 dynamic-slice_bitcast_fusion.2
  18.1 3.1 %collective-permute-start.7 = (bf16[64,1024]{1,0:T(8,128)(2,1)}, bf16[64,1024]{1,0:T(8,128)(2,1)S(1)}, u32[]{:S(2)}, u32[]{:S(2)}) collective-permute-start(bf16[64,1024]{1,0:T(8,128)(2,1)} %get-tuple-element.12), channel_id=1, source_target_pairs={{0,2},{2,4},{4,6},{6,0},{1,3},{3,5},{5,7},{7,1},{8,10},{10,12},{12... | collective-permute-start | bytes 393224 | tf_op jit(solution)/shard_map/ppermute | solution.py:45
  21.2 4.4 %collective-permute-start.8 = (bf16[64,1024]{1,0:T(8,128)(2,1)}, bf16[64,1024]{1,0:T(8,128)(2,1)S(1)}, u32[]{:S(2)}, u32[]{:S(2)}) collective-permute-start(bf16[64,1024]{1,0:T(8,128)(2,1)} %get-tuple-element.14), channel_id=1, source_target_pairs={{0,4},{2,6},{4,0},{6,2},{1,5},{3,7},{5,1},{7,3},{8,12},{10,14},{12... | collective-permute-start | bytes 393224 | tf_op jit(solution)/shard_map/ppermute | solution.py:45
  25.5 3.1 %collective-permute-start.9 = (bf16[64,1024]{1,0:T(8,128)(2,1)}, bf16[64,1024]{1,0:T(8,128)(2,1)S(1)}, u32[]{:S(2)}, u32[]{:S(2)}) collective-permute-start(bf16[64,1024]{1,0:T(8,128)(2,1)} %get-tuple-element.13), channel_id=1, source_target_pairs={{0,6},{2,0},{4,2},{6,4},{1,7},{3,1},{5,3},{7,5},{8,14},{10,8},{12,... | collective-permute-start | bytes 393224 | tf_op jit(solution)/shard_map/ppermute | solution.py:45
  28.6 0.0 collective-permute-done.7
  28.6 0.7 collective-permute-done.8
  29.4 2.5 %collective-permute-done.9 = bf16[64,1024]{1,0:T(8,128)(2,1)S(1)} collective-permute-done((bf16[64,1024]{1,0:T(8,128)(2,1)}, bf16[64,1024]{1,0:T(8,128)(2,1)S(1)}, u32[]{:S(2)}, u32[]{:S(2)}) %collective-permute-start.9) | collective-permute-done | bytes 131104 | tf_op jit(solution)/shard_map/ppermute | solution.py:45
  31.9 0.7 fusion.13
  32.6 3.2 %collective-permute-start.10 = (bf16[64,1024]{1,0:T(8,128)(2,1)}, bf16[64,1024]{1,0:T(8,128)(2,1)}, u32[]{:S(2)}, u32[]{:S(2)}) collective-permute-start(bf16[64,1024]{1,0:T(8,128)(2,1)} %fusion.13), channel_id=1, source_target_pairs={{0,1},{1,0},{2,3},{3,2},{4,5},{5,4},{6,7},{7,6},{8,9},{9,8},{10,11... | collective-permute-start | bytes 393224 | tf_op jit(solution)/shard_map/ppermute | solution.py:45
  35.8 3.5 %collective-permute-start = (bf16[128,1024]{0,1:T(8,128)(2,1)}, bf16[128,1024]{0,1:T(8,128)(2,1)}, u32[]{:S(2)}, u32[]{:S(2)}) collective-permute-start(bf16[128,1024]{0,1:T(8,128)(2,1)} %bitcast.82), channel_id=1, source_target_pairs={{0,2},{2,4},{4,6},{6,0},{1,3},{3,5},{5,7},{7,1},{8,10},{10,12},{12... | collective-permute-start | bytes 786440 | tf_op jit(solution)/shard_map/ppermute | solution.py:45
  39.3 3.8 %collective-permute-start.1 = (bf16[128,1024]{0,1:T(8,128)(2,1)}, bf16[128,1024]{0,1:T(8,128)(2,1)}, u32[]{:S(2)}, u32[]{:S(2)}) collective-permute-start(bf16[128,1024]{0,1:T(8,128)(2,1)} %bitcast.83), channel_id=1, source_target_pairs={{0,4},{2,6},{4,0},{6,2},{1,5},{3,7},{5,1},{7,3},{8,12},{10,14},{12... | collective-permute-start | bytes 786440 | tf_op jit(solution)/shard_map/ppermute | solution.py:45
  43.2 2.7 %collective-permute-start.2 = (bf16[128,1024]{0,1:T(8,128)(2,1)}, bf16[128,1024]{0,1:T(8,128)(2,1)}, u32[]{:S(2)}, u32[]{:S(2)}) collective-permute-start(bf16[128,1024]{0,1:T(8,128)(2,1)} %bitcast.84), channel_id=1, source_target_pairs={{0,6},{2,0},{4,2},{6,4},{1,7},{3,1},{5,3},{7,5},{8,14},{10,8},{12,... | collective-permute-start | bytes 786440 | tf_op jit(solution)/shard_map/ppermute | solution.py:45
  46.0 0.0 collective-permute-done.10
  46.0 1.1 multiply_convert_fusion.2
  47.1 0.0 copy-start.5
  47.1 0.0 all-to-all-done
  47.1 1.1 broadcast_in_dim.9
  48.2 6.6 %all-to-all-start.1 = ((bf16[8,64,1024]{2,1,0:T(8,128)(2,1)}), bf16[8,64,1024]{2,1,0:T(8,128)(2,1)S(1)}, u32[]{:S(2)}, u32[]{:S(2)}) async-start(bf16[8,64,1024]{2,1,0:T(8,128)(2,1)} %broadcast_in_dim.9), calls=%async_computation.1 | async-start | bytes 2097152 | tf_op jit(solution)/shard_map/all_to_all | solution.py:23
  54.8 0.0 collective-permute-done
  54.8 0.0 collective-permute-done.1
  54.8 0.0 collective-permute-done.2
  54.8 1.2 select_select_fusion.3
  56.1 0.1 pad_maximum_fusion
  56.2 1.9 fusion.2
  58.1 1.0 copy-done.2
  59.2 5.1 %collective-permute-start.3 = (bf16[4,64,512]{2,1,0:T(8,128)(2,1)S(1)}, bf16[4,64,512]{2,1,0:T(8,128)(2,1)}, u32[]{:S(2)}, u32[]{:S(2)}) collective-permute-start(bf16[4,64,512]{2,1,0:T(8,128)(2,1)S(1)} %fusion.6), channel_id=1, source_target_pairs={{0,8},{8,0},{1,9},{9,1},{2,10},{10,2},{3,11},{11,3},{4,12},{12,4},... | collective-permute-start | bytes 786440 | tf_op jit(solution)/shard_map/ppermute | solution.py:45
  64.3 1.2 collective-permute-done.3
  65.5 2.0 fusion.14
  67.5 4.2 %collective-permute-start.4 = (bf16[64,512]{1,0:T(8,128)(2,1)S(1)}, bf16[64,512]{1,0:T(8,128)(2,1)S(1)}, u32[]{:S(2)}, u32[]{:S(2)}) collective-permute-start(bf16[64,512]{1,0:T(8,128)(2,1)S(1)} %get-tuple-element.15), channel_id=1, source_target_pairs={{0,16},{16,32},{32,48},{48,0},{1,17},{17,33},{33,49},{49,1},{2,18}... | collective-permute-start | bytes 196616 | tf_op jit(solution)/shard_map/ppermute | solution.py:45
  71.8 4.8 %collective-permute-start.5 = (bf16[64,512]{1,0:T(8,128)(2,1)S(1)}, bf16[64,512]{1,0:T(8,128)(2,1)S(1)}, u32[]{:S(2)}, u32[]{:S(2)}) collective-permute-start(bf16[64,512]{1,0:T(8,128)(2,1)S(1)} %get-tuple-element.17), channel_id=1, source_target_pairs={{0,32},{16,48},{32,0},{48,16},{1,33},{17,49},{33,1},{49,17},{2,34}... | collective-permute-start | bytes 196616 | tf_op jit(solution)/shard_map/ppermute | solution.py:45
  76.5 5.0 %collective-permute-start.6 = (bf16[64,512]{1,0:T(8,128)(2,1)S(1)}, bf16[64,512]{1,0:T(8,128)(2,1)S(1)}, u32[]{:S(2)}, u32[]{:S(2)}) collective-permute-start(bf16[64,512]{1,0:T(8,128)(2,1)S(1)} %get-tuple-element.16), channel_id=1, source_target_pairs={{0,48},{16,0},{32,16},{48,32},{1,49},{17,1},{33,17},{49,33},{2,50}... | collective-permute-start | bytes 196616 | tf_op jit(solution)/shard_map/ppermute | solution.py:45
  81.5 0.0 collective-permute-done.4
  81.5 2.0 collective-permute-done.5
  83.5 0.9 fusion.12
  84.5 19.1 %all_gather.6 = bf16[512,512]{1,0:T(8,128)(2,1)} all-gather(bf16[64,512]{1,0:T(8,128)(2,1)S(1)} %fusion.12), channel_id=1, replica_groups=mesh['tok'=8,'yh'=4,'core'=2,'x'=4,'yl'=2] {'yh','core'}, dimensions={0}, use_global_device_ids=true | all-gather | bytes 589824 | tf_op jit(solution)/shard_map/all_gather | solution.py:88
  103.5 0.0 all-to-all-done.1
  103.5 2.8 %convolution_convert_fusion.1 = bf16[512,1024]{1,0:T(8,128)(2,1)} fusion(bf16[512,1024]{1,0:T(8,128)(2,1)S(1)} %bitcast.77, bf16[512,512]{1,0:T(8,128)(2,1)} %all_gather.6), kind=kOutput, calls=%fused_computation.4 | convolution fusion | flops 538181632 | bytes 2621440 | tf_op jit(solution)/shard_map/dot_general | solution.py:14
  106.3 3.5 %all-to-all-start.2 = ((bf16[4,128,1024]{2,1,0:T(8,128)(2,1)}), bf16[4,128,1024]{2,1,0:T(8,128)(2,1)S(1)}, u32[]{:S(2)}, u32[]{:S(2)}) async-start(bf16[4,128,1024]{2,1,0:T(8,128)(2,1)} %bitcast.78), calls=%async_computation.2 | async-start | bytes 2097152 | tf_op jit(solution)/shard_map/all_to_all | solution.py:23
  109.8 2.0 copy.10
  111.9 13.0 %all-to-all-done.2 = bf16[4,128,1024]{2,1,0:T(8,128)(2,1)S(1)} async-done(((bf16[4,128,1024]{2,1,0:T(8,128)(2,1)}), bf16[4,128,1024]{2,1,0:T(8,128)(2,1)S(1)}, u32[]{:S(2)}, u32[]{:S(2)}) %all-to-all-start.2) | async-done | bytes 1048608 | tf_op jit(solution)/shard_map/all_to_all | solution.py:23
  124.8 0.2 convert_reduce_fusion
  125.0 1.9 fusion.5
  127.0 0.1 broadcast_in_dim.10
  127.1 16.7 %all_to_all.53 = bf16[4,128,1024]{2,1,0:T(8,128)(2,1)S(1)} all-to-all(bf16[4,128,1024]{2,1,0:T(8,128)(2,1)S(1)} %broadcast_in_dim.10), channel_id=1, replica_groups=mesh['tok'=8,'yh'=4,'core'=2,'x'=4,'yl'=2] {'x'}, dimensions={0} | all-to-all | bytes 2097152 | tf_op jit(solution)/shard_map/all_to_all | solution.py:23
  143.8 0.7 convolution_convert_fusion
  144.5 33.2 %all_to_all.54 = bf16[16,32,1024]{2,1,0:T(8,128)(2,1)S(1)} all-to-all(bf16[16,32,1024]{2,1,0:T(8,128)(2,1)S(1)} %bitcast.80), channel_id=1, replica_groups=mesh['tok'=8,'yh'=4,'core'=2,'x'=4,'yl'=2] {'tok','yl'}, dimensions={0} | all-to-all | bytes 2097152 | tf_op jit(solution)/shard_map/all_to_all | solution.py:23
  177.7 0.2 reduce_sum.34
  177.9 0.1 broadcast_in_dim.11
  178.0 12.8 %all_to_all.55 = bf16[8,32,1024]{2,1,0:T(8,128)(2,1)S(1)} all-to-all(bf16[8,32,1024]{2,1,0:T(8,128)(2,1)S(1)} %broadcast_in_dim.11), channel_id=1, replica_groups=mesh['tok'=8,'yh'=4,'core'=2,'x'=4,'yl'=2] {'x','yl'}, dimensions={0} | all-to-all | bytes 1048576 | tf_op jit(solution)/shard_map/all_to_all | solution.py:23
  190.8 0.7 fusion
  191.5 4.4 %collective-permute-start.11 = (bf16[4,32,1024]{2,1,0:T(8,128)(2,1)S(1)}, bf16[4,32,1024]{2,1,0:T(8,128)(2,1)S(1)}, u32[]{:S(2)}, u32[]{:S(2)}) collective-permute-start(bf16[4,32,1024]{2,1,0:T(8,128)(2,1)S(1)} %fusion.7), channel_id=1, source_target_pairs={{0,8},{8,0},{1,9},{9,1},{2,10},{10,2},{3,11},{11,3},{4,12},{12,4},... | collective-permute-start | bytes 786440 | tf_op jit(solution)/shard_map/ppermute | solution.py:45
  195.9 1.1 collective-permute-done.11
  197.1 0.8 fusion.4
  197.8 4.5 %all-to-all-start.6 = ((bf16[4,32,1024]{2,1,0:T(8,128)(2,1)}), bf16[4,32,1024]{2,1,0:T(8,128)(2,1)S(1)}, u32[]{:S(2)}, u32[]{:S(2)}) async-start(bf16[4,32,1024]{2,1,0:T(8,128)(2,1)} %fusion.4), calls=%async_computation.6 | async-start | bytes 524288 | tf_op jit(solution)/shard_map/all_to_all | solution.py:23
  202.3 1.0 copy.11
  203.3 7.7 %all-to-all-done.6 = bf16[4,32,1024]{2,1,0:T(8,128)(2,1)S(1)} async-done(((bf16[4,32,1024]{2,1,0:T(8,128)(2,1)}), bf16[4,32,1024]{2,1,0:T(8,128)(2,1)S(1)}, u32[]{:S(2)}, u32[]{:S(2)}) %all-to-all-start.6) | async-done | bytes 262176 | tf_op jit(solution)/shard_map/all_to_all | solution.py:23
  211.0 17.7 %all_gather.7 = bf16[256,1024]{1,0:T(8,128)(2,1)S(1)} all-gather(bf16[32,1024]{1,0:T(8,128)(2,1)S(1)} %reduce_sum.35), channel_id=1, replica_groups=mesh['tok'=8,'yh'=4,'core'=2,'x'=4,'yl'=2] {'yh','core'}, dimensions={0}, use_global_device_ids=true | all-gather | bytes 589824 | tf_op jit(solution)/shard_map/all_gather | solution.py:100
  228.7 0.8 copy.16
  (14 shorter events, 0.1 us)
Async XLA Ops:
  0.6 13.0 %copy-start = (bf16[1024,1024]{1,0:T(8,128)(2,1)S(1)}, bf16[1024,1024]{1,0:T(8,128)(2,1)}, u32[]{:S(2)}) copy-start(bf16[1024,1024]{1,0:T(8,128)(2,1)} %param.8) | copy-start | bytes 6291460
  2.8 44.3 %all-to-all-start = ((bf16[8,64,1024]{2,1,0:T(8,128)(2,1)}), bf16[8,64,1024]{2,1,0:T(8,128)(2,1)}, u32[]{:S(2)}, u32[]{:S(2)}) async-start(bf16[8,64,1024]{2,1,0:T(8,128)(2,1)} %broadcast_in_dim.8), calls=%async_computation | async-start | bytes 2097152 | tf_op jit(solution)/shard_map/all_to_all | solution.py:23
  18.1 10.6 %collective-permute-start.7 = (bf16[64,1024]{1,0:T(8,128)(2,1)}, bf16[64,1024]{1,0:T(8,128)(2,1)S(1)}, u32[]{:S(2)}, u32[]{:S(2)}) collective-permute-start(bf16[64,1024]{1,0:T(8,128)(2,1)} %get-tuple-element.12), channel_id=1, source_target_pairs={{0,2},{2,4},{4,6},{6,0},{1,3},{3,5},{5,7},{7,1},{8,10},{10,12},{12... | collective-permute-start | bytes 393224 | tf_op jit(solution)/shard_map/ppermute | solution.py:45
  21.2 8.2 %collective-permute-start.8 = (bf16[64,1024]{1,0:T(8,128)(2,1)}, bf16[64,1024]{1,0:T(8,128)(2,1)S(1)}, u32[]{:S(2)}, u32[]{:S(2)}) collective-permute-start(bf16[64,1024]{1,0:T(8,128)(2,1)} %get-tuple-element.14), channel_id=1, source_target_pairs={{0,4},{2,6},{4,0},{6,2},{1,5},{3,7},{5,1},{7,3},{8,12},{10,14},{12... | collective-permute-start | bytes 393224 | tf_op jit(solution)/shard_map/ppermute | solution.py:45
  25.5 6.3 %collective-permute-start.9 = (bf16[64,1024]{1,0:T(8,128)(2,1)}, bf16[64,1024]{1,0:T(8,128)(2,1)S(1)}, u32[]{:S(2)}, u32[]{:S(2)}) collective-permute-start(bf16[64,1024]{1,0:T(8,128)(2,1)} %get-tuple-element.13), channel_id=1, source_target_pairs={{0,6},{2,0},{4,2},{6,4},{1,7},{3,1},{5,3},{7,5},{8,14},{10,8},{12,... | collective-permute-start | bytes 393224 | tf_op jit(solution)/shard_map/ppermute | solution.py:45
  31.9 14.1 %copy-start.4 = (bf16[64,1024]{1,0:T(8,128)(2,1)}, bf16[64,1024]{1,0:T(8,128)(2,1)S(1)}, u32[]{:S(2)}) copy-start(bf16[64,1024]{1,0:T(8,128)(2,1)S(1)} %collective-permute-done.9) | copy-start | bytes 393220
  32.6 13.4 %collective-permute-start.10 = (bf16[64,1024]{1,0:T(8,128)(2,1)}, bf16[64,1024]{1,0:T(8,128)(2,1)}, u32[]{:S(2)}, u32[]{:S(2)}) collective-permute-start(bf16[64,1024]{1,0:T(8,128)(2,1)} %fusion.13), channel_id=1, source_target_pairs={{0,1},{1,0},{2,3},{3,2},{4,5},{5,4},{6,7},{7,6},{8,9},{9,8},{10,11... | collective-permute-start | bytes 393224 | tf_op jit(solution)/shard_map/ppermute | solution.py:45
  35.8 19.0 %collective-permute-start = (bf16[128,1024]{0,1:T(8,128)(2,1)}, bf16[128,1024]{0,1:T(8,128)(2,1)}, u32[]{:S(2)}, u32[]{:S(2)}) collective-permute-start(bf16[128,1024]{0,1:T(8,128)(2,1)} %bitcast.82), channel_id=1, source_target_pairs={{0,2},{2,4},{4,6},{6,0},{1,3},{3,5},{5,7},{7,1},{8,10},{10,12},{12... | collective-permute-start | bytes 786440 | tf_op jit(solution)/shard_map/ppermute | solution.py:45
  39.3 15.5 %collective-permute-start.1 = (bf16[128,1024]{0,1:T(8,128)(2,1)}, bf16[128,1024]{0,1:T(8,128)(2,1)}, u32[]{:S(2)}, u32[]{:S(2)}) collective-permute-start(bf16[128,1024]{0,1:T(8,128)(2,1)} %bitcast.83), channel_id=1, source_target_pairs={{0,4},{2,6},{4,0},{6,2},{1,5},{3,7},{5,1},{7,3},{8,12},{10,14},{12... | collective-permute-start | bytes 786440 | tf_op jit(solution)/shard_map/ppermute | solution.py:45
  43.2 11.6 %collective-permute-start.2 = (bf16[128,1024]{0,1:T(8,128)(2,1)}, bf16[128,1024]{0,1:T(8,128)(2,1)}, u32[]{:S(2)}, u32[]{:S(2)}) collective-permute-start(bf16[128,1024]{0,1:T(8,128)(2,1)} %bitcast.84), channel_id=1, source_target_pairs={{0,6},{2,0},{4,2},{6,4},{1,7},{3,1},{5,3},{7,5},{8,14},{10,8},{12,... | collective-permute-start | bytes 786440 | tf_op jit(solution)/shard_map/ppermute | solution.py:45
  47.1 7.7 %copy-start.5 = (bf16[1024,128]{1,0:T(8,128)(2,1)S(1)}, bf16[1024,128]{1,0:T(8,128)(2,1)}, u32[]{:S(2)}) copy-start(bf16[1024,128]{1,0:T(8,128)(2,1)} %param.7) | copy-start | bytes 786436
  48.2 55.3 %all-to-all-start.1 = ((bf16[8,64,1024]{2,1,0:T(8,128)(2,1)}), bf16[8,64,1024]{2,1,0:T(8,128)(2,1)S(1)}, u32[]{:S(2)}, u32[]{:S(2)}) async-start(bf16[8,64,1024]{2,1,0:T(8,128)(2,1)} %broadcast_in_dim.9), calls=%async_computation.1 | async-start | bytes 2097152 | tf_op jit(solution)/shard_map/all_to_all | solution.py:23
  58.1 1.0 copy-start.2
  59.2 6.3 %collective-permute-start.3 = (bf16[4,64,512]{2,1,0:T(8,128)(2,1)S(1)}, bf16[4,64,512]{2,1,0:T(8,128)(2,1)}, u32[]{:S(2)}, u32[]{:S(2)}) collective-permute-start(bf16[4,64,512]{2,1,0:T(8,128)(2,1)S(1)} %fusion.6), channel_id=1, source_target_pairs={{0,8},{8,0},{1,9},{9,1},{2,10},{10,2},{3,11},{11,3},{4,12},{12,4},... | collective-permute-start | bytes 786440 | tf_op jit(solution)/shard_map/ppermute | solution.py:45
  67.5 14.0 %collective-permute-start.4 = (bf16[64,512]{1,0:T(8,128)(2,1)S(1)}, bf16[64,512]{1,0:T(8,128)(2,1)S(1)}, u32[]{:S(2)}, u32[]{:S(2)}) collective-permute-start(bf16[64,512]{1,0:T(8,128)(2,1)S(1)} %get-tuple-element.15), channel_id=1, source_target_pairs={{0,16},{16,32},{32,48},{48,0},{1,17},{17,33},{33,49},{49,1},{2,18}... | collective-permute-start | bytes 196616 | tf_op jit(solution)/shard_map/ppermute | solution.py:45
  71.8 11.8 %collective-permute-start.5 = (bf16[64,512]{1,0:T(8,128)(2,1)S(1)}, bf16[64,512]{1,0:T(8,128)(2,1)S(1)}, u32[]{:S(2)}, u32[]{:S(2)}) collective-permute-start(bf16[64,512]{1,0:T(8,128)(2,1)S(1)} %get-tuple-element.17), channel_id=1, source_target_pairs={{0,32},{16,48},{32,0},{48,16},{1,33},{17,49},{33,1},{49,17},{2,34}... | collective-permute-start | bytes 196616 | tf_op jit(solution)/shard_map/ppermute | solution.py:45
  76.5 7.0 %collective-permute-start.6 = (bf16[64,512]{1,0:T(8,128)(2,1)S(1)}, bf16[64,512]{1,0:T(8,128)(2,1)S(1)}, u32[]{:S(2)}, u32[]{:S(2)}) collective-permute-start(bf16[64,512]{1,0:T(8,128)(2,1)S(1)} %get-tuple-element.16), channel_id=1, source_target_pairs={{0,48},{16,0},{32,16},{48,32},{1,49},{17,1},{33,17},{49,33},{2,50}... | collective-permute-start | bytes 196616 | tf_op jit(solution)/shard_map/ppermute | solution.py:45
  106.3 18.5 %all-to-all-start.2 = ((bf16[4,128,1024]{2,1,0:T(8,128)(2,1)}), bf16[4,128,1024]{2,1,0:T(8,128)(2,1)S(1)}, u32[]{:S(2)}, u32[]{:S(2)}) async-start(bf16[4,128,1024]{2,1,0:T(8,128)(2,1)} %bitcast.78), calls=%async_computation.2 | async-start | bytes 2097152 | tf_op jit(solution)/shard_map/all_to_all | solution.py:23
  127.0 16.9 %copy-start.3 = (bf16[512,512]{1,0:T(8,128)(2,1)S(1)}, bf16[512,512]{1,0:T(8,128)(2,1)}, u32[]{:S(2)}) copy-start(bf16[512,512]{1,0:T(8,128)(2,1)} %all_gather.6) | copy-start | bytes 1572868
  190.7 11.6 %copy-start.1 = (f32[1024,128]{0,1:T(8,128)S(1)}, f32[1024,128]{0,1:T(8,128)}, u32[]{:S(2)}) copy-start(f32[1024,128]{0,1:T(8,128)} %get-tuple-element.11) | copy-start | bytes 1572868
  191.5 5.5 %collective-permute-start.11 = (bf16[4,32,1024]{2,1,0:T(8,128)(2,1)S(1)}, bf16[4,32,1024]{2,1,0:T(8,128)(2,1)S(1)}, u32[]{:S(2)}, u32[]{:S(2)}) collective-permute-start(bf16[4,32,1024]{2,1,0:T(8,128)(2,1)S(1)} %fusion.7), channel_id=1, source_target_pairs={{0,8},{8,0},{1,9},{9,1},{2,10},{10,2},{3,11},{11,3},{4,12},{12,4},... | collective-permute-start | bytes 786440 | tf_op jit(solution)/shard_map/ppermute | solution.py:45
  197.8 13.2 %all-to-all-start.6 = ((bf16[4,32,1024]{2,1,0:T(8,128)(2,1)}), bf16[4,32,1024]{2,1,0:T(8,128)(2,1)S(1)}, u32[]{:S(2)}, u32[]{:S(2)}) async-start(bf16[4,32,1024]{2,1,0:T(8,128)(2,1)} %fusion.4), calls=%async_computation.6 | async-start | bytes 524288 | tf_op jit(solution)/shard_map/all_to_all | solution.py:23
where the time goes:
time: 231 us; the launch traced here: 229 us
  blocking collectives  99.4 us (43%)
  starting transfers between devices  72.6 us (31%)
  waiting for transfers between devices  28.3 us (12%)
  local copies, waits for them, and re-layouts  10.1 us (4%)
  other arithmetic  10.1 us (4%)
  matrix products  7.9 us (3%)
    all_to_all x3, blocking collectives, exchange(): return lax.all_to_all(blocks, axes, 0, 0, tiled=True)  62.7 us
    ppermute x12, starting transfers between devices, shifted(): lax.ppermute(block, axis, [(i, (i + step) % members) for i in range(membe...  47.2 us
    all_to_all x4, starting transfers between devices, exchange(): return lax.all_to_all(blocks, axes, 0, 0, tiled=True)  25.5 us
    all_to_all x4, waiting for transfers between devices, exchange(): return lax.all_to_all(blocks, axes, 0, 0, tiled=True)  20.6 us
    all_gather x1, blocking collectives, plan(): act_half = lax.all_gather(act_proj.astype(narrow), row, axis=0, tiled=True)  19.1 us
    all_gather x1, blocking collectives, plan(): output_shift = lax.all_gather(shift, row, axis=0, tiled=True)  17.7 us
    dot_general x5, matrix products, contract(): lax.dot_general(former, latter, (((former_dim,), (latter_dim,)), ((), ())...  7.9 us
    ppermute x12, waiting for transfers between devices, shifted(): lax.ppermute(block, axis, [(i, (i + step) % members) for i in range(membe...  7.64 us
  transfers between devices with their start and end apart: 16, of which 7 were waited for; matrix products, arithmetic and copies ran while one was open for 7% of the time, Pallas kernels for 0%

commit v1 on v0

--- a/solution.py
+++ b/solution.py
@@ -1,6 +1,7 @@
 import jax
 import jax.numpy as jnp
 from jax import lax
+from jax.experimental.layout import Layout, with_layout_constraint
 from jax.sharding import Mesh, PartitionSpec as P
 
 damping = 0.1
@@ -48,8 +49,8 @@
 def pair_sum(partial, axis):
     half = partial.reshape(4, 2, partial.shape[0] // 8, partial.shape[1])
     mine = lax.axis_index(axis)
-    theirs = shifted(pick(half, 1 - mine, 1).astype(narrow), axis, 1)
-    return pick(half, mine, 1) + theirs.astype(wide)
+    sent, kept = lax.optimization_barrier((pick(half, 1 - mine, 1).astype(narrow), pick(half, mine, 1)))
+    return kept + shifted(sent, axis, 1).astype(wide)
 
 
 def ring_sum(halves, axis):
@@ -61,12 +62,19 @@
     return total
 
 
-def gather_by_permutes(block, axis):
+def gather_and_ring_sum(block, halves, axis):
     members = lax.axis_size(axis)
     mine = lax.axis_index(axis)
-    behind = [block] + [shifted(block, axis, step) for step in range(1, members)]
+    depth = block.shape[0]
+    sent = [pick(halves, (mine + step) % members, 0).astype(narrow) for step in range(1, members)]
+    sent = [jnp.concatenate((block, part), axis=0) for part in sent]
+    got = [shifted(message, axis, step) for step, message in enumerate(sent, 1)]
+    total = pick(halves, mine, 0)
+    for message in got:
+        total = total + message[depth:].astype(wide)
+    behind = [block] + [message[:depth] for message in got]
     placed = [lax.select_n((mine - place) % members, *behind) for place in range(members)]
-    return lax.optimization_barrier(jnp.concatenate(placed, axis=0))
+    return lax.optimization_barrier(jnp.concatenate(placed, axis=0)), total
 
 
 def plan(activations, gradients, act_basis, grad_basis, eigen_noise):
@@ -75,10 +83,9 @@
 
     own_rows = lax.dynamic_slice_in_dim(activations, lax.axis_index("x") * slab, slab, 0)
     act_rows = spread(own_rows, "tok")
-    basis_t = gather_by_permutes(act_basis.T, "x")
-
     grad_part = contract(gradients, grad_basis, 1, 0)
-    grad_half = ring_sum(grad_part.reshape(4, slab, grad_part.shape[1]), "x")
+    grad_part = grad_part.reshape(-1, slab, grad_part.shape[1])
+    basis_t, grad_half = gather_and_ring_sum(with_layout_constraint(act_basis.T, Layout((0, 1))), grad_part, "x")
     grad_proj = grad_half + shifted(grad_half.astype(narrow), "yl", 1).astype(wide)
     grad_sq = (grad_proj * grad_proj).astype(narrow)
 

time: 231 us -> 232 us (level)
  waiting for transfers between devices: 28.3 us -> 38.8 us
  starting transfers between devices: 72.6 us -> 62.8 us
  local copies, waits for them, and re-layouts: 10.1 us -> 7.7 us
    ppermute x12 -> x9, waiting for transfers between devices: 7.64 us -> 18.4 us  [shifted(): lax.ppermute(block, axis, [(i, (i + step) % members) for i in range(membe...]
    ppermute x12 -> x9, starting transfers between devices: 47.2 us -> 36.4 us  [shifted(): lax.ppermute(block, axis, [(i, (i + step) % members) for i in range(membe...]
    convert_element_type x2 -> x1, other arithmetic: 2.88 us -> 0.09 us  [ring_sum(): sent = halves.astype(narrow)]
    select_n x1 -> x2, other arithmetic: 1.23 us -> 3.97 us  [gather_and_ring_sum(): lax.select_n((mine - place) % members, *behind)]
    unnamed x15 -> x18, local copies, waits for them, and re-layouts: 4.85 us -> 4 us
  transfers between devices with their start and end apart: 16 -> 13, of which waited for: 7 -> 8; matrix products, arithmetic and copies ran while one was open for 7% -> 7% of each run, Pallas kernels for 0% -> 0%
where the time goes in v1:
time: 232 us; the launch traced here: 231 us
  blocking collectives  100 us (43%)
  starting transfers between devices  62.8 us (27%)
  waiting for transfers between devices  38.8 us (17%)
  other arithmetic  11.7 us (5%)
  matrix products  8.34 us (4%)
  local copies, waits for them, and re-layouts  7.7 us (3%)
    all_to_all x3, blocking collectives, exchange(): return lax.all_to_all(blocks, axes, 0, 0, tiled=True)  63.7 us
    ppermute x9, starting transfers between devices, shifted(): lax.ppermute(block, axis, [(i, (i + step) % members) for i in range(membe...  36.4 us
    all_to_all x4, starting transfers between devices, exchange(): return lax.all_to_all(blocks, axes, 0, 0, tiled=True)  26.3 us
    all_to_all x4, waiting for transfers between devices, exchange(): return lax.all_to_all(blocks, axes, 0, 0, tiled=True)  20.4 us
    all_gather x1, blocking collectives, plan(): act_half = lax.all_gather(act_proj.astype(narrow), row, axis=0, tiled=True)  19 us
    ppermute x9, waiting for transfers between devices, shifted(): lax.ppermute(block, axis, [(i, (i + step) % members) for i in range(membe...  18.4 us
    all_gather x1, blocking collectives, plan(): output_shift = lax.all_gather(shift, row, axis=0, tiled=True)  17.7 us
    dot_general x5, matrix products, contract(): lax.dot_general(former, latter, (((former_dim,), (latter_dim,)), ((), ())...  8.34 us
  transfers between devices with their start and end apart: 13, of which 8 were waited for; matrix products, arithmetic and copies ran while one was open for 7% of the time, Pallas kernels for 0%

profile of v1, /device:TPU:1, one launch (start us, length us, event | category | flops | bytes accessed | tf_op | source)
XLA Modules:
  0.0 230.7 jit_solution(1501550341847492887)
XLA Ops:
  0.6 0.0 copy-start
  0.6 0.0 copy-start.6
  0.7 1.1 constant_dynamic-slice_fusion
  1.7 1.1 broadcast_in_dim.8
  2.8 10.9 %all-to-all-start = ((bf16[8,64,1024]{2,1,0:T(8,128)(2,1)}), bf16[8,64,1024]{2,1,0:T(8,128)(2,1)}, u32[]{:S(2)}, u32[]{:S(2)}) async-start(bf16[8,64,1024]{2,1,0:T(8,128)(2,1)} %broadcast_in_dim.8), calls=%async_computation | async-start | bytes 2097152 | tf_op jit(solution)/shard_map/all_to_all | solution.py:24
  13.7 0.0 copy-done.6
  13.7 0.1 copy.9
  13.9 1.7 fusion.17
  15.6 0.1 fusion.9
  15.7 1.1 pad_maximum_fusion.3
  16.8 3.1 %collective-permute-start = (bf16[192,1024]{1,0:T(8,128)(2,1)}, bf16[192,1024]{1,0:T(8,128)(2,1)}, u32[]{:S(2)}, u32[]{:S(2)}) collective-permute-start(bf16[192,1024]{1,0:T(8,128)(2,1)} %get-tuple-element.25), channel_id=1, source_target_pairs={{0,2},{2,4},{4,6},{6,0},{1,3},{3,5},{5,7},{7,1},{8,10},{10,12},{12... | collective-permute-start | bytes 1179656 | tf_op jit(solution)/shard_map/ppermute | solution.py:46
  19.9 4.4 %collective-permute-start.1 = (bf16[192,1024]{1,0:T(8,128)(2,1)}, bf16[192,1024]{1,0:T(8,128)(2,1)}, u32[]{:S(2)}, u32[]{:S(2)}) collective-permute-start(bf16[192,1024]{1,0:T(8,128)(2,1)} %get-tuple-element.26), channel_id=1, source_target_pairs={{0,4},{2,6},{4,0},{6,2},{1,5},{3,7},{5,1},{7,3},{8,12},{10,14},{12... | collective-permute-start | bytes 1179656 | tf_op jit(solution)/shard_map/ppermute | solution.py:46
  24.3 3.1 %collective-permute-start.2 = (bf16[192,1024]{1,0:T(8,128)(2,1)}, bf16[192,1024]{1,0:T(8,128)(2,1)}, u32[]{:S(2)}, u32[]{:S(2)}) collective-permute-start(bf16[192,1024]{1,0:T(8,128)(2,1)} %get-tuple-element.27), channel_id=1, source_target_pairs={{0,6},{2,0},{4,2},{6,4},{1,7},{3,1},{5,3},{7,5},{8,14},{10,8},{12,... | collective-permute-start | bytes 1179656 | tf_op jit(solution)/shard_map/ppermute | solution.py:46
  27.5 2.5 %collective-permute-done = bf16[192,1024]{1,0:T(8,128)(2,1)} collective-permute-done((bf16[192,1024]{1,0:T(8,128)(2,1)}, bf16[192,1024]{1,0:T(8,128)(2,1)}, u32[]{:S(2)}, u32[]{:S(2)}) %collective-permute-start) | collective-permute-done | bytes 393248 | tf_op jit(solution)/shard_map/ppermute | solution.py:46
  29.9 9.4 %collective-permute-done.1 = bf16[192,1024]{1,0:T(8,128)(2,1)} collective-permute-done((bf16[192,1024]{1,0:T(8,128)(2,1)}, bf16[192,1024]{1,0:T(8,128)(2,1)}, u32[]{:S(2)}, u32[]{:S(2)}) %collective-permute-start.1) | collective-permute-done | bytes 393248 | tf_op jit(solution)/shard_map/ppermute | solution.py:46
  39.4 1.8 collective-permute-done.2
  41.2 1.1 fusion.15
  42.3 3.2 %collective-permute-start.7 = (bf16[64,1024]{1,0:T(8,128)(2,1)S(1)}, bf16[64,1024]{1,0:T(8,128)(2,1)S(1)}, u32[]{:S(2)}, u32[]{:S(2)}) collective-permute-start(bf16[64,1024]{1,0:T(8,128)(2,1)S(1)} %fusion.15), channel_id=1, source_target_pairs={{0,1},{1,0},{2,3},{3,2},{4,5},{5,4},{6,7},{7,6},{8,9},{9,8},{10,11... | collective-permute-start | bytes 393224 | tf_op jit(solution)/shard_map/ppermute | solution.py:46
  45.5 2.1 select_select_fusion.3
  47.6 1.9 select_select_fusion
  49.4 0.0 collective-permute-done.7
  49.5 1.2 multiply_convert_fusion.2
  50.6 0.0 copy-start.3
  50.6 0.0 all-to-all-done
  50.6 1.1 broadcast_in_dim.9
  51.7 6.6 %all-to-all-start.1 = ((bf16[8,64,1024]{2,1,0:T(8,128)(2,1)}), bf16[8,64,1024]{2,1,0:T(8,128)(2,1)}, u32[]{:S(2)}, u32[]{:S(2)}) async-start(bf16[8,64,1024]{2,1,0:T(8,128)(2,1)} %broadcast_in_dim.9), calls=%async_computation.1 | async-start | bytes 2097152 | tf_op jit(solution)/shard_map/all_to_all | solution.py:24
  58.4 0.0 copy-done.2
  58.4 0.0 copy-done.3
  58.4 1.1 pad_maximum_fusion
  59.5 2.0 fusion.2
  61.6 4.0 %collective-permute-start.3 = (bf16[4,64,512]{2,1,0:T(8,128)(2,1)S(1)}, bf16[4,64,512]{2,1,0:T(8,128)(2,1)S(1)}, u32[]{:S(2)}, u32[]{:S(2)}) collective-permute-start(bf16[4,64,512]{2,1,0:T(8,128)(2,1)S(1)} %fusion.5), channel_id=1, source_target_pairs={{0,8},{8,0},{1,9},{9,1},{2,10},{10,2},{3,11},{11,3},{4,12},{12,4},... | collective-permute-start | bytes 786440 | tf_op jit(solution)/shard_map/ppermute | solution.py:46
  65.7 1.1 collective-permute-done.3
  66.8 0.1 fusion.16
  66.9 4.2 %collective-permute-start.4 = (bf16[64,512]{1,0:T(8,128)(2,1)S(1)}, bf16[64,512]{1,0:T(8,128)(2,1)S(1)}, u32[]{:S(2)}, u32[]{:S(2)}) collective-permute-start(bf16[64,512]{1,0:T(8,128)(2,1)S(1)} %get-tuple-element.22), channel_id=1, source_target_pairs={{0,16},{16,32},{32,48},{48,0},{1,17},{17,33},{33,49},{49,1},{2,18}... | collective-permute-start | bytes 196616 | tf_op jit(solution)/shard_map/ppermute | solution.py:46
  71.1 3.2 %collective-permute-start.6 = (bf16[64,512]{1,0:T(8,128)(2,1)S(1)}, bf16[64,512]{1,0:T(8,128)(2,1)S(1)}, u32[]{:S(2)}, u32[]{:S(2)}) collective-permute-start(bf16[64,512]{1,0:T(8,128)(2,1)S(1)} %get-tuple-element.23), channel_id=1, source_target_pairs={{0,48},{16,0},{32,16},{48,32},{1,49},{17,1},{33,17},{49,33},{2,50}... | collective-permute-start | bytes 196616 | tf_op jit(solution)/shard_map/ppermute | solution.py:46
  74.3 6.8 %collective-permute-start.5 = (bf16[64,512]{1,0:T(8,128)(2,1)S(1)}, bf16[64,512]{1,0:T(8,128)(2,1)S(1)}, u32[]{:S(2)}, u32[]{:S(2)}) collective-permute-start(bf16[64,512]{1,0:T(8,128)(2,1)S(1)} %get-tuple-element.24), channel_id=1, source_target_pairs={{0,32},{16,48},{32,0},{48,16},{1,33},{17,49},{33,1},{49,17},{2,34}... | collective-permute-start | bytes 196616 | tf_op jit(solution)/shard_map/ppermute | solution.py:46
  81.1 0.0 collective-permute-done.4
  81.2 0.0 collective-permute-done.6
  81.2 2.5 %collective-permute-done.5 = bf16[64,512]{1,0:T(8,128)(2,1)S(1)} collective-permute-done((bf16[64,512]{1,0:T(8,128)(2,1)S(1)}, bf16[64,512]{1,0:T(8,128)(2,1)S(1)}, u32[]{:S(2)}, u32[]{:S(2)}) %collective-permute-start.5) | collective-permute-done | bytes 65568 | tf_op jit(solution)/shard_map/ppermute | solution.py:46
  83.7 19.0 %all_gather.6 = bf16[512,512]{1,0:T(8,128)(2,1)S(1)} all-gather(bf16[64,512]{1,0:T(8,128)(2,1)S(1)} %fusion.14), channel_id=1, replica_groups=mesh['tok'=8,'yh'=4,'core'=2,'x'=4,'yl'=2] {'yh','core'}, dimensions={0}, use_global_device_ids=true | all-gather | bytes 589824 | tf_op jit(solution)/shard_map/all_gather | solution.py:95
  102.7 0.0 all-to-all-done.1
  102.7 3.1 %convolution_convert_fusion.1 = bf16[512,1024]{1,0:T(8,128)(2,1)} fusion(bf16[512,1024]{1,0:T(8,128)(2,1)} %bitcast.15, bf16[512,512]{1,0:T(8,128)(2,1)S(1)} %all_gather.6), kind=kOutput, calls=%fused_computation.4 | convolution fusion | flops 538181632 | bytes 2621440 | tf_op jit(solution)/shard_map/dot_general | solution.py:15
  105.8 4.2 %all-to-all-start.2 = ((bf16[4,128,1024]{2,1,0:T(8,128)(2,1)}), bf16[4,128,1024]{2,1,0:T(8,128)(2,1)S(1)}, u32[]{:S(2)}, u32[]{:S(2)}) async-start(bf16[4,128,1024]{2,1,0:T(8,128)(2,1)} %bitcast.77), calls=%async_computation.2 | async-start | bytes 2097152 | tf_op jit(solution)/shard_map/all_to_all | solution.py:24
  110.1 2.0 copy.10
  112.1 12.7 %all-to-all-done.2 = bf16[4,128,1024]{2,1,0:T(8,128)(2,1)S(1)} async-done(((bf16[4,128,1024]{2,1,0:T(8,128)(2,1)}), bf16[4,128,1024]{2,1,0:T(8,128)(2,1)S(1)}, u32[]{:S(2)}, u32[]{:S(2)}) %all-to-all-start.2) | async-done | bytes 1048608 | tf_op jit(solution)/shard_map/all_to_all | solution.py:24
  124.8 0.2 convert_reduce_fusion
  125.0 1.9 fusion.4
  126.9 0.1 broadcast_in_dim.10
  127.1 17.6 %all_to_all.53 = bf16[4,128,1024]{2,1,0:T(8,128)(2,1)S(1)} all-to-all(bf16[4,128,1024]{2,1,0:T(8,128)(2,1)S(1)} %broadcast_in_dim.10), channel_id=1, replica_groups=mesh['tok'=8,'yh'=4,'core'=2,'x'=4,'yl'=2] {'x'}, dimensions={0} | all-to-all | bytes 2097152 | tf_op jit(solution)/shard_map/all_to_all | solution.py:24
  144.7 0.7 convolution_convert_fusion
  145.4 33.3 %all_to_all.54 = bf16[16,32,1024]{2,1,0:T(8,128)(2,1)S(1)} all-to-all(bf16[16,32,1024]{2,1,0:T(8,128)(2,1)S(1)} %bitcast.79), channel_id=1, replica_groups=mesh['tok'=8,'yh'=4,'core'=2,'x'=4,'yl'=2] {'tok','yl'}, dimensions={0} | all-to-all | bytes 2097152 | tf_op jit(solution)/shard_map/all_to_all | solution.py:24
  178.7 0.2 reduce_sum.34
  178.9 0.1 broadcast_in_dim.11
  178.9 12.8 %all_to_all.55 = bf16[8,32,1024]{2,1,0:T(8,128)(2,1)S(1)} all-to-all(bf16[8,32,1024]{2,1,0:T(8,128)(2,1)S(1)} %broadcast_in_dim.11), channel_id=1, replica_groups=mesh['tok'=8,'yh'=4,'core'=2,'x'=4,'yl'=2] {'x','yl'}, dimensions={0} | all-to-all | bytes 1048576 | tf_op jit(solution)/shard_map/all_to_all | solution.py:24
  191.8 0.7 fusion
  192.5 0.0 copy-start.1
  192.6 4.5 %collective-permute-start.8 = (bf16[4,32,1024]{2,1,0:T(8,128)(2,1)S(1)}, bf16[4,32,1024]{2,1,0:T(8,128)(2,1)S(1)}, u32[]{:S(2)}, u32[]{:S(2)}) collective-permute-start(bf16[4,32,1024]{2,1,0:T(8,128)(2,1)S(1)} %fusion.6), channel_id=1, source_target_pairs={{0,8},{8,0},{1,9},{9,1},{2,10},{10,2},{3,11},{11,3},{4,12},{12,4},... | collective-permute-start | bytes 786440 | tf_op jit(solution)/shard_map/ppermute | solution.py:46
  197.1 1.1 collective-permute-done.8
  198.3 0.8 add_convert_fusion
  199.0 4.6 %all-to-all-start.6 = ((bf16[4,32,1024]{2,1,0:T(8,128)(2,1)}), bf16[4,32,1024]{2,1,0:T(8,128)(2,1)S(1)}, u32[]{:S(2)}, u32[]{:S(2)}) async-start(bf16[4,32,1024]{2,1,0:T(8,128)(2,1)} %add_convert_fusion), calls=%async_computation.6 | async-start | bytes 524288 | tf_op jit(solution)/shard_map/all_to_all | solution.py:24
  203.6 1.0 copy.11
  204.6 7.7 %all-to-all-done.6 = bf16[4,32,1024]{2,1,0:T(8,128)(2,1)S(1)} async-done(((bf16[4,32,1024]{2,1,0:T(8,128)(2,1)}), bf16[4,32,1024]{2,1,0:T(8,128)(2,1)S(1)}, u32[]{:S(2)}, u32[]{:S(2)}) %all-to-all-start.6) | async-done | bytes 262176 | tf_op jit(solution)/shard_map/all_to_all | solution.py:24
  212.3 17.7 %all_gather.7 = bf16[256,1024]{1,0:T(8,128)(2,1)S(1)} all-gather(bf16[32,1024]{1,0:T(8,128)(2,1)S(1)} %reduce_sum.35), channel_id=1, replica_groups=mesh['tok'=8,'yh'=4,'core'=2,'x'=4,'yl'=2] {'yh','core'}, dimensions={0}, use_global_device_ids=true | all-gather | bytes 589824 | tf_op jit(solution)/shard_map/all_gather | solution.py:107
  229.9 0.8 copy.15
  (14 shorter events, 0.3 us)
Async XLA Ops:
  0.6 13.2 %copy-start = (bf16[1024,1024]{1,0:T(8,128)(2,1)S(1)}, bf16[1024,1024]{1,0:T(8,128)(2,1)}, u32[]{:S(2)}) copy-start(bf16[1024,1024]{1,0:T(8,128)(2,1)} %param.8) | copy-start | bytes 6291460
  0.6 13.1 %copy-start.6 = (bf16[1024,128]{1,0:T(8,128)(2,1)S(1)}, bf16[1024,128]{1,0:T(8,128)(2,1)}, u32[]{:S(2)}) copy-start(bf16[1024,128]{1,0:T(8,128)(2,1)} %param.7) | copy-start | bytes 786436
  2.8 47.8 %all-to-all-start = ((bf16[8,64,1024]{2,1,0:T(8,128)(2,1)}), bf16[8,64,1024]{2,1,0:T(8,128)(2,1)}, u32[]{:S(2)}, u32[]{:S(2)}) async-start(bf16[8,64,1024]{2,1,0:T(8,128)(2,1)} %broadcast_in_dim.8), calls=%async_computation | async-start | bytes 2097152 | tf_op jit(solution)/shard_map/all_to_all | solution.py:24
  16.8 13.1 %collective-permute-start = (bf16[192,1024]{1,0:T(8,128)(2,1)}, bf16[192,1024]{1,0:T(8,128)(2,1)}, u32[]{:S(2)}, u32[]{:S(2)}) collective-permute-start(bf16[192,1024]{1,0:T(8,128)(2,1)} %get-tuple-element.25), channel_id=1, source_target_pairs={{0,2},{2,4},{4,6},{6,0},{1,3},{3,5},{5,7},{7,1},{8,10},{10,12},{12... | collective-permute-start | bytes 1179656 | tf_op jit(solution)/shard_map/ppermute | solution.py:46
  19.9 19.4 %collective-permute-start.1 = (bf16[192,1024]{1,0:T(8,128)(2,1)}, bf16[192,1024]{1,0:T(8,128)(2,1)}, u32[]{:S(2)}, u32[]{:S(2)}) collective-permute-start(bf16[192,1024]{1,0:T(8,128)(2,1)} %get-tuple-element.26), channel_id=1, source_target_pairs={{0,4},{2,6},{4,0},{6,2},{1,5},{3,7},{5,1},{7,3},{8,12},{10,14},{12... | collective-permute-start | bytes 1179656 | tf_op jit(solution)/shard_map/ppermute | solution.py:46
  24.3 16.9 %collective-permute-start.2 = (bf16[192,1024]{1,0:T(8,128)(2,1)}, bf16[192,1024]{1,0:T(8,128)(2,1)}, u32[]{:S(2)}, u32[]{:S(2)}) collective-permute-start(bf16[192,1024]{1,0:T(8,128)(2,1)} %get-tuple-element.27), channel_id=1, source_target_pairs={{0,6},{2,0},{4,2},{6,4},{1,7},{3,1},{5,3},{7,5},{8,14},{10,8},{12,... | collective-permute-start | bytes 1179656 | tf_op jit(solution)/shard_map/ppermute | solution.py:46
  42.3 7.2 %collective-permute-start.7 = (bf16[64,1024]{1,0:T(8,128)(2,1)S(1)}, bf16[64,1024]{1,0:T(8,128)(2,1)S(1)}, u32[]{:S(2)}, u32[]{:S(2)}) collective-permute-start(bf16[64,1024]{1,0:T(8,128)(2,1)S(1)} %fusion.15), channel_id=1, source_target_pairs={{0,1},{1,0},{2,3},{3,2},{4,5},{5,4},{6,7},{7,6},{8,9},{9,8},{10,11... | collective-permute-start | bytes 393224 | tf_op jit(solution)/shard_map/ppermute | solution.py:46
  49.4 8.9 %copy-start.2 = (bf16[128,1024]{1,0:T(8,128)(2,1)S(1)}, bf16[128,1024]{1,0:T(8,128)(2,1)}, u32[]{:S(2)}) copy-start(bf16[128,1024]{1,0:T(8,128)(2,1)} %get-tuple-element.14) | copy-start | bytes 786436
  50.6 7.8 %copy-start.3 = (bf16[128,1024]{1,0:T(8,128)(2,1)S(1)}, bf16[128,1024]{1,0:T(8,128)(2,1)}, u32[]{:S(2)}) copy-start(bf16[128,1024]{1,0:T(8,128)(2,1)} %select_select_fusion) | copy-start | bytes 786436
  51.7 50.9 %all-to-all-start.1 = ((bf16[8,64,1024]{2,1,0:T(8,128)(2,1)}), bf16[8,64,1024]{2,1,0:T(8,128)(2,1)}, u32[]{:S(2)}, u32[]{:S(2)}) async-start(bf16[8,64,1024]{2,1,0:T(8,128)(2,1)} %broadcast_in_dim.9), calls=%async_computation.1 | async-start | bytes 2097152 | tf_op jit(solution)/shard_map/all_to_all | solution.py:24
  61.6 5.2 %collective-permute-start.3 = (bf16[4,64,512]{2,1,0:T(8,128)(2,1)S(1)}, bf16[4,64,512]{2,1,0:T(8,128)(2,1)S(1)}, u32[]{:S(2)}, u32[]{:S(2)}) collective-permute-start(bf16[4,64,512]{2,1,0:T(8,128)(2,1)S(1)} %fusion.5), channel_id=1, source_target_pairs={{0,8},{8,0},{1,9},{9,1},{2,10},{10,2},{3,11},{11,3},{4,12},{12,4},... | collective-permute-start | bytes 786440 | tf_op jit(solution)/shard_map/ppermute | solution.py:46
  66.9 14.2 %collective-permute-start.4 = (bf16[64,512]{1,0:T(8,128)(2,1)S(1)}, bf16[64,512]{1,0:T(8,128)(2,1)S(1)}, u32[]{:S(2)}, u32[]{:S(2)}) collective-permute-start(bf16[64,512]{1,0:T(8,128)(2,1)S(1)} %get-tuple-element.22), channel_id=1, source_target_pairs={{0,16},{16,32},{32,48},{48,0},{1,17},{17,33},{33,49},{49,1},{2,18}... | collective-permute-start | bytes 196616 | tf_op jit(solution)/shard_map/ppermute | solution.py:46
  71.1 10.0 %collective-permute-start.6 = (bf16[64,512]{1,0:T(8,128)(2,1)S(1)}, bf16[64,512]{1,0:T(8,128)(2,1)S(1)}, u32[]{:S(2)}, u32[]{:S(2)}) collective-permute-start(bf16[64,512]{1,0:T(8,128)(2,1)S(1)} %get-tuple-element.23), channel_id=1, source_target_pairs={{0,48},{16,0},{32,16},{48,32},{1,49},{17,1},{33,17},{49,33},{2,50}... | collective-permute-start | bytes 196616 | tf_op jit(solution)/shard_map/ppermute | solution.py:46
  74.3 9.3 %collective-permute-start.5 = (bf16[64,512]{1,0:T(8,128)(2,1)S(1)}, bf16[64,512]{1,0:T(8,128)(2,1)S(1)}, u32[]{:S(2)}, u32[]{:S(2)}) collective-permute-start(bf16[64,512]{1,0:T(8,128)(2,1)S(1)} %get-tuple-element.24), channel_id=1, source_target_pairs={{0,32},{16,48},{32,0},{48,16},{1,33},{17,49},{33,1},{49,17},{2,34}... | collective-permute-start | bytes 196616 | tf_op jit(solution)/shard_map/ppermute | solution.py:46
  102.7 3.1 %copy-start.4 = (bf16[512,512]{1,0:T(8,128)(2,1)}, bf16[512,512]{1,0:T(8,128)(2,1)S(1)}, u32[]{:S(2)}) copy-start(bf16[512,512]{1,0:T(8,128)(2,1)S(1)} %all_gather.6) | copy-start | bytes 1572868
  105.8 19.0 %all-to-all-start.2 = ((bf16[4,128,1024]{2,1,0:T(8,128)(2,1)}), bf16[4,128,1024]{2,1,0:T(8,128)(2,1)S(1)}, u32[]{:S(2)}, u32[]{:S(2)}) async-start(bf16[4,128,1024]{2,1,0:T(8,128)(2,1)} %bitcast.77), calls=%async_computation.2 | async-start | bytes 2097152 | tf_op jit(solution)/shard_map/all_to_all | solution.py:24
  126.9 17.7 %copy-start.5 = (bf16[512,512]{1,0:T(8,128)(2,1)S(1)}, bf16[512,512]{1,0:T(8,128)(2,1)}, u32[]{:S(2)}) copy-start(bf16[512,512]{1,0:T(8,128)(2,1)} %copy-done.4) | copy-start | bytes 1572868
  192.5 11.1 %copy-start.1 = (f32[1024,128]{0,1:T(8,128)S(1)}, f32[1024,128]{0,1:T(8,128)}, u32[]{:S(2)}) copy-start(f32[1024,128]{0,1:T(8,128)} %get-tuple-element.21) | copy-start | bytes 1572868
  192.6 5.6 %collective-permute-start.8 = (bf16[4,32,1024]{2,1,0:T(8,128)(2,1)S(1)}, bf16[4,32,1024]{2,1,0:T(8,128)(2,1)S(1)}, u32[]{:S(2)}, u32[]{:S(2)}) collective-permute-start(bf16[4,32,1024]{2,1,0:T(8,128)(2,1)S(1)} %fusion.6), channel_id=1, source_target_pairs={{0,8},{8,0},{1,9},{9,1},{2,10},{10,2},{3,11},{11,3},{4,12},{12,4},... | collective-permute-start | bytes 786440 | tf_op jit(solution)/shard_map/ppermute | solution.py:46
  199.0 13.2 %all-to-all-start.6 = ((bf16[4,32,1024]{2,1,0:T(8,128)(2,1)}), bf16[4,32,1024]{2,1,0:T(8,128)(2,1)S(1)}, u32[]{:S(2)}, u32[]{:S(2)}) async-start(bf16[4,32,1024]{2,1,0:T(8,128)(2,1)} %add_convert_fusion), calls=%async_computation.6 | async-start | bytes 524288 | tf_op jit(solution)/shard_map/all_to_all | solution.py:24

commit v2 on v1

--- a/solution.py
+++ b/solution.py
@@ -72,9 +72,14 @@
     total = pick(halves, mine, 0)
     for message in got:
         total = total + message[depth:].astype(wide)
-    behind = [block] + [message[:depth] for message in got]
-    placed = [lax.select_n((mine - place) % members, *behind) for place in range(members)]
-    return lax.optimization_barrier(jnp.concatenate(placed, axis=0)), total
+    return jnp.concatenate([block] + [message[:depth] for message in got], axis=0), total
+
+
+def placed(columns, axis):
+    members = lax.axis_size(axis)
+    mine = lax.axis_index(axis)
+    behind = jnp.split(columns, members, axis=1)
+    return jnp.concatenate([lax.select_n((mine - place) % members, *behind) for place in range(members)], axis=1)
 
 
 def plan(activations, gradients, act_basis, grad_basis, eigen_noise):
@@ -92,7 +97,9 @@
     act_halves = pair_sum(contract(act_rows, basis_t, 1, 1), "core")
     act_proj = ring_sum(act_halves, "yh")
     grad_sq = spread(grad_sq, "tok")
-    act_half = lax.all_gather(act_proj.astype(narrow), row, axis=0, tiled=True)
+    act_half = lax.all_gather(placed(act_proj.astype(narrow), "x"), row, axis=0, tiled=True)
+    own_basis, act_half = lax.optimization_barrier((grad_basis, act_half))
+    their_basis = shifted(own_basis, "core", 1)
     act_wide = act_half.astype(wide)
     act_sq = (act_wide * act_wide).astype(narrow)
 
@@ -100,10 +107,15 @@
     scaled_t = (eigen_noise.T * lax.rsqrt(token_count * (scales_t + damping))).astype(narrow)
     widened_t = spread(scaled_t, "x")
 
-    hidden = scatter_sum(contract(act_half, widened_t, 1, 0), ("tok", "yl")).astype(narrow)
+    parts = exchange(contract(act_half, widened_t, 1, 0).astype(narrow), ("tok", "core", "yl"))
+    parts = parts.reshape(8, 2, 2, parts.shape[0] // 32, parts.shape[1])
+    hidden = jnp.sum(parts.astype(wide), axis=(0, 2)).astype(narrow)
+    mine = lax.axis_index("core")
+    hidden = jnp.concatenate((pick(hidden, mine, 0), pick(hidden, 1 - mine, 0)), axis=1)
     hidden = spread(hidden, col)
-    halves = pair_sum(contract(hidden, grad_basis, 1, 1), "core")
-    shift = scatter_sum(halves, "yh")[0].astype(narrow)
+    depth = grad_basis.shape[1]
+    shift_part = contract(hidden[:, :depth], grad_basis, 1, 1) + contract(hidden[:, depth:], their_basis, 1, 1)
+    shift = scatter_sum(shift_part, "yh").astype(narrow)
     output_shift = lax.all_gather(shift, row, axis=0, tiled=True)
     return (scales_t.T, output_shift)
 

time: 232 us -> 238 us (1.026)
  blocking collectives: 100 us -> 68 us
  waiting for transfers between devices: 38.8 us -> 62.8 us
  starting transfers between devices: 62.8 us -> 70.2 us
  local copies, waits for them, and re-layouts: 7.7 us -> 12.6 us
  matrix products: 8.34 us -> 11.6 us
    all_to_all x3 -> x2, blocking collectives: 63.7 us -> 28 us  [exchange(): return lax.all_to_all(blocks, axes, 0, 0, tiled=True)]
    all_to_all x4 -> x5, waiting for transfers between devices: 20.4 us -> 45.4 us  [exchange(): return lax.all_to_all(blocks, axes, 0, 0, tiled=True)]
    all_to_all x4 -> x5, starting transfers between devices: 26.3 us -> 36.1 us  [exchange(): return lax.all_to_all(blocks, axes, 0, 0, tiled=True)]
    slice x0 -> x3, local copies, waits for them, and re-layouts: none -> 4.05 us  [gather_and_ring_sum(): message[:depth]]
    select_n x2, other arithmetic: 3.97 us -> 0.03 us  [placed(): lax.select_n((mine - place) % members, *behind)]
    all_gather x1, blocking collectives: 17.7 us -> 21 us  [plan(): output_shift = lax.all_gather(shift, row, axis=0, tiled=True)]
    dot_general x5 -> x6, matrix products: 8.34 us -> 11.6 us  [contract(): lax.dot_general(former, latter, (((former_dim,), (latter_dim,)), ((), ())...]
  transfers between devices with their start and end apart: 13 -> 14, of which waited for: 8 -> 8; matrix products, arithmetic and copies ran while one was open for 7% -> 8% of each run, Pallas kernels for 0% -> 0%
where the time goes in v2:
time: 238 us; the launch traced here: 237 us
  starting transfers between devices  70.2 us (29%)
  blocking collectives  68 us (29%)
  waiting for transfers between devices  62.8 us (26%)
  local copies, waits for them, and re-layouts  12.6 us (5%)
  matrix products  11.6 us (5%)
  other arithmetic  10.3 us (4%)
    all_to_all x5, waiting for transfers between devices, exchange(): return lax.all_to_all(blocks, axes, 0, 0, tiled=True)  45.4 us
    all_to_all x5, starting transfers between devices, exchange(): return lax.all_to_all(blocks, axes, 0, 0, tiled=True)  36.1 us
    ppermute x9, starting transfers between devices, shifted(): lax.ppermute(block, axis, [(i, (i + step) % members) for i in range(membe...  34.1 us
    all_to_all x2, blocking collectives, exchange(): return lax.all_to_all(blocks, axes, 0, 0, tiled=True)  28 us
    all_gather x1, blocking collectives, plan(): output_shift = lax.all_gather(shift, row, axis=0, tiled=True)  21 us
    all_gather x1, blocking collectives, plan(): lax.all_gather(placed(act_proj.astype(narrow), 'x'), row, axis=0, tiled=T...  19 us
    ppermute x9, waiting for transfers between devices, shifted(): lax.ppermute(block, axis, [(i, (i + step) % members) for i in range(membe...  17.5 us
    dot_general x6, matrix products, contract(): lax.dot_general(former, latter, (((former_dim,), (latter_dim,)), ((), ())...  11.6 us
  transfers between devices with their start and end apart: 14, of which 8 were waited for; matrix products, arithmetic and copies ran while one was open for 8% of the time, Pallas kernels for 0%

profile of v2, /device:TPU:1, one launch (start us, length us, event | category | flops | bytes accessed | tf_op | source)
XLA Modules:
  0.0 236.7 jit_solution(5255543577833097053)
XLA Ops:
  0.6 0.0 copy-start
  0.6 0.0 copy-start.5
  0.7 0.0 copy-start.1
  0.7 1.1 constant_dynamic-slice_fusion
  1.7 1.1 broadcast_in_dim.8
  2.8 10.9 %all-to-all-start = ((bf16[8,64,1024]{2,1,0:T(8,128)(2,1)}), bf16[8,64,1024]{2,1,0:T(8,128)(2,1)}, u32[]{:S(2)}, u32[]{:S(2)}) async-start(bf16[8,64,1024]{2,1,0:T(8,128)(2,1)} %broadcast_in_dim.8), calls=%async_computation | async-start | bytes 2097152 | tf_op jit(solution)/shard_map/all_to_all | solution.py:24
  13.7 0.0 copy-done.5
  13.7 0.1 copy.9
  13.9 0.7 fusion.24
  14.6 1.0 copy-done.2
  15.6 1.1 pad_maximum_fusion.2
  16.8 3.1 %collective-permute-start = (bf16[192,1024]{1,0:T(8,128)(2,1)}, bf16[192,1024]{1,0:T(8,128)(2,1)S(1)}, u32[]{:S(2)}, u32[]{:S(2)}) collective-permute-start(bf16[192,1024]{1,0:T(8,128)(2,1)} %get-tuple-element.22), channel_id=1, source_target_pairs={{0,2},{2,4},{4,6},{6,0},{1,3},{3,5},{5,7},{7,1},{8,10},{10,12},{12... | collective-permute-start | bytes 1179656 | tf_op jit(solution)/shard_map/ppermute | solution.py:46
  19.9 4.4 %collective-permute-start.1 = (bf16[192,1024]{1,0:T(8,128)(2,1)}, bf16[192,1024]{1,0:T(8,128)(2,1)}, u32[]{:S(2)}, u32[]{:S(2)}) collective-permute-start(bf16[192,1024]{1,0:T(8,128)(2,1)} %get-tuple-element.23), channel_id=1, source_target_pairs={{0,4},{2,6},{4,0},{6,2},{1,5},{3,7},{5,1},{7,3},{8,12},{10,14},{12... | collective-permute-start | bytes 1179656 | tf_op jit(solution)/shard_map/ppermute | solution.py:46
  24.3 3.1 %collective-permute-start.2 = (bf16[192,1024]{1,0:T(8,128)(2,1)}, bf16[192,1024]{1,0:T(8,128)(2,1)}, u32[]{:S(2)}, u32[]{:S(2)}) collective-permute-start(bf16[192,1024]{1,0:T(8,128)(2,1)} %get-tuple-element.24), channel_id=1, source_target_pairs={{0,6},{2,0},{4,2},{6,4},{1,7},{3,1},{5,3},{7,5},{8,14},{10,8},{12,... | collective-permute-start | bytes 1179656 | tf_op jit(solution)/shard_map/ppermute | solution.py:46
  27.3 2.6 %collective-permute-done = bf16[192,1024]{1,0:T(8,128)(2,1)S(1)} collective-permute-done((bf16[192,1024]{1,0:T(8,128)(2,1)}, bf16[192,1024]{1,0:T(8,128)(2,1)S(1)}, u32[]{:S(2)}, u32[]{:S(2)}) %collective-permute-start) | collective-permute-done | bytes 393248 | tf_op jit(solution)/shard_map/ppermute | solution.py:46
  29.9 9.4 %collective-permute-done.1 = bf16[192,1024]{1,0:T(8,128)(2,1)} collective-permute-done((bf16[192,1024]{1,0:T(8,128)(2,1)}, bf16[192,1024]{1,0:T(8,128)(2,1)}, u32[]{:S(2)}, u32[]{:S(2)}) %collective-permute-start.1) | collective-permute-done | bytes 393248 | tf_op jit(solution)/shard_map/ppermute | solution.py:46
  39.3 1.8 collective-permute-done.2
  41.1 1.1 fusion.22
  42.3 3.2 %collective-permute-start.7 = (bf16[64,1024]{1,0:T(8,128)(2,1)S(1)}, bf16[64,1024]{1,0:T(8,128)(2,1)S(1)}, u32[]{:S(2)}, u32[]{:S(2)}) collective-permute-start(bf16[64,1024]{1,0:T(8,128)(2,1)S(1)} %fusion.22), channel_id=1, source_target_pairs={{0,1},{1,0},{2,3},{3,2},{4,5},{5,4},{6,7},{7,6},{8,9},{9,8},{10,11... | collective-permute-start | bytes 393224 | tf_op jit(solution)/shard_map/ppermute | solution.py:46
  45.5 0.7 slice.32
  46.2 1.7 slice.33
  47.9 1.7 slice.34
  49.5 0.0 collective-permute-done.7
  49.5 1.2 multiply_convert_fusion.2
  50.7 0.0 copy-start.6
  50.7 0.0 all-to-all-done
  50.7 1.1 broadcast_in_dim.9
  51.9 6.6 %all-to-all-start.1 = ((bf16[8,64,1024]{2,1,0:T(8,128)(2,1)}), bf16[8,64,1024]{2,1,0:T(8,128)(2,1)}, u32[]{:S(2)}, u32[]{:S(2)}) async-start(bf16[8,64,1024]{2,1,0:T(8,128)(2,1)} %broadcast_in_dim.9), calls=%async_computation.1 | async-start | bytes 2097152 | tf_op jit(solution)/shard_map/all_to_all | solution.py:24
  58.5 2.1 fusion.1
  60.7 4.0 %collective-permute-start.3 = (bf16[4,64,512]{2,1,0:T(8,128)(2,1)S(1)}, bf16[4,64,512]{2,1,0:T(8,128)(2,1)}, u32[]{:S(2)}, u32[]{:S(2)}) collective-permute-start(bf16[4,64,512]{2,1,0:T(8,128)(2,1)S(1)} %fusion.9), channel_id=1, source_target_pairs={{0,8},{8,0},{1,9},{9,1},{2,10},{10,2},{3,11},{11,3},{4,12},{12,4},... | collective-permute-start | bytes 786440 | tf_op jit(solution)/shard_map/ppermute | solution.py:46
  64.8 1.2 collective-permute-done.3
  66.0 1.8 fusion.23
  67.9 4.2 %collective-permute-start.4 = (bf16[64,512]{1,0:T(8,128)(2,1)S(1)}, bf16[64,512]{1,0:T(8,128)(2,1)S(1)}, u32[]{:S(2)}, u32[]{:S(2)}) collective-permute-start(bf16[64,512]{1,0:T(8,128)(2,1)S(1)} %get-tuple-element.19), channel_id=1, source_target_pairs={{0,16},{16,32},{32,48},{48,0},{1,17},{17,33},{33,49},{49,1},{2,18}... | collective-permute-start | bytes 196616 | tf_op jit(solution)/shard_map/ppermute | solution.py:46
  72.1 3.2 %collective-permute-start.6 = (bf16[64,512]{1,0:T(8,128)(2,1)S(1)}, bf16[64,512]{1,0:T(8,128)(2,1)S(1)}, u32[]{:S(2)}, u32[]{:S(2)}) collective-permute-start(bf16[64,512]{1,0:T(8,128)(2,1)S(1)} %get-tuple-element.20), channel_id=1, source_target_pairs={{0,48},{16,0},{32,16},{48,32},{1,49},{17,1},{33,17},{49,33},{2,50}... | collective-permute-start | bytes 196616 | tf_op jit(solution)/shard_map/ppermute | solution.py:46
  75.3 6.8 %collective-permute-start.5 = (bf16[64,512]{1,0:T(8,128)(2,1)S(1)}, bf16[64,512]{1,0:T(8,128)(2,1)S(1)}, u32[]{:S(2)}, u32[]{:S(2)}) collective-permute-start(bf16[64,512]{1,0:T(8,128)(2,1)S(1)} %get-tuple-element.21), channel_id=1, source_target_pairs={{0,32},{16,48},{32,0},{48,16},{1,33},{17,49},{33,1},{49,17},{2,34}... | collective-permute-start | bytes 196616 | tf_op jit(solution)/shard_map/ppermute | solution.py:46
  82.1 0.0 collective-permute-done.4
  82.1 0.0 collective-permute-done.6
  82.1 2.4 %collective-permute-done.5 = bf16[64,512]{1,0:T(8,128)(2,1)S(1)} collective-permute-done((bf16[64,512]{1,0:T(8,128)(2,1)S(1)}, bf16[64,512]{1,0:T(8,128)(2,1)S(1)}, u32[]{:S(2)}, u32[]{:S(2)}) %collective-permute-start.5) | collective-permute-done | bytes 65568 | tf_op jit(solution)/shard_map/ppermute | solution.py:46
  84.6 0.9 fusion.20
  85.6 19.0 %all_gather.6 = bf16[512,512]{1,0:T(8,128)(2,1)S(1)} all-gather(bf16[64,512]{1,0:T(8,128)(2,1)S(1)} %pad_maximum_fusion.3), channel_id=1, replica_groups=mesh['tok'=8,'yh'=4,'core'=2,'x'=4,'yl'=2] {'yh','core'}, dimensions={0}, use_global_device_ids=true | all-gather | bytes 589824 | tf_op jit(solution)/shard_map/all_gather | solution.py:100
  104.5 0.0 all-to-all-done.1
  104.6 3.2 %convolution_convert_fusion.1 = bf16[512,1024]{1,0:T(8,128)(2,1)} fusion(bf16[512,1024]{1,0:T(8,128)(2,1)} %bitcast.15, bf16[512,512]{1,0:T(8,128)(2,1)S(1)} %all_gather.6), kind=kOutput, calls=%fused_computation.2 | convolution fusion | flops 538181632 | bytes 2621440 | tf_op jit(solution)/shard_map/dot_general | solution.py:15
  107.7 4.5 %all-to-all-start.2 = ((bf16[4,128,1024]{2,1,0:T(8,128)(2,1)}), bf16[4,128,1024]{2,1,0:T(8,128)(2,1)}, u32[]{:S(2)}, u32[]{:S(2)}) async-start(bf16[4,128,1024]{2,1,0:T(8,128)(2,1)} %bitcast.75), calls=%async_computation.2 | async-start | bytes 2097152 | tf_op jit(solution)/shard_map/all_to_all | solution.py:24
  112.2 2.0 copy.10
  114.2 12.8 %all-to-all-done.2 = bf16[4,128,1024]{2,1,0:T(8,128)(2,1)} async-done(((bf16[4,128,1024]{2,1,0:T(8,128)(2,1)}), bf16[4,128,1024]{2,1,0:T(8,128)(2,1)}, u32[]{:S(2)}, u32[]{:S(2)}) %all-to-all-start.2) | async-done | bytes 1048608 | tf_op jit(solution)/shard_map/all_to_all | solution.py:24
  127.1 1.5 convert_reduce_fusion
  128.5 1.2 fusion.8
  129.7 0.0 copy-start.4
  129.7 0.1 broadcast_in_dim.10
  129.8 17.9 %all_to_all.60 = bf16[4,128,1024]{2,1,0:T(8,128)(2,1)S(1)} all-to-all(bf16[4,128,1024]{2,1,0:T(8,128)(2,1)S(1)} %broadcast_in_dim.10), channel_id=1, replica_groups=mesh['tok'=8,'yh'=4,'core'=2,'x'=4,'yl'=2] {'x'}, dimensions={0} | all-to-all | bytes 2097152 | tf_op jit(solution)/shard_map/all_to_all | solution.py:24
  147.8 1.7 convolution_convert_fusion
  149.4 9.5 %all-to-all-start.4 = ((bf16[32,16,1024]{2,1,0:T(8,128)(2,1)}), bf16[32,16,1024]{2,1,0:T(8,128)(2,1)}, u32[]{:S(2)}, u32[]{:S(2)}) async-start(bf16[32,16,1024]{2,1,0:T(8,128)(2,1)} %bitcast.74), calls=%async_computation.4 | async-start | bytes 2097152 | tf_op jit(solution)/shard_map/all_to_all | solution.py:24
  159.0 2.2 collective-permute-start.8
  161.2 25.5 %all-to-all-done.4 = bf16[32,16,1024]{2,1,0:T(8,128)(2,1)} async-done(((bf16[32,16,1024]{2,1,0:T(8,128)(2,1)}), bf16[32,16,1024]{2,1,0:T(8,128)(2,1)}, u32[]{:S(2)}, u32[]{:S(2)}) %all-to-all-start.4) | async-done | bytes 1048608 | tf_op jit(solution)/shard_map/all_to_all | solution.py:24
  186.7 1.4 reduce_sum.34
  188.2 10.0 %all_to_all.61 = bf16[8,16,2048]{2,1,0:T(8,128)(2,1)S(1)} all-to-all(bf16[8,16,2048]{2,1,0:T(8,128)(2,1)S(1)} %broadcast_in_dim.11), channel_id=1, replica_groups=mesh['tok'=8,'yh'=4,'core'=2,'x'=4,'yl'=2] {'x','yl'}, dimensions={0} | all-to-all | bytes 1048576 | tf_op jit(solution)/shard_map/all_to_all | solution.py:24
  198.2 0.8 fusion.11
  199.1 0.0 collective-permute-done.8
  199.1 3.1 %fusion = bf16[128,1024]{1,0:T(8,128)(2,1)} fusion(f32[128,1024]{1,0:T(8,128)S(1)} %fusion.11, bf16[1024,1024]{1,0:T(8,128)(2,1)} %collective-permute-done.8, bf16[128,2048]{1,0:T(8,128)(2,1)S(1)} %bitcast.71), kind=kOutput, calls=%fused_computation.4 | convolution fusion | flops 268697600 | bytes 3145728 | tf_op jit(solution)/shard_map/dot_general | solution.py:15
  202.2 4.6 %all-to-all-start.6 = ((bf16[4,32,1024]{2,1,0:T(8,128)(2,1)}), bf16[4,32,1024]{2,1,0:T(8,128)(2,1)S(1)}, u32[]{:S(2)}, u32[]{:S(2)}) async-start(bf16[4,32,1024]{2,1,0:T(8,128)(2,1)} %bitcast.25), calls=%async_computation.6 | async-start | bytes 524288 | tf_op jit(solution)/shard_map/all_to_all | solution.py:24
  206.8 1.0 copy.11
  207.8 7.0 %all-to-all-done.6 = bf16[4,32,1024]{2,1,0:T(8,128)(2,1)S(1)} async-done(((bf16[4,32,1024]{2,1,0:T(8,128)(2,1)}), bf16[4,32,1024]{2,1,0:T(8,128)(2,1)S(1)}, u32[]{:S(2)}, u32[]{:S(2)}) %all-to-all-start.6) | async-done | bytes 262176 | tf_op jit(solution)/shard_map/all_to_all | solution.py:24
  214.8 21.0 %all_gather.7 = bf16[256,1024]{1,0:T(8,128)(2,1)S(1)} all-gather(bf16[32,1024]{1,0:T(8,128)(2,1)S(1)} %reduce_sum.35), channel_id=1, replica_groups=mesh['tok'=8,'yh'=4,'core'=2,'x'=4,'yl'=2] {'yh','core'}, dimensions={0}, use_global_device_ids=true | all-gather | bytes 589824 | tf_op jit(solution)/shard_map/all_gather | solution.py:119
  235.9 0.8 copy.14
  (18 shorter events, 0.3 us)
Async XLA Ops:
  0.6 13.2 %copy-start = (bf16[256,1024]{1,0:T(8,128)(2,1)S(1)}, bf16[256,1024]{1,0:T(8,128)(2,1)}, u32[]{:S(2)}) copy-start(bf16[256,1024]{1,0:T(8,128)(2,1)} %param.6) | copy-start | bytes 1572868
  0.6 13.0 %copy-start.5 = (bf16[1024,128]{1,0:T(8,128)(2,1)S(1)}, bf16[1024,128]{1,0:T(8,128)(2,1)}, u32[]{:S(2)}) copy-start(bf16[1024,128]{1,0:T(8,128)(2,1)} %param.7) | copy-start | bytes 786436
  0.7 13.2 %copy-start.1 = (bf16[1024,1024]{1,0:T(8,128)(2,1)S(1)}, bf16[1024,1024]{1,0:T(8,128)(2,1)}, u32[]{:S(2)}) copy-start(bf16[1024,1024]{1,0:T(8,128)(2,1)} %param.8) | copy-start | bytes 6291460
  2.8 47.9 %all-to-all-start = ((bf16[8,64,1024]{2,1,0:T(8,128)(2,1)}), bf16[8,64,1024]{2,1,0:T(8,128)(2,1)}, u32[]{:S(2)}, u32[]{:S(2)}) async-start(bf16[8,64,1024]{2,1,0:T(8,128)(2,1)} %broadcast_in_dim.8), calls=%async_computation | async-start | bytes 2097152 | tf_op jit(solution)/shard_map/all_to_all | solution.py:24
  14.6 1.0 copy-start.2
  16.8 13.1 %collective-permute-start = (bf16[192,1024]{1,0:T(8,128)(2,1)}, bf16[192,1024]{1,0:T(8,128)(2,1)S(1)}, u32[]{:S(2)}, u32[]{:S(2)}) collective-permute-start(bf16[192,1024]{1,0:T(8,128)(2,1)} %get-tuple-element.22), channel_id=1, source_target_pairs={{0,2},{2,4},{4,6},{6,0},{1,3},{3,5},{5,7},{7,1},{8,10},{10,12},{12... | collective-permute-start | bytes 1179656 | tf_op jit(solution)/shard_map/ppermute | solution.py:46
  19.9 19.4 %collective-permute-start.1 = (bf16[192,1024]{1,0:T(8,128)(2,1)}, bf16[192,1024]{1,0:T(8,128)(2,1)}, u32[]{:S(2)}, u32[]{:S(2)}) collective-permute-start(bf16[192,1024]{1,0:T(8,128)(2,1)} %get-tuple-element.23), channel_id=1, source_target_pairs={{0,4},{2,6},{4,0},{6,2},{1,5},{3,7},{5,1},{7,3},{8,12},{10,14},{12... | collective-permute-start | bytes 1179656 | tf_op jit(solution)/shard_map/ppermute | solution.py:46
  24.3 16.9 %collective-permute-start.2 = (bf16[192,1024]{1,0:T(8,128)(2,1)}, bf16[192,1024]{1,0:T(8,128)(2,1)}, u32[]{:S(2)}, u32[]{:S(2)}) collective-permute-start(bf16[192,1024]{1,0:T(8,128)(2,1)} %get-tuple-element.24), channel_id=1, source_target_pairs={{0,6},{2,0},{4,2},{6,4},{1,7},{3,1},{5,3},{7,5},{8,14},{10,8},{12,... | collective-permute-start | bytes 1179656 | tf_op jit(solution)/shard_map/ppermute | solution.py:46
  42.3 7.3 %collective-permute-start.7 = (bf16[64,1024]{1,0:T(8,128)(2,1)S(1)}, bf16[64,1024]{1,0:T(8,128)(2,1)S(1)}, u32[]{:S(2)}, u32[]{:S(2)}) collective-permute-start(bf16[64,1024]{1,0:T(8,128)(2,1)S(1)} %fusion.22), channel_id=1, source_target_pairs={{0,1},{1,0},{2,3},{3,2},{4,5},{5,4},{6,7},{7,6},{8,9},{9,8},{10,11... | collective-permute-start | bytes 393224 | tf_op jit(solution)/shard_map/ppermute | solution.py:46
  50.7 7.8 %copy-start.6 = (bf16[128,1024]{1,0:T(8,128)(2,1)S(1)}, bf16[128,1024]{1,0:T(8,128)(2,1)}, u32[]{:S(2)}) copy-start(bf16[128,1024]{1,0:T(8,128)(2,1)} %slice.34) | copy-start | bytes 786436
  51.9 52.7 %all-to-all-start.1 = ((bf16[8,64,1024]{2,1,0:T(8,128)(2,1)}), bf16[8,64,1024]{2,1,0:T(8,128)(2,1)}, u32[]{:S(2)}, u32[]{:S(2)}) async-start(bf16[8,64,1024]{2,1,0:T(8,128)(2,1)} %broadcast_in_dim.9), calls=%async_computation.1 | async-start | bytes 2097152 | tf_op jit(solution)/shard_map/all_to_all | solution.py:24
  60.7 5.3 %collective-permute-start.3 = (bf16[4,64,512]{2,1,0:T(8,128)(2,1)S(1)}, bf16[4,64,512]{2,1,0:T(8,128)(2,1)}, u32[]{:S(2)}, u32[]{:S(2)}) collective-permute-start(bf16[4,64,512]{2,1,0:T(8,128)(2,1)S(1)} %fusion.9), channel_id=1, source_target_pairs={{0,8},{8,0},{1,9},{9,1},{2,10},{10,2},{3,11},{11,3},{4,12},{12,4},... | collective-permute-start | bytes 786440 | tf_op jit(solution)/shard_map/ppermute | solution.py:46
  67.9 14.3 %collective-permute-start.4 = (bf16[64,512]{1,0:T(8,128)(2,1)S(1)}, bf16[64,512]{1,0:T(8,128)(2,1)S(1)}, u32[]{:S(2)}, u32[]{:S(2)}) collective-permute-start(bf16[64,512]{1,0:T(8,128)(2,1)S(1)} %get-tuple-element.19), channel_id=1, source_target_pairs={{0,16},{16,32},{32,48},{48,0},{1,17},{17,33},{33,49},{49,1},{2,18}... | collective-permute-start | bytes 196616 | tf_op jit(solution)/shard_map/ppermute | solution.py:46
  72.1 10.0 %collective-permute-start.6 = (bf16[64,512]{1,0:T(8,128)(2,1)S(1)}, bf16[64,512]{1,0:T(8,128)(2,1)S(1)}, u32[]{:S(2)}, u32[]{:S(2)}) collective-permute-start(bf16[64,512]{1,0:T(8,128)(2,1)S(1)} %get-tuple-element.20), channel_id=1, source_target_pairs={{0,48},{16,0},{32,16},{48,32},{1,49},{17,1},{33,17},{49,33},{2,50}... | collective-permute-start | bytes 196616 | tf_op jit(solution)/shard_map/ppermute | solution.py:46
  75.3 9.3 %collective-permute-start.5 = (bf16[64,512]{1,0:T(8,128)(2,1)S(1)}, bf16[64,512]{1,0:T(8,128)(2,1)S(1)}, u32[]{:S(2)}, u32[]{:S(2)}) collective-permute-start(bf16[64,512]{1,0:T(8,128)(2,1)S(1)} %get-tuple-element.21), channel_id=1, source_target_pairs={{0,32},{16,48},{32,0},{48,16},{1,33},{17,49},{33,1},{49,17},{2,34}... | collective-permute-start | bytes 196616 | tf_op jit(solution)/shard_map/ppermute | solution.py:46
  104.5 3.2 %copy-start.3 = (bf16[512,512]{1,0:T(8,128)(2,1)}, bf16[512,512]{1,0:T(8,128)(2,1)S(1)}, u32[]{:S(2)}) copy-start(bf16[512,512]{1,0:T(8,128)(2,1)S(1)} %all_gather.6) | copy-start | bytes 1572868
  107.7 19.4 %all-to-all-start.2 = ((bf16[4,128,1024]{2,1,0:T(8,128)(2,1)}), bf16[4,128,1024]{2,1,0:T(8,128)(2,1)}, u32[]{:S(2)}, u32[]{:S(2)}) async-start(bf16[4,128,1024]{2,1,0:T(8,128)(2,1)} %bitcast.75), calls=%async_computation.2 | async-start | bytes 2097152 | tf_op jit(solution)/shard_map/all_to_all | solution.py:24
  129.7 18.1 %copy-start.4 = (bf16[512,512]{1,0:T(8,128)(2,1)S(1)}, bf16[512,512]{1,0:T(8,128)(2,1)}, u32[]{:S(2)}) copy-start(bf16[512,512]{1,0:T(8,128)(2,1)} %copy-done.3) | copy-start | bytes 1572868
  149.4 37.3 %all-to-all-start.4 = ((bf16[32,16,1024]{2,1,0:T(8,128)(2,1)}), bf16[32,16,1024]{2,1,0:T(8,128)(2,1)}, u32[]{:S(2)}, u32[]{:S(2)}) async-start(bf16[32,16,1024]{2,1,0:T(8,128)(2,1)} %bitcast.74), calls=%async_computation.4 | async-start | bytes 2097152 | tf_op jit(solution)/shard_map/all_to_all | solution.py:24
  159.0 40.1 %collective-permute-start.8 = (bf16[1024,1024]{1,0:T(8,128)(2,1)S(1)}, bf16[1024,1024]{1,0:T(8,128)(2,1)}, u32[]{:S(2)}, u32[]{:S(2)}) collective-permute-start(bf16[1024,1024]{1,0:T(8,128)(2,1)S(1)} %copy-done.1), channel_id=1, source_target_pairs={{0,8},{8,0},{1,9},{9,1},{2,10},{10,2},{3,11},{11,3},{4,12},{12,4},... | collective-permute-start | bytes 6291464 | tf_op jit(solution)/shard_map/ppermute | solution.py:46
  202.2 12.6 %all-to-all-start.6 = ((bf16[4,32,1024]{2,1,0:T(8,128)(2,1)}), bf16[4,32,1024]{2,1,0:T(8,128)(2,1)S(1)}, u32[]{:S(2)}, u32[]{:S(2)}) async-start(bf16[4,32,1024]{2,1,0:T(8,128)(2,1)} %bitcast.25), calls=%async_computation.6 | async-start | bytes 524288 | tf_op jit(solution)/shard_map/all_to_all | solution.py:24

commit v3 on v0

--- a/solution.py
+++ b/solution.py
@@ -48,25 +48,18 @@
 def pair_sum(partial, axis):
     half = partial.reshape(4, 2, partial.shape[0] // 8, partial.shape[1])
     mine = lax.axis_index(axis)
-    theirs = shifted(pick(half, 1 - mine, 1).astype(narrow), axis, 1)
-    return pick(half, mine, 1) + theirs.astype(wide)
+    sent, kept = lax.optimization_barrier((pick(half, 1 - mine, 1).astype(narrow), pick(half, mine, 1)))
+    return kept + pick(lax.all_gather(sent, axis), 1 - mine, 0).astype(wide)
 
 
-def ring_sum(halves, axis):
+def ring_sum(blocks, axis):
     mine = lax.axis_index(axis)
-    sent = halves.astype(narrow)
-    total = pick(halves, mine, 0)
-    for step in range(1, 4):
-        total = total + shifted(pick(sent, (mine + step) % 4, 0), axis, step).astype(wide)
+    members = lax.axis_size(axis)
+    sent = blocks.astype(narrow)
+    total = pick(blocks, mine, 0)
+    for step in range(1, members):
+        total = total + shifted(pick(sent, (mine + step) % members, 0), axis, step).astype(wide)
     return total
-
-
-def gather_by_permutes(block, axis):
-    members = lax.axis_size(axis)
-    mine = lax.axis_index(axis)
-    behind = [block] + [shifted(block, axis, step) for step in range(1, members)]
-    placed = [lax.select_n((mine - place) % members, *behind) for place in range(members)]
-    return lax.optimization_barrier(jnp.concatenate(placed, axis=0))
 
 
 def plan(activations, gradients, act_basis, grad_basis, eigen_noise):
@@ -75,16 +68,16 @@
 
     own_rows = lax.dynamic_slice_in_dim(activations, lax.axis_index("x") * slab, slab, 0)
     act_rows = spread(own_rows, "tok")
-    basis_t = gather_by_permutes(act_basis.T, "x")
-
     grad_part = contract(gradients, grad_basis, 1, 0)
-    grad_half = ring_sum(grad_part.reshape(4, slab, grad_part.shape[1]), "x")
+    grad_part = grad_part.reshape(-1, slab, grad_part.shape[1])
+    basis = lax.all_gather(act_basis, "x", axis=1, tiled=True)
+    grad_half = ring_sum(grad_part, "x")
     grad_proj = grad_half + shifted(grad_half.astype(narrow), "yl", 1).astype(wide)
     grad_sq = (grad_proj * grad_proj).astype(narrow)
 
-    act_halves = pair_sum(contract(act_rows, basis_t, 1, 1), "core")
-    act_proj = ring_sum(act_halves, "yh")
-    grad_sq = spread(grad_sq, "tok")
+    act_halves = pair_sum(contract(act_rows, basis, 1, 0), "core")
+    act_proj = scatter_sum(act_halves, "yh")[0]
+    grad_sq = lax.all_gather(grad_sq, "tok", axis=0, tiled=True)
     act_half = lax.all_gather(act_proj.astype(narrow), row, axis=0, tiled=True)
     act_wide = act_half.astype(wide)
     act_sq = (act_wide * act_wide).astype(narrow)

time: 231 us -> 215 us (0.931)
  starting transfers between devices: 72.6 us -> 31.8 us
  blocking collectives: 99.4 us -> 120 us
  between operations: 1.07 us -> 14.3 us
  other arithmetic: 10.1 us -> 4.92 us
    ppermute x12 -> x4, starting transfers between devices: 47.2 us -> 13.9 us  [shifted(): lax.ppermute(block, axis, [(i, (i + step) % members) for i in range(membe...]
    all_to_all x3 -> x4, blocking collectives: 62.7 us -> 75 us  [exchange(): return lax.all_to_all(blocks, axes, 0, 0, tiled=True)]
    all_gather x0 -> x2, blocking collectives: none -> 9.16 us  [pair_sum(): return kept + pick(lax.all_gather(sent, axis), 1 - mine, 0).astype(wide)]
    all_to_all x4 -> x3, starting transfers between devices: 25.5 us -> 17.8 us  [exchange(): return lax.all_to_all(blocks, axes, 0, 0, tiled=True)]
    all_to_all x4 -> x3, waiting for transfers between devices: 20.6 us -> 16.5 us  [exchange(): return lax.all_to_all(blocks, axes, 0, 0, tiled=True)]
    convert_element_type x3 -> x1, other arithmetic: 3.82 us -> 0.87 us  [ring_sum(): sent = blocks.astype(narrow)]
    ppermute x12 -> x4, waiting for transfers between devices: 7.64 us -> 9.13 us  [shifted(): lax.ppermute(block, axis, [(i, (i + step) % members) for i in range(membe...]
    unnamed x15 -> x11, local copies, waits for them, and re-layouts: 4.85 us -> 3.85 us
  transfers between devices with their start and end apart: 16 -> 9, of which waited for: 7 -> 6; matrix products, arithmetic and copies ran while one was open for 7% -> 6% of each run, Pallas kernels for 0% -> 0%
where the time goes in v3:
time: 215 us; the launch traced here: 214 us
  blocking collectives  120 us (56%)
  starting transfers between devices  31.8 us (15%)
  waiting for transfers between devices  26.3 us (12%)
  between operations  14.3 us (7%)
  matrix products  8.57 us (4%)
  local copies, waits for them, and re-layouts  8 us (4%)
  other arithmetic  4.92 us (2%)
    all_to_all x4, blocking collectives, exchange(): return lax.all_to_all(blocks, axes, 0, 0, tiled=True)  75 us
    all_gather x1, blocking collectives, plan(): act_half = lax.all_gather(act_proj.astype(narrow), row, axis=0, tiled=True)  18.2 us
    all_gather x1, blocking collectives, plan(): output_shift = lax.all_gather(shift, row, axis=0, tiled=True)  18.1 us
    all_to_all x3, starting transfers between devices, exchange(): return lax.all_to_all(blocks, axes, 0, 0, tiled=True)  17.8 us
    all_to_all x3, waiting for transfers between devices, exchange(): return lax.all_to_all(blocks, axes, 0, 0, tiled=True)  16.5 us
    ppermute x4, starting transfers between devices, shifted(): lax.ppermute(block, axis, [(i, (i + step) % members) for i in range(membe...  13.9 us
    all_gather x2, blocking collectives, pair_sum(): return kept + pick(lax.all_gather(sent, axis), 1 - mine, 0).astype(wide)  9.16 us
    ppermute x4, waiting for transfers between devices, shifted(): lax.ppermute(block, axis, [(i, (i + step) % members) for i in range(membe...  9.13 us
  transfers between devices with their start and end apart: 9, of which 6 were waited for; matrix products, arithmetic and copies ran while one was open for 6% of the time, Pallas kernels for 0%

profile of v3, /device:TPU:1, one launch (start us, length us, event | category | flops | bytes accessed | tf_op | source)
XLA Modules:
  0.0 214.3 jit_solution(7111973549212509468)
XLA Ops:
  7.2 0.0 copy-start
  7.2 0.0 all-gather.5.cloned.1.call-start
  7.2 0.7 all-gather.5.cloned.1.call-update
  7.9 0.9 constant_dynamic-slice_fusion
  8.8 1.1 broadcast_in_dim.6
  10.0 10.9 %all-to-all-start = ((bf16[8,64,1024]{2,1,0:T(8,128)(2,1)}), bf16[8,64,1024]{2,1,0:T(8,128)(2,1)}, u32[]{:S(2)}, u32[]{:S(2)}) async-start(bf16[8,64,1024]{2,1,0:T(8,128)(2,1)} %broadcast_in_dim.6), calls=%async_computation | async-start | bytes 2097152 | tf_op jit(solution)/shard_map/all_to_all | solution.py:23
  20.8 0.0 all-gather.7.cloned.1.call-start
  20.9 0.0 copy-done
  20.9 1.7 fusion.12
  22.7 0.9 convert_element_type.84
  23.5 1.8 dynamic-slice_bitcast_fusion.4
  25.3 3.1 %collective-permute-start = (bf16[64,1024]{1,0:T(8,128)(2,1)}, bf16[64,1024]{1,0:T(8,128)(2,1)S(1)}, u32[]{:S(2)}, u32[]{:S(2)}) collective-permute-start(bf16[64,1024]{1,0:T(8,128)(2,1)} %get-tuple-element.14), channel_id=1, source_target_pairs={{0,2},{2,4},{4,6},{6,0},{1,3},{3,5},{5,7},{7,1},{8,10},{10,12},{12... | collective-permute-start | bytes 393224 | tf_op jit(solution)/shard_map/ppermute | solution.py:45
  28.4 4.4 %collective-permute-start.1 = (bf16[64,1024]{1,0:T(8,128)(2,1)}, bf16[64,1024]{1,0:T(8,128)(2,1)S(1)}, u32[]{:S(2)}, u32[]{:S(2)}) collective-permute-start(bf16[64,1024]{1,0:T(8,128)(2,1)} %get-tuple-element.16), channel_id=1, source_target_pairs={{0,4},{2,6},{4,0},{6,2},{1,5},{3,7},{5,1},{7,3},{8,12},{10,14},{12... | collective-permute-start | bytes 393224 | tf_op jit(solution)/shard_map/ppermute | solution.py:45
  32.8 3.1 %collective-permute-start.2 = (bf16[64,1024]{1,0:T(8,128)(2,1)}, bf16[64,1024]{1,0:T(8,128)(2,1)S(1)}, u32[]{:S(2)}, u32[]{:S(2)}) collective-permute-start(bf16[64,1024]{1,0:T(8,128)(2,1)} %get-tuple-element.15), channel_id=1, source_target_pairs={{0,6},{2,0},{4,2},{6,4},{1,7},{3,1},{5,3},{7,5},{8,14},{10,8},{12,... | collective-permute-start | bytes 393224 | tf_op jit(solution)/shard_map/ppermute | solution.py:45
  35.9 0.0 collective-permute-done
  35.9 4.4 %collective-permute-done.1 = bf16[64,1024]{1,0:T(8,128)(2,1)S(1)} collective-permute-done((bf16[64,1024]{1,0:T(8,128)(2,1)}, bf16[64,1024]{1,0:T(8,128)(2,1)S(1)}, u32[]{:S(2)}, u32[]{:S(2)}) %collective-permute-start.1) | collective-permute-done | bytes 131104 | tf_op jit(solution)/shard_map/ppermute | solution.py:45
  40.2 2.0 collective-permute-done.2
  42.3 0.1 fusion.11
  42.3 3.4 %collective-permute-start.3 = (bf16[64,1024]{1,0:T(8,128)(2,1)S(1)}, bf16[64,1024]{1,0:T(8,128)(2,1)S(1)}, u32[]{:S(2)}, u32[]{:S(2)}) collective-permute-start(bf16[64,1024]{1,0:T(8,128)(2,1)S(1)} %fusion.11), channel_id=1, source_target_pairs={{0,1},{1,0},{2,3},{3,2},{4,5},{5,4},{6,7},{7,6},{8,9},{9,8},{10,11... | collective-permute-start | bytes 393224 | tf_op jit(solution)/shard_map/ppermute | solution.py:45
  45.7 2.7 %collective-permute-done.3 = bf16[64,1024]{1,0:T(8,128)(2,1)S(1)} collective-permute-done((bf16[64,1024]{1,0:T(8,128)(2,1)S(1)}, bf16[64,1024]{1,0:T(8,128)(2,1)S(1)}, u32[]{:S(2)}, u32[]{:S(2)}) %collective-permute-start.3) | collective-permute-done | bytes 131104 | tf_op jit(solution)/shard_map/ppermute | solution.py:45
  48.5 0.7 multiply_convert_fusion.2
  49.2 0.0 all-gather.7.cloned.1.call-update
  49.2 0.0 all-gather.5.cloned.1.call-done
  49.3 0.8 all-to-all-done
  50.1 2.2 %fusion.2 = f32[4,2,64,512]{3,2,1,0:T(8,128)S(1)} fusion(bf16[4,2,64,1024]{3,2,1,0:T(8,128)(2,1)} %bitcast, bf16[1024,512]{1,0:T(8,128)(2,1)} %all-gather.5.cloned.1.call-done), kind=kOutput, calls=%fused_computation.5 | convolution fusion | flops 536870912 | bytes 3145728 | tf_op jit(solution)/shard_map/dot_general | solution.py:14
  52.5 3.8 %all-gather = bf16[8,64,512]{2,1,0:T(8,128)(2,1)S(1)} all-gather(bf16[4,64,512]{2,1,0:T(8,128)(2,1)S(1)} %fusion.7), channel_id=2, replica_groups=mesh['tok'=8,'yh'=4,'core'=2,'x'=4,'yl'=2] {'core'}, dimensions={0}, use_global_device_ids=true | all-gather | bytes 786432 | tf_op jit(solution)/shard_map/all_gather | solution.py:52
  56.2 0.1 fusion.5
  56.3 16.1 %all_to_all.49 = bf16[4,64,512]{2,1,0:T(8,128)(2,1)S(1)} all-to-all(bf16[4,64,512]{2,1,0:T(8,128)(2,1)S(1)} %fusion.5), channel_id=1, replica_groups=mesh['tok'=8,'yh'=4,'core'=2,'x'=4,'yl'=2] {'yh'}, dimensions={0} | all-to-all | bytes 524288 | tf_op jit(solution)/shard_map/all_to_all | solution.py:23
  72.4 18.2 %all_gather.27 = bf16[512,512]{1,0:T(8,128)(2,1)S(1)} all-gather(bf16[64,512]{1,0:T(8,128)(2,1)S(1)} %reduce_sum.45), channel_id=1, replica_groups=mesh['tok'=8,'yh'=4,'core'=2,'x'=4,'yl'=2] {'yh','core'}, dimensions={0}, use_global_device_ids=true | all-gather | bytes 589824 | tf_op jit(solution)/shard_map/all_gather | solution.py:81
  90.6 0.0 copy-start.2
  90.6 0.0 all-gather.7.cloned.1.call-done
  90.6 3.1 %convolution_convert_fusion.1 = bf16[512,1024]{1,0:T(8,128)(2,1)} fusion(bf16[512,1024]{1,0:T(8,128)(2,1)} %all-gather.7.cloned.1.call-done, bf16[512,512]{1,0:T(8,128)(2,1)S(1)} %all_gather.27), kind=kOutput, calls=%fused_computation.4 | convolution fusion | flops 538181632 | bytes 2621440 | tf_op jit(solution)/shard_map/dot_general | solution.py:14
  93.8 0.0 copy-done.2
  93.8 3.5 %all-to-all-start.2 = ((bf16[4,128,1024]{2,1,0:T(8,128)(2,1)}), bf16[4,128,1024]{2,1,0:T(8,128)(2,1)S(1)}, u32[]{:S(2)}, u32[]{:S(2)}) async-start(bf16[4,128,1024]{2,1,0:T(8,128)(2,1)} %bitcast.66), calls=%async_computation.2 | async-start | bytes 2097152 | tf_op jit(solution)/shard_map/all_to_all | solution.py:23
  97.3 2.0 copy.8
  99.3 7.7 %all-to-all-done.2 = bf16[4,128,1024]{2,1,0:T(8,128)(2,1)S(1)} async-done(((bf16[4,128,1024]{2,1,0:T(8,128)(2,1)}), bf16[4,128,1024]{2,1,0:T(8,128)(2,1)S(1)}, u32[]{:S(2)}, u32[]{:S(2)}) %all-to-all-start.2) | async-done | bytes 1048608 | tf_op jit(solution)/shard_map/all_to_all | solution.py:23
  107.0 0.2 convert_reduce_fusion
  107.2 1.9 fusion.6
  109.1 0.0 copy-start.3
  109.1 0.1 broadcast_in_dim.7
  109.3 12.3 %all_to_all.50 = bf16[4,128,1024]{2,1,0:T(8,128)(2,1)S(1)} all-to-all(bf16[4,128,1024]{2,1,0:T(8,128)(2,1)S(1)} %broadcast_in_dim.7), channel_id=1, replica_groups=mesh['tok'=8,'yh'=4,'core'=2,'x'=4,'yl'=2] {'x'}, dimensions={0} | all-to-all | bytes 2097152 | tf_op jit(solution)/shard_map/all_to_all | solution.py:23
  121.6 0.0 copy-done.3
  121.6 0.7 convolution_convert_fusion
  122.3 35.2 %all_to_all.51 = bf16[16,32,1024]{2,1,0:T(8,128)(2,1)S(1)} all-to-all(bf16[16,32,1024]{2,1,0:T(8,128)(2,1)S(1)} %bitcast.68), channel_id=1, replica_groups=mesh['tok'=8,'yh'=4,'core'=2,'x'=4,'yl'=2] {'tok','yl'}, dimensions={0} | all-to-all | bytes 2097152 | tf_op jit(solution)/shard_map/all_to_all | solution.py:23
  157.5 0.2 reduce_sum.47
  157.7 0.1 broadcast_in_dim.8
  157.8 11.4 %all_to_all.52 = bf16[8,32,1024]{2,1,0:T(8,128)(2,1)S(1)} all-to-all(bf16[8,32,1024]{2,1,0:T(8,128)(2,1)S(1)} %broadcast_in_dim.8), channel_id=1, replica_groups=mesh['tok'=8,'yh'=4,'core'=2,'x'=4,'yl'=2] {'x','yl'}, dimensions={0} | all-to-all | bytes 1048576 | tf_op jit(solution)/shard_map/all_to_all | solution.py:23
  169.2 0.7 fusion
  169.9 0.0 copy-start.1
  170.0 5.4 %all-gather.1 = bf16[8,32,1024]{2,1,0:T(8,128)(2,1)S(1)} all-gather(bf16[4,32,1024]{2,1,0:T(8,128)(2,1)S(1)} %fusion.8), channel_id=3, replica_groups=mesh['tok'=8,'yh'=4,'core'=2,'x'=4,'yl'=2] {'core'}, dimensions={0}, use_global_device_ids=true | all-gather | bytes 786432 | tf_op jit(solution)/shard_map/all_gather | solution.py:52
  175.4 0.8 fusion.4
  176.2 3.4 %all-to-all-start.6 = ((bf16[4,32,1024]{2,1,0:T(8,128)(2,1)}), bf16[4,32,1024]{2,1,0:T(8,128)(2,1)S(1)}, u32[]{:S(2)}, u32[]{:S(2)}) async-start(bf16[4,32,1024]{2,1,0:T(8,128)(2,1)} %fusion.4), calls=%async_computation.6 | async-start | bytes 524288 | tf_op jit(solution)/shard_map/all_to_all | solution.py:23
  179.6 0.0 copy-done.1
  179.6 1.0 copy.9
  180.6 8.0 %all-to-all-done.6 = bf16[4,32,1024]{2,1,0:T(8,128)(2,1)S(1)} async-done(((bf16[4,32,1024]{2,1,0:T(8,128)(2,1)}), bf16[4,32,1024]{2,1,0:T(8,128)(2,1)S(1)}, u32[]{:S(2)}, u32[]{:S(2)}) %all-to-all-start.6) | async-done | bytes 262176 | tf_op jit(solution)/shard_map/all_to_all | solution.py:23
  188.6 18.1 %all_gather.31 = bf16[256,1024]{1,0:T(8,128)(2,1)S(1)} all-gather(bf16[32,1024]{1,0:T(8,128)(2,1)S(1)} %reduce_sum.48), channel_id=1, replica_groups=mesh['tok'=8,'yh'=4,'core'=2,'x'=4,'yl'=2] {'yh','core'}, dimensions={0}, use_global_device_ids=true | all-gather | bytes 589824 | tf_op jit(solution)/shard_map/all_gather | solution.py:93
  206.7 0.8 copy.13
  (6 shorter events, 0.2 us)
Async XLA Ops:
  7.2 13.7 %copy-start = (bf16[1024,1024]{1,0:T(8,128)(2,1)S(1)}, bf16[1024,1024]{1,0:T(8,128)(2,1)}, u32[]{:S(2)}) copy-start(bf16[1024,1024]{1,0:T(8,128)(2,1)} %param.8) | copy-start | bytes 6291460
  7.2 42.1 %all-gather.5.cloned.1.call-start = ((), (), s32[]{:S(2)}) async-start(), calls=%async_computation.7 | async-start | bytes 1310720 | tf_op jit(solution)/shard_map/all_gather | solution.py:73
  10.0 40.2 %all-to-all-start = ((bf16[8,64,1024]{2,1,0:T(8,128)(2,1)}), bf16[8,64,1024]{2,1,0:T(8,128)(2,1)}, u32[]{:S(2)}, u32[]{:S(2)}) async-start(bf16[8,64,1024]{2,1,0:T(8,128)(2,1)} %broadcast_in_dim.6), calls=%async_computation | async-start | bytes 2097152 | tf_op jit(solution)/shard_map/all_to_all | solution.py:23
  20.8 69.8 %all-gather.7.cloned.1.call-start = ((), (), s32[]{:S(2)}) async-start(), calls=%async_computation.8 | async-start | bytes 1179648 | tf_op jit(solution)/shard_map/all_gather | solution.py:80
  25.3 10.6 %collective-permute-start = (bf16[64,1024]{1,0:T(8,128)(2,1)}, bf16[64,1024]{1,0:T(8,128)(2,1)S(1)}, u32[]{:S(2)}, u32[]{:S(2)}) collective-permute-start(bf16[64,1024]{1,0:T(8,128)(2,1)} %get-tuple-element.14), channel_id=1, source_target_pairs={{0,2},{2,4},{4,6},{6,0},{1,3},{3,5},{5,7},{7,1},{8,10},{10,12},{12... | collective-permute-start | bytes 393224 | tf_op jit(solution)/shard_map/ppermute | solution.py:45
  28.4 11.8 %collective-permute-start.1 = (bf16[64,1024]{1,0:T(8,128)(2,1)}, bf16[64,1024]{1,0:T(8,128)(2,1)S(1)}, u32[]{:S(2)}, u32[]{:S(2)}) collective-permute-start(bf16[64,1024]{1,0:T(8,128)(2,1)} %get-tuple-element.16), channel_id=1, source_target_pairs={{0,4},{2,6},{4,0},{6,2},{1,5},{3,7},{5,1},{7,3},{8,12},{10,14},{12... | collective-permute-start | bytes 393224 | tf_op jit(solution)/shard_map/ppermute | solution.py:45
  32.8 9.5 %collective-permute-start.2 = (bf16[64,1024]{1,0:T(8,128)(2,1)}, bf16[64,1024]{1,0:T(8,128)(2,1)S(1)}, u32[]{:S(2)}, u32[]{:S(2)}) collective-permute-start(bf16[64,1024]{1,0:T(8,128)(2,1)} %get-tuple-element.15), channel_id=1, source_target_pairs={{0,6},{2,0},{4,2},{6,4},{1,7},{3,1},{5,3},{7,5},{8,14},{10,8},{12,... | collective-permute-start | bytes 393224 | tf_op jit(solution)/shard_map/ppermute | solution.py:45
  42.3 6.1 %collective-permute-start.3 = (bf16[64,1024]{1,0:T(8,128)(2,1)S(1)}, bf16[64,1024]{1,0:T(8,128)(2,1)S(1)}, u32[]{:S(2)}, u32[]{:S(2)}) collective-permute-start(bf16[64,1024]{1,0:T(8,128)(2,1)S(1)} %fusion.11), channel_id=1, source_target_pairs={{0,1},{1,0},{2,3},{3,2},{4,5},{5,4},{6,7},{7,6},{8,9},{9,8},{10,11... | collective-permute-start | bytes 393224 | tf_op jit(solution)/shard_map/ppermute | solution.py:45
  90.6 3.1 %copy-start.2 = (bf16[512,512]{1,0:T(8,128)(2,1)}, bf16[512,512]{1,0:T(8,128)(2,1)S(1)}, u32[]{:S(2)}) copy-start(bf16[512,512]{1,0:T(8,128)(2,1)S(1)} %all_gather.27) | copy-start | bytes 1572868
  93.8 13.2 %all-to-all-start.2 = ((bf16[4,128,1024]{2,1,0:T(8,128)(2,1)}), bf16[4,128,1024]{2,1,0:T(8,128)(2,1)S(1)}, u32[]{:S(2)}, u32[]{:S(2)}) async-start(bf16[4,128,1024]{2,1,0:T(8,128)(2,1)} %bitcast.66), calls=%async_computation.2 | async-start | bytes 2097152 | tf_op jit(solution)/shard_map/all_to_all | solution.py:23
  109.1 12.4 %copy-start.3 = (bf16[512,512]{1,0:T(8,128)(2,1)S(1)}, bf16[512,512]{1,0:T(8,128)(2,1)}, u32[]{:S(2)}) copy-start(bf16[512,512]{1,0:T(8,128)(2,1)} %copy-done.2) | copy-start | bytes 1572868
  169.9 9.7 %copy-start.1 = (f32[1024,128]{0,1:T(8,128)S(1)}, f32[1024,128]{0,1:T(8,128)}, u32[]{:S(2)}) copy-start(f32[1024,128]{0,1:T(8,128)} %get-tuple-element.13) | copy-start | bytes 1572868
  176.2 12.4 %all-to-all-start.6 = ((bf16[4,32,1024]{2,1,0:T(8,128)(2,1)}), bf16[4,32,1024]{2,1,0:T(8,128)(2,1)S(1)}, u32[]{:S(2)}, u32[]{:S(2)}) async-start(bf16[4,32,1024]{2,1,0:T(8,128)(2,1)} %fusion.4), calls=%async_computation.6 | async-start | bytes 524288 | tf_op jit(solution)/shard_map/all_to_all | solution.py:23
Sparse Core Ops, SparseCore 0:
  10.1 38.2 all-gather.4
  51.0 38.6 all-gather.6

commit v4 on v3

--- a/solution.py
+++ b/solution.py
@@ -55,10 +55,9 @@
 def ring_sum(blocks, axis):
     mine = lax.axis_index(axis)
     members = lax.axis_size(axis)
-    sent = blocks.astype(narrow)
-    total = pick(blocks, mine, 0)
-    for step in range(1, members):
-        total = total + shifted(pick(sent, (mine + step) % members, 0), axis, step).astype(wide)
+    total = pick(blocks, mine, 0).astype(wide)
+    for step in sorted(range(1, members), key=lambda step: abs(2 * step - members)):
+        total = total + shifted(pick(blocks, (mine + step) % members, 0), axis, step).astype(wide)
     return total
 
 
@@ -68,7 +67,7 @@
 
     own_rows = lax.dynamic_slice_in_dim(activations, lax.axis_index("x") * slab, slab, 0)
     act_rows = spread(own_rows, "tok")
-    grad_part = contract(gradients, grad_basis, 1, 0)
+    grad_part = contract(gradients, grad_basis, 1, 0).astype(narrow)
     grad_part = grad_part.reshape(-1, slab, grad_part.shape[1])
     basis = lax.all_gather(act_basis, "x", axis=1, tiled=True)
     grad_half = ring_sum(grad_part, "x")
@@ -82,8 +81,12 @@
     act_wide = act_half.astype(wide)
     act_sq = (act_wide * act_wide).astype(narrow)
 
-    scales_t = scatter_sum(contract(act_sq, grad_sq, 0, 0), "x") / token_count
-    scaled_t = (eigen_noise.T * lax.rsqrt(token_count * (scales_t + damping))).astype(narrow)
+    summed_t = scatter_sum(contract(act_sq, grad_sq, 0, 0), "x")
+    summed_t = lax.optimization_barrier(summed_t)
+    spread_t = token_count * (summed_t / token_count + damping)
+    scaled_t = (eigen_noise.T * lax.rsqrt(spread_t)).astype(narrow)
+    scaled_t, summed_t = lax.optimization_barrier((scaled_t, summed_t))
+    scales = (summed_t / token_count).T
     widened_t = spread(scaled_t, "x")
 
     hidden = scatter_sum(contract(act_half, widened_t, 1, 0), ("tok", "yl")).astype(narrow)
@@ -91,7 +94,7 @@
     halves = pair_sum(contract(hidden, grad_basis, 1, 1), "core")
     shift = scatter_sum(halves, "yh")[0].astype(narrow)
     output_shift = lax.all_gather(shift, row, axis=0, tiled=True)
-    return (scales_t.T, output_shift)
+    return (scales, output_shift)
 
 
 def solution(mesh):

time: 215 us -> 215 us (level)
    convert_element_type x2 -> x1, other arithmetic: 2.81 us -> 0.1 us  [plan(): scaled_t = (eigen_noise.T * lax.rsqrt(spread_t)).astype(narrow)]
    reduce_sum x4, other arithmetic: 0.46 us -> 2.96 us  [scatter_sum(): return jnp.sum(parts.astype(wide), axis=0)]
  transfers between devices with their start and end apart: 9 -> 9, of which waited for: 6 -> 6; matrix products, arithmetic and copies ran while one was open for 6% -> 5% of each run, Pallas kernels for 0% -> 0%
where the time goes in v4:
time: 215 us; the launch traced here: 214 us
  blocking collectives  119 us (55%)
  starting transfers between devices  33 us (15%)
  waiting for transfers between devices  26.1 us (12%)
  between operations  14.3 us (7%)
  matrix products  8.24 us (4%)
  local copies, waits for them, and re-layouts  6.98 us (3%)
  other arithmetic  6.57 us (3%)
    all_to_all x4, blocking collectives, exchange(): return lax.all_to_all(blocks, axes, 0, 0, tiled=True)  74.8 us
    all_to_all x3, starting transfers between devices, exchange(): return lax.all_to_all(blocks, axes, 0, 0, tiled=True)  18.7 us
    all_gather x1, blocking collectives, plan(): output_shift = lax.all_gather(shift, row, axis=0, tiled=True)  18.1 us
    all_to_all x3, waiting for transfers between devices, exchange(): return lax.all_to_all(blocks, axes, 0, 0, tiled=True)  17.9 us
    all_gather x1, blocking collectives, plan(): act_half = lax.all_gather(act_proj.astype(narrow), row, axis=0, tiled=True)  17.6 us
    ppermute x4, starting transfers between devices, shifted(): lax.ppermute(block, axis, [(i, (i + step) % members) for i in range(membe...  14.2 us
    dot_general x5, matrix products, contract(): lax.dot_general(former, latter, (((former_dim,), (latter_dim,)), ((), ())...  8.24 us
    all_gather x2, blocking collectives, pair_sum(): return kept + pick(lax.all_gather(sent, axis), 1 - mine, 0).astype(wide)  8.04 us
  transfers between devices with their start and end apart: 9, of which 6 were waited for; matrix products, arithmetic and copies ran while one was open for 5% of the time, Pallas kernels for 0%

profile of v4, /device:TPU:1, one launch (start us, length us, event | category | flops | bytes accessed | tf_op | source)
XLA Modules:
  0.0 213.7 jit_solution(9270405010622773800)
XLA Ops:
  7.2 0.0 copy-start
  7.2 0.0 all-gather.5.cloned.1.call-start
  7.2 0.7 all-gather.5.cloned.1.call-update
  7.9 0.9 constant_dynamic-slice_fusion
  8.8 1.1 broadcast_in_dim.6
  10.0 10.9 %all-to-all-start = ((bf16[8,64,1024]{2,1,0:T(8,128)(2,1)}), bf16[8,64,1024]{2,1,0:T(8,128)(2,1)S(1)}, u32[]{:S(2)}, u32[]{:S(2)}) async-start(bf16[8,64,1024]{2,1,0:T(8,128)(2,1)} %broadcast_in_dim.6), calls=%async_computation | async-start | bytes 2097152 | tf_op jit(solution)/shard_map/all_to_all | solution.py:23
  20.8 0.0 all-gather.7.cloned.1.call-start
  20.9 0.0 copy-done
  20.9 1.8 convolution_convert_fusion.2
  22.7 0.0 copy-start.1
  22.7 0.8 copy-done.1
  23.5 0.7 dynamic-slice_bitcast_fusion.4
  24.2 4.6 %collective-permute-start = (bf16[64,1024]{1,0:T(8,128)(2,1)}, bf16[64,1024]{1,0:T(8,128)(2,1)S(1)}, u32[]{:S(2)}, u32[]{:S(2)}) collective-permute-start(bf16[64,1024]{1,0:T(8,128)(2,1)} %get-tuple-element.16), channel_id=1, source_target_pairs={{0,4},{2,6},{4,0},{6,2},{1,5},{3,7},{5,1},{7,3},{8,12},{10,14},{12... | collective-permute-start | bytes 393224 | tf_op jit(solution)/shard_map/ppermute | solution.py:45
  28.9 2.2 %collective-permute-start.1 = (bf16[64,1024]{1,0:T(8,128)(2,1)}, bf16[64,1024]{1,0:T(8,128)(2,1)S(1)}, u32[]{:S(2)}, u32[]{:S(2)}) collective-permute-start(bf16[64,1024]{1,0:T(8,128)(2,1)} %get-tuple-element.18), channel_id=1, source_target_pairs={{0,2},{2,4},{4,6},{6,0},{1,3},{3,5},{5,7},{7,1},{8,10},{10,12},{12... | collective-permute-start | bytes 393224 | tf_op jit(solution)/shard_map/ppermute | solution.py:45
  31.1 4.3 %collective-permute-start.2 = (bf16[64,1024]{1,0:T(8,128)(2,1)}, bf16[64,1024]{1,0:T(8,128)(2,1)S(1)}, u32[]{:S(2)}, u32[]{:S(2)}) collective-permute-start(bf16[64,1024]{1,0:T(8,128)(2,1)} %get-tuple-element.17), channel_id=1, source_target_pairs={{0,6},{2,0},{4,2},{6,4},{1,7},{3,1},{5,3},{7,5},{8,14},{10,8},{12,... | collective-permute-start | bytes 393224 | tf_op jit(solution)/shard_map/ppermute | solution.py:45
  35.4 0.0 collective-permute-done
  35.4 4.2 %collective-permute-done.1 = bf16[64,1024]{1,0:T(8,128)(2,1)S(1)} collective-permute-done((bf16[64,1024]{1,0:T(8,128)(2,1)}, bf16[64,1024]{1,0:T(8,128)(2,1)S(1)}, u32[]{:S(2)}, u32[]{:S(2)}) %collective-permute-start.1) | collective-permute-done | bytes 131104 | tf_op jit(solution)/shard_map/ppermute | solution.py:45
  39.7 0.0 collective-permute-done.2
  39.7 1.0 fusion.11
  40.6 3.1 %collective-permute-start.3 = (bf16[64,1024]{1,0:T(8,128)(2,1)S(1)}, bf16[64,1024]{1,0:T(8,128)(2,1)S(1)}, u32[]{:S(2)}, u32[]{:S(2)}) collective-permute-start(bf16[64,1024]{1,0:T(8,128)(2,1)S(1)} %fusion.11), channel_id=1, source_target_pairs={{0,1},{1,0},{2,3},{3,2},{4,5},{5,4},{6,7},{7,6},{8,9},{9,8},{10,11... | collective-permute-start | bytes 393224 | tf_op jit(solution)/shard_map/ppermute | solution.py:45
  43.8 2.9 %collective-permute-done.3 = bf16[64,1024]{1,0:T(8,128)(2,1)S(1)} collective-permute-done((bf16[64,1024]{1,0:T(8,128)(2,1)S(1)}, bf16[64,1024]{1,0:T(8,128)(2,1)S(1)}, u32[]{:S(2)}, u32[]{:S(2)}) %collective-permute-start.3) | collective-permute-done | bytes 131104 | tf_op jit(solution)/shard_map/ppermute | solution.py:45
  46.7 1.7 multiply_convert_fusion.2
  48.3 0.0 all-gather.7.cloned.1.call-update
  48.4 0.3 all-gather.5.cloned.1.call-done
  48.7 1.3 all-to-all-done
  50.0 1.9 fusion.2
  52.1 2.8 %all-gather = bf16[8,64,512]{2,1,0:T(8,128)(2,1)S(1)} all-gather(bf16[4,64,512]{2,1,0:T(8,128)(2,1)S(1)} %fusion.7), channel_id=2, replica_groups=mesh['tok'=8,'yh'=4,'core'=2,'x'=4,'yl'=2] {'core'}, dimensions={0}, use_global_device_ids=true | all-gather | bytes 786432 | tf_op jit(solution)/shard_map/all_gather | solution.py:52
  54.9 0.1 fusion.5
  54.9 16.4 %all_to_all.49 = bf16[4,64,512]{2,1,0:T(8,128)(2,1)S(1)} all-to-all(bf16[4,64,512]{2,1,0:T(8,128)(2,1)S(1)} %fusion.5), channel_id=1, replica_groups=mesh['tok'=8,'yh'=4,'core'=2,'x'=4,'yl'=2] {'yh'}, dimensions={0} | all-to-all | bytes 524288 | tf_op jit(solution)/shard_map/all_to_all | solution.py:23
  71.3 17.6 %all_gather.27 = bf16[512,512]{1,0:T(8,128)(2,1)S(1)} all-gather(bf16[64,512]{1,0:T(8,128)(2,1)S(1)} %reduce_sum.45), channel_id=1, replica_groups=mesh['tok'=8,'yh'=4,'core'=2,'x'=4,'yl'=2] {'yh','core'}, dimensions={0}, use_global_device_ids=true | all-gather | bytes 589824 | tf_op jit(solution)/shard_map/all_gather | solution.py:80
  89.0 0.0 copy-start.2
  89.0 0.0 all-gather.7.cloned.1.call-done
  89.0 3.1 %convolution_convert_fusion.1 = bf16[512,1024]{1,0:T(8,128)(2,1)} fusion(bf16[512,1024]{1,0:T(8,128)(2,1)} %all-gather.7.cloned.1.call-done, bf16[512,512]{1,0:T(8,128)(2,1)S(1)} %all_gather.27), kind=kOutput, calls=%fused_computation.4 | convolution fusion | flops 538181632 | bytes 2621440 | tf_op jit(solution)/shard_map/dot_general | solution.py:14
  92.1 0.0 copy-done.2
  92.1 4.4 %all-to-all-start.2 = ((bf16[4,128,1024]{2,1,0:T(8,128)(2,1)}), bf16[4,128,1024]{2,1,0:T(8,128)(2,1)}, u32[]{:S(2)}, u32[]{:S(2)}) async-start(bf16[4,128,1024]{2,1,0:T(8,128)(2,1)} %bitcast.13), calls=%async_computation.2 | async-start | bytes 2097152 | tf_op jit(solution)/shard_map/all_to_all | solution.py:23
  96.5 1.2 copy.8
  97.7 8.6 %all-to-all-done.2 = bf16[4,128,1024]{2,1,0:T(8,128)(2,1)} async-done(((bf16[4,128,1024]{2,1,0:T(8,128)(2,1)}), bf16[4,128,1024]{2,1,0:T(8,128)(2,1)}, u32[]{:S(2)}, u32[]{:S(2)}) %all-to-all-start.2) | async-done | bytes 1048608 | tf_op jit(solution)/shard_map/all_to_all | solution.py:23
  106.4 1.5 convert_reduce_fusion
  107.8 0.0 copy-start.3
  107.8 0.1 fusion.6
  107.9 0.1 broadcast_in_dim.7
  108.1 12.2 %all_to_all.50 = bf16[4,128,1024]{2,1,0:T(8,128)(2,1)S(1)} all-to-all(bf16[4,128,1024]{2,1,0:T(8,128)(2,1)S(1)} %broadcast_in_dim.7), channel_id=1, replica_groups=mesh['tok'=8,'yh'=4,'core'=2,'x'=4,'yl'=2] {'x'}, dimensions={0} | all-to-all | bytes 2097152 | tf_op jit(solution)/shard_map/all_to_all | solution.py:23
  120.2 0.0 copy-done.3
  120.2 0.7 convolution_convert_fusion
  120.9 34.9 %all_to_all.51 = bf16[16,32,1024]{2,1,0:T(8,128)(2,1)} all-to-all(bf16[16,32,1024]{2,1,0:T(8,128)(2,1)S(1)} %bitcast.62), channel_id=1, replica_groups=mesh['tok'=8,'yh'=4,'core'=2,'x'=4,'yl'=2] {'tok','yl'}, dimensions={0} | all-to-all | bytes 2097152 | tf_op jit(solution)/shard_map/all_to_all | solution.py:23
  155.9 1.4 reduce_sum.47
  157.3 0.1 broadcast_in_dim.8
  157.3 11.3 %all_to_all.52 = bf16[8,32,1024]{2,1,0:T(8,128)(2,1)S(1)} all-to-all(bf16[8,32,1024]{2,1,0:T(8,128)(2,1)S(1)} %broadcast_in_dim.8), channel_id=1, replica_groups=mesh['tok'=8,'yh'=4,'core'=2,'x'=4,'yl'=2] {'x','yl'}, dimensions={0} | all-to-all | bytes 1048576 | tf_op jit(solution)/shard_map/all_to_all | solution.py:23
  168.7 0.7 fusion
  169.5 5.2 %all-gather.1 = bf16[8,32,1024]{2,1,0:T(8,128)(2,1)S(1)} all-gather(bf16[4,32,1024]{2,1,0:T(8,128)(2,1)S(1)} %fusion.8), channel_id=3, replica_groups=mesh['tok'=8,'yh'=4,'core'=2,'x'=4,'yl'=2] {'core'}, dimensions={0}, use_global_device_ids=true | all-gather | bytes 786432 | tf_op jit(solution)/shard_map/all_gather | solution.py:52
  174.8 0.8 fusion.4
  175.5 3.4 %all-to-all-start.6 = ((bf16[4,32,1024]{2,1,0:T(8,128)(2,1)}), bf16[4,32,1024]{2,1,0:T(8,128)(2,1)S(1)}, u32[]{:S(2)}, u32[]{:S(2)}) async-start(bf16[4,32,1024]{2,1,0:T(8,128)(2,1)} %fusion.4), calls=%async_computation.6 | async-start | bytes 524288 | tf_op jit(solution)/shard_map/all_to_all | solution.py:23
  179.0 1.0 copy.9
  180.0 7.9 %all-to-all-done.6 = bf16[4,32,1024]{2,1,0:T(8,128)(2,1)S(1)} async-done(((bf16[4,32,1024]{2,1,0:T(8,128)(2,1)}), bf16[4,32,1024]{2,1,0:T(8,128)(2,1)S(1)}, u32[]{:S(2)}, u32[]{:S(2)}) %all-to-all-start.6) | async-done | bytes 262176 | tf_op jit(solution)/shard_map/all_to_all | solution.py:23
  187.9 18.1 %all_gather.31 = bf16[256,1024]{1,0:T(8,128)(2,1)S(1)} all-gather(bf16[32,1024]{1,0:T(8,128)(2,1)S(1)} %reduce_sum.48), channel_id=1, replica_groups=mesh['tok'=8,'yh'=4,'core'=2,'x'=4,'yl'=2] {'yh','core'}, dimensions={0}, use_global_device_ids=true | all-gather | bytes 589824 | tf_op jit(solution)/shard_map/all_gather | solution.py:96
  206.1 0.8 copy.13
  (7 shorter events, 0.3 us)
Async XLA Ops:
  7.2 13.8 %copy-start = (bf16[1024,1024]{1,0:T(8,128)(2,1)S(1)}, bf16[1024,1024]{1,0:T(8,128)(2,1)}, u32[]{:S(2)}) copy-start(bf16[1024,1024]{1,0:T(8,128)(2,1)} %param.8) | copy-start | bytes 6291460
  7.2 41.5 %all-gather.5.cloned.1.call-start = ((), (), s32[]{:S(2)}) async-start(), calls=%async_computation.7 | async-start | bytes 1310720 | tf_op jit(solution)/shard_map/all_gather | solution.py:72
  10.0 40.0 %all-to-all-start = ((bf16[8,64,1024]{2,1,0:T(8,128)(2,1)}), bf16[8,64,1024]{2,1,0:T(8,128)(2,1)S(1)}, u32[]{:S(2)}, u32[]{:S(2)}) async-start(bf16[8,64,1024]{2,1,0:T(8,128)(2,1)} %broadcast_in_dim.6), calls=%async_computation | async-start | bytes 2097152 | tf_op jit(solution)/shard_map/all_to_all | solution.py:23
  20.8 68.1 %all-gather.7.cloned.1.call-start = ((), (), s32[]{:S(2)}) async-start(), calls=%async_computation.8 | async-start | bytes 1179648 | tf_op jit(solution)/shard_map/all_gather | solution.py:79
  22.7 0.8 copy-start.1
  24.2 11.2 %collective-permute-start = (bf16[64,1024]{1,0:T(8,128)(2,1)}, bf16[64,1024]{1,0:T(8,128)(2,1)S(1)}, u32[]{:S(2)}, u32[]{:S(2)}) collective-permute-start(bf16[64,1024]{1,0:T(8,128)(2,1)} %get-tuple-element.16), channel_id=1, source_target_pairs={{0,4},{2,6},{4,0},{6,2},{1,5},{3,7},{5,1},{7,3},{8,12},{10,14},{12... | collective-permute-start | bytes 393224 | tf_op jit(solution)/shard_map/ppermute | solution.py:45
  28.9 10.8 %collective-permute-start.1 = (bf16[64,1024]{1,0:T(8,128)(2,1)}, bf16[64,1024]{1,0:T(8,128)(2,1)S(1)}, u32[]{:S(2)}, u32[]{:S(2)}) collective-permute-start(bf16[64,1024]{1,0:T(8,128)(2,1)} %get-tuple-element.18), channel_id=1, source_target_pairs={{0,2},{2,4},{4,6},{6,0},{1,3},{3,5},{5,7},{7,1},{8,10},{10,12},{12... | collective-permute-start | bytes 393224 | tf_op jit(solution)/shard_map/ppermute | solution.py:45
  31.1 8.5 %collective-permute-start.2 = (bf16[64,1024]{1,0:T(8,128)(2,1)}, bf16[64,1024]{1,0:T(8,128)(2,1)S(1)}, u32[]{:S(2)}, u32[]{:S(2)}) collective-permute-start(bf16[64,1024]{1,0:T(8,128)(2,1)} %get-tuple-element.17), channel_id=1, source_target_pairs={{0,6},{2,0},{4,2},{6,4},{1,7},{3,1},{5,3},{7,5},{8,14},{10,8},{12,... | collective-permute-start | bytes 393224 | tf_op jit(solution)/shard_map/ppermute | solution.py:45
  40.6 6.1 %collective-permute-start.3 = (bf16[64,1024]{1,0:T(8,128)(2,1)S(1)}, bf16[64,1024]{1,0:T(8,128)(2,1)S(1)}, u32[]{:S(2)}, u32[]{:S(2)}) collective-permute-start(bf16[64,1024]{1,0:T(8,128)(2,1)S(1)} %fusion.11), channel_id=1, source_target_pairs={{0,1},{1,0},{2,3},{3,2},{4,5},{5,4},{6,7},{7,6},{8,9},{9,8},{10,11... | collective-permute-start | bytes 393224 | tf_op jit(solution)/shard_map/ppermute | solution.py:45
  89.0 3.1 %copy-start.2 = (bf16[512,512]{1,0:T(8,128)(2,1)}, bf16[512,512]{1,0:T(8,128)(2,1)S(1)}, u32[]{:S(2)}) copy-start(bf16[512,512]{1,0:T(8,128)(2,1)S(1)} %all_gather.27) | copy-start | bytes 1572868
  92.1 14.3 %all-to-all-start.2 = ((bf16[4,128,1024]{2,1,0:T(8,128)(2,1)}), bf16[4,128,1024]{2,1,0:T(8,128)(2,1)}, u32[]{:S(2)}, u32[]{:S(2)}) async-start(bf16[4,128,1024]{2,1,0:T(8,128)(2,1)} %bitcast.13), calls=%async_computation.2 | async-start | bytes 2097152 | tf_op jit(solution)/shard_map/all_to_all | solution.py:23
  107.8 12.4 %copy-start.3 = (bf16[512,512]{1,0:T(8,128)(2,1)S(1)}, bf16[512,512]{1,0:T(8,128)(2,1)}, u32[]{:S(2)}) copy-start(bf16[512,512]{1,0:T(8,128)(2,1)} %copy-done.2) | copy-start | bytes 1572868
  175.5 12.4 %all-to-all-start.6 = ((bf16[4,32,1024]{2,1,0:T(8,128)(2,1)}), bf16[4,32,1024]{2,1,0:T(8,128)(2,1)S(1)}, u32[]{:S(2)}, u32[]{:S(2)}) async-start(bf16[4,32,1024]{2,1,0:T(8,128)(2,1)} %fusion.4), calls=%async_computation.6 | async-start | bytes 524288 | tf_op jit(solution)/shard_map/all_to_all | solution.py:23
Sparse Core Ops, SparseCore 0:
  10.1 38.5 all-gather.4
  51.3 37.2 all-gather.6

commit v5 on v4

--- a/solution.py
+++ b/solution.py
@@ -1,6 +1,9 @@
 import jax
 import jax.numpy as jnp
 from jax import lax
+from jax.experimental import pallas as pl
+from jax.experimental.layout import Layout, with_layout_constraint
+from jax.experimental.pallas import tpu as pltpu
 from jax.sharding import Mesh, PartitionSpec as P
 
 damping = 0.1
@@ -27,6 +30,26 @@
     members = lax.axis_size(axes)
     copies = jnp.broadcast_to(block[None], (members, *block.shape))
     return exchange(copies.reshape(members * block.shape[0], *block.shape[1:]), axes)
+
+
+def copy_block(place_ref, rows_ref, copy_ref):
+    copy_ref[0] = rows_ref[...]
+
+
+def copies_of_slab(rows, place, slab, copies):
+    width = rows.shape[1]
+    out = pl.pallas_call(
+        copy_block,
+        grid_spec=pltpu.PrefetchScalarGridSpec(
+            num_scalar_prefetch=1,
+            grid=(copies,),
+            in_specs=[pl.BlockSpec((slab, width), lambda step, place_ref: (place_ref[0], 0))],
+            out_specs=pl.BlockSpec((1, slab, width), lambda step, place_ref: (step, 0, 0)),
+        ),
+        out_shape=jax.ShapeDtypeStruct((copies, slab, width), rows.dtype),
+        cost_estimate=pl.CostEstimate(flops=0, bytes_accessed=2 * copies * slab * width, transcendentals=0),
+    )(place.reshape(1).astype(jnp.int32), rows)
+    return out.reshape(copies * slab, width)
 
 
 def scatter_sum(partial, axes):
@@ -65,16 +88,16 @@
     token_count = activations.shape[0] * lax.axis_size("tok")
     slab = activations.shape[0] // lax.axis_size("x")
 
-    own_rows = lax.dynamic_slice_in_dim(activations, lax.axis_index("x") * slab, slab, 0)
-    act_rows = spread(own_rows, "tok")
+    act_rows = exchange(copies_of_slab(activations, lax.axis_index("x"), slab, lax.axis_size("tok")), "tok")
     grad_part = contract(gradients, grad_basis, 1, 0).astype(narrow)
     grad_part = grad_part.reshape(-1, slab, grad_part.shape[1])
-    basis = lax.all_gather(act_basis, "x", axis=1, tiled=True)
+    own_basis_t = with_layout_constraint(act_basis.T, Layout((0, 1)))
+    basis_t = lax.all_gather(own_basis_t, "x", axis=0, tiled=True)
     grad_half = ring_sum(grad_part, "x")
     grad_proj = grad_half + shifted(grad_half.astype(narrow), "yl", 1).astype(wide)
     grad_sq = (grad_proj * grad_proj).astype(narrow)
 
-    act_halves = pair_sum(contract(act_rows, basis, 1, 0), "core")
+    act_halves = pair_sum(contract(act_rows, basis_t, 1, 1), "core")
     act_proj = scatter_sum(act_halves, "yh")[0]
     grad_sq = lax.all_gather(grad_sq, "tok", axis=0, tiled=True)
     act_half = lax.all_gather(act_proj.astype(narrow), row, axis=0, tiled=True)

time: 215 us -> 223 us (1.037)
  blocking collectives: 119 us -> 124 us
  Pallas kernels: 0 us -> 3.64 us
    pallas_call x0 -> x1, Pallas kernels: none -> 3.64 us  [copies_of_slab(): pl.pallas_call(copy_block, grid_spec=pltpu.PrefetchScalarGridSpec(num_sca...]
    all_to_all x4, blocking collectives: 74.8 us -> 77.7 us  [exchange(): return lax.all_to_all(blocks, axes, 0, 0, tiled=True)]
    unnamed x11 -> x12, local copies, waits for them, and re-layouts: 3.83 us -> 5.77 us
  transfers between devices with their start and end apart: 9 -> 9, of which waited for: 6 -> 5; matrix products, arithmetic and copies ran while one was open for 5% -> 4% of each run, Pallas kernels for 0% -> 2%
where the time goes in v5:
time: 223 us; the launch traced here: 222 us
  blocking collectives  124 us (56%)
  starting transfers between devices  32.9 us (15%)
  waiting for transfers between devices  25.4 us (11%)
  between operations  14.3 us (6%)
  matrix products  8.28 us (4%)
  local copies, waits for them, and re-layouts  6.88 us (3%)
  other arithmetic  6.56 us (3%)
  Pallas kernels  3.64 us (2%)
    all_to_all x4, blocking collectives, exchange(): return lax.all_to_all(blocks, axes, 0, 0, tiled=True)  77.7 us
    all_to_all x3, starting transfers between devices, exchange(): return lax.all_to_all(blocks, axes, 0, 0, tiled=True)  18.5 us
    all_gather x1, blocking collectives, plan(): act_half = lax.all_gather(act_proj.astype(narrow), row, axis=0, tiled=True)  18.2 us
    all_gather x1, blocking collectives, plan(): output_shift = lax.all_gather(shift, row, axis=0, tiled=True)  18.1 us
    all_to_all x3, waiting for transfers between devices, exchange(): return lax.all_to_all(blocks, axes, 0, 0, tiled=True)  16.7 us
    ppermute x4, starting transfers between devices, shifted(): lax.ppermute(block, axis, [(i, (i + step) % members) for i in range(membe...  14.4 us
    all_gather x2, blocking collectives, pair_sum(): return kept + pick(lax.all_gather(sent, axis), 1 - mine, 0).astype(wide)  10.1 us
    ppermute x4, waiting for transfers between devices, shifted(): lax.ppermute(block, axis, [(i, (i + step) % members) for i in range(membe...  8.66 us
  transfers between devices with their start and end apart: 9, of which 5 were waited for; matrix products, arithmetic and copies ran while one was open for 4% of the time, Pallas kernels for 2%

profile of v5, /device:TPU:1, one launch (start us, length us, event | category | flops | bytes accessed | tf_op | source)
XLA Modules:
  0.0 222.2 jit_solution(5561908108474849500)
XLA Ops:
  7.2 0.0 copy-start
  7.2 0.0 all-gather.5.cloned.1.call-start
  7.2 1.9 copy.10
  9.2 0.0 all-gather.5.cloned.1.call-update
  9.2 3.6 %shard_map.68 = bf16[8,64,1024]{2,1,0:T(8,128)(2,1)} custom-call(s32[1]{0:T(128)} %bitcast.1.place_ref, bf16[256,1024]{1,0:T(8,128)(2,1)} %rows_ref.1), custom_call_target="tpu_custom_call" | custom-call | bytes 1048576 | tf_op jit(solution)/shard_map/pallas_call | solution.py:41
  12.8 10.9 %all-to-all-start = ((bf16[8,64,1024]{2,1,0:T(8,128)(2,1)}), bf16[8,64,1024]{2,1,0:T(8,128)(2,1)S(1)}, u32[]{:S(2)}, u32[]{:S(2)}) async-start(bf16[8,64,1024]{2,1,0:T(8,128)(2,1)} %shard_map.68), calls=%async_computation | async-start | bytes 2097152 | tf_op jit(solution)/shard_map/all_to_all | solution.py:26
  23.7 0.0 all-gather.7.cloned.1.call-start
  23.8 0.0 copy-done
  23.8 1.8 convolution_convert_fusion.2
  25.5 0.0 copy-start.1
  25.5 0.8 copy-done.1
  26.3 0.8 dynamic-slice_bitcast_fusion.4
  27.1 4.6 %collective-permute-start = (bf16[64,1024]{1,0:T(8,128)(2,1)}, bf16[64,1024]{1,0:T(8,128)(2,1)S(1)}, u32[]{:S(2)}, u32[]{:S(2)}) collective-permute-start(bf16[64,1024]{1,0:T(8,128)(2,1)} %get-tuple-element.16), channel_id=1, source_target_pairs={{0,4},{2,6},{4,0},{6,2},{1,5},{3,7},{5,1},{7,3},{8,12},{10,14},{12... | collective-permute-start | bytes 393224 | tf_op jit(solution)/shard_map/ppermute | solution.py:68
  31.8 2.2 collective-permute-start.1
  34.0 4.3 %collective-permute-start.2 = (bf16[64,1024]{1,0:T(8,128)(2,1)}, bf16[64,1024]{1,0:T(8,128)(2,1)S(1)}, u32[]{:S(2)}, u32[]{:S(2)}) collective-permute-start(bf16[64,1024]{1,0:T(8,128)(2,1)} %get-tuple-element.17), channel_id=1, source_target_pairs={{0,6},{2,0},{4,2},{6,4},{1,7},{3,1},{5,3},{7,5},{8,14},{10,8},{12,... | collective-permute-start | bytes 393224 | tf_op jit(solution)/shard_map/ppermute | solution.py:68
  38.3 0.0 collective-permute-done
  38.3 4.9 %collective-permute-done.1 = bf16[64,1024]{1,0:T(8,128)(2,1)S(1)} collective-permute-done((bf16[64,1024]{1,0:T(8,128)(2,1)}, bf16[64,1024]{1,0:T(8,128)(2,1)S(1)}, u32[]{:S(2)}, u32[]{:S(2)}) %collective-permute-start.1) | collective-permute-done | bytes 131104 | tf_op jit(solution)/shard_map/ppermute | solution.py:68
  43.2 1.0 collective-permute-done.2
  44.2 1.0 fusion.11
  45.1 3.2 %collective-permute-start.3 = (bf16[64,1024]{1,0:T(8,128)(2,1)S(1)}, bf16[64,1024]{1,0:T(8,128)(2,1)S(1)}, u32[]{:S(2)}, u32[]{:S(2)}) collective-permute-start(bf16[64,1024]{1,0:T(8,128)(2,1)S(1)} %fusion.11), channel_id=1, source_target_pairs={{0,1},{1,0},{2,3},{3,2},{4,5},{5,4},{6,7},{7,6},{8,9},{9,8},{10,11... | collective-permute-start | bytes 393224 | tf_op jit(solution)/shard_map/ppermute | solution.py:68
  48.4 2.8 %collective-permute-done.3 = bf16[64,1024]{1,0:T(8,128)(2,1)S(1)} collective-permute-done((bf16[64,1024]{1,0:T(8,128)(2,1)S(1)}, bf16[64,1024]{1,0:T(8,128)(2,1)S(1)}, u32[]{:S(2)}, u32[]{:S(2)}) %collective-permute-start.3) | collective-permute-done | bytes 131104 | tf_op jit(solution)/shard_map/ppermute | solution.py:68
  51.2 1.7 multiply_convert_fusion.2
  52.8 0.0 all-gather.7.cloned.1.call-update
  52.8 0.0 all-gather.5.cloned.1.call-done
  52.9 0.0 all-to-all-done
  52.9 2.0 fusion.2
  55.0 4.6 %all-gather = bf16[8,64,512]{2,1,0:T(8,128)(2,1)S(1)} all-gather(bf16[4,64,512]{2,1,0:T(8,128)(2,1)S(1)} %fusion.7), channel_id=2, replica_groups=mesh['tok'=8,'yh'=4,'core'=2,'x'=4,'yl'=2] {'core'}, dimensions={0}, use_global_device_ids=true | all-gather | bytes 786432 | tf_op jit(solution)/shard_map/all_gather | solution.py:75
  59.6 0.1 fusion.5
  59.6 16.0 %all_to_all.49 = bf16[4,64,512]{2,1,0:T(8,128)(2,1)S(1)} all-to-all(bf16[4,64,512]{2,1,0:T(8,128)(2,1)S(1)} %fusion.5), channel_id=1, replica_groups=mesh['tok'=8,'yh'=4,'core'=2,'x'=4,'yl'=2] {'yh'}, dimensions={0} | all-to-all | bytes 524288 | tf_op jit(solution)/shard_map/all_to_all | solution.py:26
  75.7 18.2 %all_gather.27 = bf16[512,512]{1,0:T(8,128)(2,1)S(1)} all-gather(bf16[64,512]{1,0:T(8,128)(2,1)S(1)} %reduce_sum.45), channel_id=1, replica_groups=mesh['tok'=8,'yh'=4,'core'=2,'x'=4,'yl'=2] {'yh','core'}, dimensions={0}, use_global_device_ids=true | all-gather | bytes 589824 | tf_op jit(solution)/shard_map/all_gather | solution.py:103
  93.9 0.0 copy-start.2
  93.9 0.0 all-gather.7.cloned.1.call-done
  93.9 3.1 %convolution_convert_fusion.1 = bf16[512,1024]{1,0:T(8,128)(2,1)} fusion(bf16[512,1024]{1,0:T(8,128)(2,1)} %all-gather.7.cloned.1.call-done, bf16[512,512]{1,0:T(8,128)(2,1)S(1)} %all_gather.27), kind=kOutput, calls=%fused_computation.4 | convolution fusion | flops 538181632 | bytes 2621440 | tf_op jit(solution)/shard_map/dot_general | solution.py:17
  97.0 0.0 copy-done.2
  97.0 4.3 %all-to-all-start.2 = ((bf16[4,128,1024]{2,1,0:T(8,128)(2,1)}), bf16[4,128,1024]{2,1,0:T(8,128)(2,1)}, u32[]{:S(2)}, u32[]{:S(2)}) async-start(bf16[4,128,1024]{2,1,0:T(8,128)(2,1)} %bitcast.15), calls=%async_computation.2 | async-start | bytes 2097152 | tf_op jit(solution)/shard_map/all_to_all | solution.py:26
  101.3 1.2 copy.9
  102.5 8.8 %all-to-all-done.2 = bf16[4,128,1024]{2,1,0:T(8,128)(2,1)} async-done(((bf16[4,128,1024]{2,1,0:T(8,128)(2,1)}), bf16[4,128,1024]{2,1,0:T(8,128)(2,1)}, u32[]{:S(2)}, u32[]{:S(2)}) %all-to-all-start.2) | async-done | bytes 1048608 | tf_op jit(solution)/shard_map/all_to_all | solution.py:26
  111.3 1.5 convert_reduce_fusion
  112.8 0.0 copy-start.3
  112.8 0.1 fusion.6
  112.9 0.1 broadcast_in_dim.4
  113.1 12.2 %all_to_all.50 = bf16[4,128,1024]{2,1,0:T(8,128)(2,1)S(1)} all-to-all(bf16[4,128,1024]{2,1,0:T(8,128)(2,1)S(1)} %broadcast_in_dim.4), channel_id=1, replica_groups=mesh['tok'=8,'yh'=4,'core'=2,'x'=4,'yl'=2] {'x'}, dimensions={0} | all-to-all | bytes 2097152 | tf_op jit(solution)/shard_map/all_to_all | solution.py:26
  125.2 0.0 copy-done.3
  125.2 0.7 convolution_convert_fusion
  125.9 38.1 %all_to_all.51 = bf16[16,32,1024]{2,1,0:T(8,128)(2,1)} all-to-all(bf16[16,32,1024]{2,1,0:T(8,128)(2,1)S(1)} %bitcast.64), channel_id=1, replica_groups=mesh['tok'=8,'yh'=4,'core'=2,'x'=4,'yl'=2] {'tok','yl'}, dimensions={0} | all-to-all | bytes 2097152 | tf_op jit(solution)/shard_map/all_to_all | solution.py:26
  164.0 1.4 reduce_sum.47
  165.4 0.1 broadcast_in_dim.5
  165.5 11.5 %all_to_all.52 = bf16[8,32,1024]{2,1,0:T(8,128)(2,1)S(1)} all-to-all(bf16[8,32,1024]{2,1,0:T(8,128)(2,1)S(1)} %broadcast_in_dim.5), channel_id=1, replica_groups=mesh['tok'=8,'yh'=4,'core'=2,'x'=4,'yl'=2] {'x','yl'}, dimensions={0} | all-to-all | bytes 1048576 | tf_op jit(solution)/shard_map/all_to_all | solution.py:26
  176.9 0.7 fusion
  177.8 5.5 %all-gather.1 = bf16[8,32,1024]{2,1,0:T(8,128)(2,1)S(1)} all-gather(bf16[4,32,1024]{2,1,0:T(8,128)(2,1)S(1)} %fusion.8), channel_id=3, replica_groups=mesh['tok'=8,'yh'=4,'core'=2,'x'=4,'yl'=2] {'core'}, dimensions={0}, use_global_device_ids=true | all-gather | bytes 786432 | tf_op jit(solution)/shard_map/all_gather | solution.py:75
  183.3 0.8 fusion.4
  184.0 3.4 %all-to-all-start.6 = ((bf16[4,32,1024]{2,1,0:T(8,128)(2,1)}), bf16[4,32,1024]{2,1,0:T(8,128)(2,1)S(1)}, u32[]{:S(2)}, u32[]{:S(2)}) async-start(bf16[4,32,1024]{2,1,0:T(8,128)(2,1)} %fusion.4), calls=%async_computation.6 | async-start | bytes 524288 | tf_op jit(solution)/shard_map/all_to_all | solution.py:26
  187.5 1.0 copy.11
  188.5 7.9 %all-to-all-done.6 = bf16[4,32,1024]{2,1,0:T(8,128)(2,1)S(1)} async-done(((bf16[4,32,1024]{2,1,0:T(8,128)(2,1)}), bf16[4,32,1024]{2,1,0:T(8,128)(2,1)S(1)}, u32[]{:S(2)}, u32[]{:S(2)}) %all-to-all-start.6) | async-done | bytes 262176 | tf_op jit(solution)/shard_map/all_to_all | solution.py:26
  196.5 18.1 %all_gather.31 = bf16[256,1024]{1,0:T(8,128)(2,1)S(1)} all-gather(bf16[32,1024]{1,0:T(8,128)(2,1)S(1)} %reduce_sum.48), channel_id=1, replica_groups=mesh['tok'=8,'yh'=4,'core'=2,'x'=4,'yl'=2] {'yh','core'}, dimensions={0}, use_global_device_ids=true | all-gather | bytes 589824 | tf_op jit(solution)/shard_map/all_gather | solution.py:119
  214.6 0.8 copy.15
  (7 shorter events, 0.3 us)
Async XLA Ops:
  7.2 16.6 %copy-start = (bf16[1024,1024]{1,0:T(8,128)(2,1)S(1)}, bf16[1024,1024]{1,0:T(8,128)(2,1)}, u32[]{:S(2)}) copy-start(bf16[1024,1024]{1,0:T(8,128)(2,1)} %param.8) | copy-start | bytes 6291460
  7.2 45.7 %all-gather.5.cloned.1.call-start = ((), (), s32[]{:S(2)}) async-start(), calls=%async_computation.7 | async-start | bytes 1310720 | tf_op jit(solution)/shard_map/all_gather | solution.py:95
  12.8 40.0 %all-to-all-start = ((bf16[8,64,1024]{2,1,0:T(8,128)(2,1)}), bf16[8,64,1024]{2,1,0:T(8,128)(2,1)S(1)}, u32[]{:S(2)}, u32[]{:S(2)}) async-start(bf16[8,64,1024]{2,1,0:T(8,128)(2,1)} %shard_map.68), calls=%async_computation | async-start | bytes 2097152 | tf_op jit(solution)/shard_map/all_to_all | solution.py:26
  23.7 70.2 %all-gather.7.cloned.1.call-start = ((), (), s32[]{:S(2)}) async-start(), calls=%async_computation.8 | async-start | bytes 1179648 | tf_op jit(solution)/shard_map/all_gather | solution.py:102
  25.5 0.8 copy-start.1
  27.1 11.2 %collective-permute-start = (bf16[64,1024]{1,0:T(8,128)(2,1)}, bf16[64,1024]{1,0:T(8,128)(2,1)S(1)}, u32[]{:S(2)}, u32[]{:S(2)}) collective-permute-start(bf16[64,1024]{1,0:T(8,128)(2,1)} %get-tuple-element.16), channel_id=1, source_target_pairs={{0,4},{2,6},{4,0},{6,2},{1,5},{3,7},{5,1},{7,3},{8,12},{10,14},{12... | collective-permute-start | bytes 393224 | tf_op jit(solution)/shard_map/ppermute | solution.py:68
  31.8 11.4 %collective-permute-start.1 = (bf16[64,1024]{1,0:T(8,128)(2,1)}, bf16[64,1024]{1,0:T(8,128)(2,1)S(1)}, u32[]{:S(2)}, u32[]{:S(2)}) collective-permute-start(bf16[64,1024]{1,0:T(8,128)(2,1)} %get-tuple-element.18), channel_id=1, source_target_pairs={{0,2},{2,4},{4,6},{6,0},{1,3},{3,5},{5,7},{7,1},{8,10},{10,12},{12... | collective-permute-start | bytes 393224 | tf_op jit(solution)/shard_map/ppermute | solution.py:68
  34.0 10.2 %collective-permute-start.2 = (bf16[64,1024]{1,0:T(8,128)(2,1)}, bf16[64,1024]{1,0:T(8,128)(2,1)S(1)}, u32[]{:S(2)}, u32[]{:S(2)}) collective-permute-start(bf16[64,1024]{1,0:T(8,128)(2,1)} %get-tuple-element.17), channel_id=1, source_target_pairs={{0,6},{2,0},{4,2},{6,4},{1,7},{3,1},{5,3},{7,5},{8,14},{10,8},{12,... | collective-permute-start | bytes 393224 | tf_op jit(solution)/shard_map/ppermute | solution.py:68
  45.1 6.0 %collective-permute-start.3 = (bf16[64,1024]{1,0:T(8,128)(2,1)S(1)}, bf16[64,1024]{1,0:T(8,128)(2,1)S(1)}, u32[]{:S(2)}, u32[]{:S(2)}) collective-permute-start(bf16[64,1024]{1,0:T(8,128)(2,1)S(1)} %fusion.11), channel_id=1, source_target_pairs={{0,1},{1,0},{2,3},{3,2},{4,5},{5,4},{6,7},{7,6},{8,9},{9,8},{10,11... | collective-permute-start | bytes 393224 | tf_op jit(solution)/shard_map/ppermute | solution.py:68
  93.9 3.1 %copy-start.2 = (bf16[512,512]{1,0:T(8,128)(2,1)}, bf16[512,512]{1,0:T(8,128)(2,1)S(1)}, u32[]{:S(2)}) copy-start(bf16[512,512]{1,0:T(8,128)(2,1)S(1)} %all_gather.27) | copy-start | bytes 1572868
  97.0 14.3 %all-to-all-start.2 = ((bf16[4,128,1024]{2,1,0:T(8,128)(2,1)}), bf16[4,128,1024]{2,1,0:T(8,128)(2,1)}, u32[]{:S(2)}, u32[]{:S(2)}) async-start(bf16[4,128,1024]{2,1,0:T(8,128)(2,1)} %bitcast.15), calls=%async_computation.2 | async-start | bytes 2097152 | tf_op jit(solution)/shard_map/all_to_all | solution.py:26
  112.8 12.4 %copy-start.3 = (bf16[512,512]{1,0:T(8,128)(2,1)S(1)}, bf16[512,512]{1,0:T(8,128)(2,1)}, u32[]{:S(2)}) copy-start(bf16[512,512]{1,0:T(8,128)(2,1)} %copy-done.2) | copy-start | bytes 1572868
  184.0 12.4 %all-to-all-start.6 = ((bf16[4,32,1024]{2,1,0:T(8,128)(2,1)}), bf16[4,32,1024]{2,1,0:T(8,128)(2,1)S(1)}, u32[]{:S(2)}, u32[]{:S(2)}) async-start(bf16[4,32,1024]{2,1,0:T(8,128)(2,1)} %fusion.4), calls=%async_computation.6 | async-start | bytes 524288 | tf_op jit(solution)/shard_map/all_to_all | solution.py:26
Sparse Core Ops, SparseCore 0:
  10.7 37.3 all-gather.4
  53.0 40.0 all-gather.6

commit v6 on v4

--- a/solution.py
+++ b/solution.py
@@ -1,6 +1,7 @@
 import jax
 import jax.numpy as jnp
 from jax import lax
+from jax.experimental.layout import Layout, with_layout_constraint
 from jax.sharding import Mesh, PartitionSpec as P
 
 damping = 0.1
@@ -79,9 +80,10 @@
     grad_sq = lax.all_gather(grad_sq, "tok", axis=0, tiled=True)
     act_half = lax.all_gather(act_proj.astype(narrow), row, axis=0, tiled=True)
     act_wide = act_half.astype(wide)
-    act_sq = (act_wide * act_wide).astype(narrow)
+    act_sq_t = with_layout_constraint((act_wide * act_wide).astype(narrow).T, Layout((0, 1)))
+    act_sq_t = lax.optimization_barrier(act_sq_t)
 
-    summed_t = scatter_sum(contract(act_sq, grad_sq, 0, 0), "x")
+    summed_t = scatter_sum(contract(act_sq_t, grad_sq, 1, 0), "x")
     summed_t = lax.optimization_barrier(summed_t)
     spread_t = token_count * (summed_t / token_count + damping)
     scaled_t = (eigen_noise.T * lax.rsqrt(spread_t)).astype(narrow)

time: 215 us -> 222 us (1.033)
  waiting for transfers between devices: 26.1 us -> 31.5 us
    all_gather x1, waiting for transfers between devices: 0.32 us -> 5.85 us  [plan(): basis = lax.all_gather(act_basis, 'x', axis=1, tiled=True)]
  transfers between devices with their start and end apart: 9 -> 9, of which waited for: 6 -> 7; matrix products, arithmetic and copies ran while one was open for 5% -> 6% of each run, Pallas kernels for 0% -> 0%
where the time goes in v6:
time: 222 us; the launch traced here: 221 us
  blocking collectives  118 us (53%)
  starting transfers between devices  31.9 us (14%)
  waiting for transfers between devices  31.5 us (14%)
  between operations  14.3 us (6%)
  matrix products  9 us (4%)
  other arithmetic  8.49 us (4%)
  local copies, waits for them, and re-layouts  7.34 us (3%)
    all_to_all x4, blocking collectives, exchange(): return lax.all_to_all(blocks, axes, 0, 0, tiled=True)  73.3 us
    all_to_all x3, starting transfers between devices, exchange(): return lax.all_to_all(blocks, axes, 0, 0, tiled=True)  18.7 us
    all_gather x1, blocking collectives, plan(): act_half = lax.all_gather(act_proj.astype(narrow), row, axis=0, tiled=True)  17.7 us
    all_gather x1, blocking collectives, plan(): output_shift = lax.all_gather(shift, row, axis=0, tiled=True)  17.7 us
    all_to_all x3, waiting for transfers between devices, exchange(): return lax.all_to_all(blocks, axes, 0, 0, tiled=True)  16.4 us
    ppermute x4, starting transfers between devices, shifted(): lax.ppermute(block, axis, [(i, (i + step) % members) for i in range(membe...  13.1 us
    all_gather x2, blocking collectives, pair_sum(): return kept + pick(lax.all_gather(sent, axis), 1 - mine, 0).astype(wide)  9.63 us
    dot_general x5, matrix products, contract(): lax.dot_general(former, latter, (((former_dim,), (latter_dim,)), ((), ())...  9 us
  transfers between devices with their start and end apart: 9, of which 7 were waited for; matrix products, arithmetic and copies ran while one was open for 6% of the time, Pallas kernels for 0%

profile of v6, /device:TPU:1, one launch (start us, length us, event | category | flops | bytes accessed | tf_op | source)
XLA Modules:
  0.0 220.8 jit_solution(16991391720311994601)
XLA Ops:
  7.2 0.0 copy-start
  7.2 1.1 constant_dynamic-slice_fusion
  8.3 1.2 broadcast_in_dim.6
  9.4 10.9 %all-to-all-start = ((bf16[8,64,1024]{2,1,0:T(8,128)(2,1)}), bf16[8,64,1024]{2,1,0:T(8,128)(2,1)S(1)}, u32[]{:S(2)}, u32[]{:S(2)}) async-start(bf16[8,64,1024]{2,1,0:T(8,128)(2,1)} %broadcast_in_dim.6), calls=%async_computation | async-start | bytes 2097152 | tf_op jit(solution)/shard_map/all_to_all | solution.py:24
  20.3 0.0 all-gather.5.cloned.1.call-start
  20.3 0.7 all-gather.5.cloned.1.call-update
  21.0 0.0 all-gather.7.cloned.1.call-start
  21.1 0.0 copy-done
  21.1 2.5 %convolution_convert_fusion.2 = bf16[256,1024]{1,0:T(8,128)(2,1)} fusion(bf16[256,1024]{1,0:T(8,128)(2,1)} %param.6, bf16[1024,1024]{1,0:T(8,128)(2,1)S(1)} %copy-done), kind=kOutput, calls=%fused_computation.5 | convolution fusion | flops 537133056 | bytes 3145728 | tf_op jit(solution)/shard_map/dot_general | solution.py:15
  23.6 1.8 dynamic-slice_bitcast_fusion.4
  25.4 4.4 %collective-permute-start.2 = (bf16[64,1024]{1,0:T(8,128)(2,1)}, bf16[64,1024]{1,0:T(8,128)(2,1)S(1)}, u32[]{:S(2)}, u32[]{:S(2)}) collective-permute-start(bf16[64,1024]{1,0:T(8,128)(2,1)} %get-tuple-element.17), channel_id=1, source_target_pairs={{0,6},{2,0},{4,2},{6,4},{1,7},{3,1},{5,3},{7,5},{8,14},{10,8},{12,... | collective-permute-start | bytes 393224 | tf_op jit(solution)/shard_map/ppermute | solution.py:46
  29.8 1.9 collective-permute-start.1
  31.7 3.6 %collective-permute-start = (bf16[64,1024]{1,0:T(8,128)(2,1)}, bf16[64,1024]{1,0:T(8,128)(2,1)S(1)}, u32[]{:S(2)}, u32[]{:S(2)}) collective-permute-start(bf16[64,1024]{1,0:T(8,128)(2,1)} %get-tuple-element.16), channel_id=1, source_target_pairs={{0,4},{2,6},{4,0},{6,2},{1,5},{3,7},{5,1},{7,3},{8,12},{10,14},{12... | collective-permute-start | bytes 393224 | tf_op jit(solution)/shard_map/ppermute | solution.py:46
  35.4 0.0 collective-permute-done.2
  35.4 1.9 collective-permute-done.1
  37.2 2.3 %collective-permute-done = bf16[64,1024]{1,0:T(8,128)(2,1)S(1)} collective-permute-done((bf16[64,1024]{1,0:T(8,128)(2,1)}, bf16[64,1024]{1,0:T(8,128)(2,1)S(1)}, u32[]{:S(2)}, u32[]{:S(2)}) %collective-permute-start) | collective-permute-done | bytes 131104 | tf_op jit(solution)/shard_map/ppermute | solution.py:46
  39.5 1.0 fusion.12
  40.5 3.2 %collective-permute-start.3 = (bf16[64,1024]{1,0:T(8,128)(2,1)S(1)}, bf16[64,1024]{1,0:T(8,128)(2,1)S(1)}, u32[]{:S(2)}, u32[]{:S(2)}) collective-permute-start(bf16[64,1024]{1,0:T(8,128)(2,1)S(1)} %fusion.12), channel_id=1, source_target_pairs={{0,1},{1,0},{2,3},{3,2},{4,5},{5,4},{6,7},{7,6},{8,9},{9,8},{10,11... | collective-permute-start | bytes 393224 | tf_op jit(solution)/shard_map/ppermute | solution.py:46
  43.7 2.9 %collective-permute-done.3 = bf16[64,1024]{1,0:T(8,128)(2,1)S(1)} collective-permute-done((bf16[64,1024]{1,0:T(8,128)(2,1)S(1)}, bf16[64,1024]{1,0:T(8,128)(2,1)S(1)}, u32[]{:S(2)}, u32[]{:S(2)}) %collective-permute-start.3) | collective-permute-done | bytes 131104 | tf_op jit(solution)/shard_map/ppermute | solution.py:46
  46.6 1.7 multiply_convert_fusion.1
  48.2 0.0 all-gather.7.cloned.1.call-update
  48.3 5.8 %all-gather.5.cloned.1.call-done = bf16[1024,512]{1,0:T(8,128)(2,1)} async-done(((bf16[1024,128]{1,0:T(8,128)(2,1)}), bf16[1024,512]{1,0:T(8,128)(2,1)}) %all-gather.5.cloned.1.call-update) | async-done | bytes 1048592 | tf_op jit(solution)/shard_map/all_gather | solution.py:73
  54.1 0.0 all-to-all-done
  54.1 1.9 fusion.2
  56.2 4.4 %all-gather = bf16[8,64,512]{2,1,0:T(8,128)(2,1)S(1)} all-gather(bf16[4,64,512]{2,1,0:T(8,128)(2,1)S(1)} %fusion.8), channel_id=2, replica_groups=mesh['tok'=8,'yh'=4,'core'=2,'x'=4,'yl'=2] {'core'}, dimensions={0}, use_global_device_ids=true | all-gather | bytes 786432 | tf_op jit(solution)/shard_map/all_gather | solution.py:53
  60.6 0.1 fusion.6
  60.6 15.7 %all_to_all.49 = bf16[4,64,512]{2,1,0:T(8,128)(2,1)S(1)} all-to-all(bf16[4,64,512]{2,1,0:T(8,128)(2,1)S(1)} %fusion.6), channel_id=1, replica_groups=mesh['tok'=8,'yh'=4,'core'=2,'x'=4,'yl'=2] {'yh'}, dimensions={0} | all-to-all | bytes 524288 | tf_op jit(solution)/shard_map/all_to_all | solution.py:24
  76.4 17.7 %all_gather.27 = bf16[512,512]{1,0:T(8,128)(2,1)S(1)} all-gather(bf16[64,512]{1,0:T(8,128)(2,1)S(1)} %reduce_sum.45), channel_id=1, replica_groups=mesh['tok'=8,'yh'=4,'core'=2,'x'=4,'yl'=2] {'yh','core'}, dimensions={0}, use_global_device_ids=true | all-gather | bytes 589824 | tf_op jit(solution)/shard_map/all_gather | solution.py:81
  94.1 0.2 copy.9
  94.3 0.9 fusion.4
  95.2 0.0 copy-start.1
  95.2 1.5 all-gather.7.cloned.1.call-done
  96.7 3.1 %convolution_convert_fusion.1 = bf16[512,1024]{1,0:T(8,128)(2,1)} fusion(bf16[512,512]{1,0:T(8,128)(2,1)} %fusion.4, bf16[512,1024]{1,0:T(8,128)(2,1)} %all-gather.7.cloned.1.call-done), kind=kOutput, calls=%fused_computation.4 | convolution fusion | flops 537395200 | bytes 2621440 | tf_op jit(solution)/shard_map/dot_general | solution.py:15
  99.7 4.2 %all-to-all-start.2 = ((bf16[4,128,1024]{2,1,0:T(8,128)(2,1)}), bf16[4,128,1024]{2,1,0:T(8,128)(2,1)}, u32[]{:S(2)}, u32[]{:S(2)}) async-start(bf16[4,128,1024]{2,1,0:T(8,128)(2,1)} %bitcast.64), calls=%async_computation.2 | async-start | bytes 2097152 | tf_op jit(solution)/shard_map/all_to_all | solution.py:24
  104.0 0.0 copy-done.1
  104.0 1.0 copy.8
  105.0 8.8 %all-to-all-done.2 = bf16[4,128,1024]{2,1,0:T(8,128)(2,1)} async-done(((bf16[4,128,1024]{2,1,0:T(8,128)(2,1)}), bf16[4,128,1024]{2,1,0:T(8,128)(2,1)}, u32[]{:S(2)}, u32[]{:S(2)}) %all-to-all-start.2) | async-done | bytes 1048608 | tf_op jit(solution)/shard_map/all_to_all | solution.py:24
  113.8 1.5 convert_reduce_fusion
  115.3 1.1 fusion.7
  116.4 0.1 broadcast_in_dim.7
  116.5 12.2 %all_to_all.50 = bf16[4,128,1024]{2,1,0:T(8,128)(2,1)S(1)} all-to-all(bf16[4,128,1024]{2,1,0:T(8,128)(2,1)S(1)} %broadcast_in_dim.7), channel_id=1, replica_groups=mesh['tok'=8,'yh'=4,'core'=2,'x'=4,'yl'=2] {'x'}, dimensions={0} | all-to-all | bytes 2097152 | tf_op jit(solution)/shard_map/all_to_all | solution.py:24
  128.7 0.7 convolution_convert_fusion
  129.4 34.1 %all_to_all.51 = bf16[16,32,1024]{2,1,0:T(8,128)(2,1)} all-to-all(bf16[16,32,1024]{2,1,0:T(8,128)(2,1)S(1)} %bitcast.66), channel_id=1, replica_groups=mesh['tok'=8,'yh'=4,'core'=2,'x'=4,'yl'=2] {'tok','yl'}, dimensions={0} | all-to-all | bytes 2097152 | tf_op jit(solution)/shard_map/all_to_all | solution.py:24
  163.5 1.4 reduce_sum.47
  165.0 0.1 broadcast_in_dim.8
  165.0 11.3 %all_to_all.52 = bf16[8,32,1024]{2,1,0:T(8,128)(2,1)S(1)} all-to-all(bf16[8,32,1024]{2,1,0:T(8,128)(2,1)S(1)} %broadcast_in_dim.8), channel_id=1, replica_groups=mesh['tok'=8,'yh'=4,'core'=2,'x'=4,'yl'=2] {'x','yl'}, dimensions={0} | all-to-all | bytes 1048576 | tf_op jit(solution)/shard_map/all_to_all | solution.py:24
  176.3 0.7 fusion
  177.1 5.2 %all-gather.1 = bf16[8,32,1024]{2,1,0:T(8,128)(2,1)S(1)} all-gather(bf16[4,32,1024]{2,1,0:T(8,128)(2,1)S(1)} %fusion.9), channel_id=3, replica_groups=mesh['tok'=8,'yh'=4,'core'=2,'x'=4,'yl'=2] {'core'}, dimensions={0}, use_global_device_ids=true | all-gather | bytes 786432 | tf_op jit(solution)/shard_map/all_gather | solution.py:53
  182.4 0.8 fusion.5
  183.1 3.6 %all-to-all-start.6 = ((bf16[4,32,1024]{2,1,0:T(8,128)(2,1)}), bf16[4,32,1024]{2,1,0:T(8,128)(2,1)S(1)}, u32[]{:S(2)}, u32[]{:S(2)}) async-start(bf16[4,32,1024]{2,1,0:T(8,128)(2,1)} %fusion.5), calls=%async_computation.6 | async-start | bytes 524288 | tf_op jit(solution)/shard_map/all_to_all | solution.py:24
  186.8 1.0 copy.10
  187.8 7.6 %all-to-all-done.6 = bf16[4,32,1024]{2,1,0:T(8,128)(2,1)S(1)} async-done(((bf16[4,32,1024]{2,1,0:T(8,128)(2,1)}), bf16[4,32,1024]{2,1,0:T(8,128)(2,1)S(1)}, u32[]{:S(2)}, u32[]{:S(2)}) %all-to-all-start.6) | async-done | bytes 262176 | tf_op jit(solution)/shard_map/all_to_all | solution.py:24
  195.5 17.7 %all_gather.31 = bf16[256,1024]{1,0:T(8,128)(2,1)S(1)} all-gather(bf16[32,1024]{1,0:T(8,128)(2,1)S(1)} %reduce_sum.48), channel_id=1, replica_groups=mesh['tok'=8,'yh'=4,'core'=2,'x'=4,'yl'=2] {'yh','core'}, dimensions={0}, use_global_device_ids=true | all-gather | bytes 589824 | tf_op jit(solution)/shard_map/all_gather | solution.py:98
  213.1 0.8 copy.14
  (7 shorter events, 0.3 us)
Async XLA Ops:
  7.2 13.9 %copy-start = (bf16[1024,1024]{1,0:T(8,128)(2,1)S(1)}, bf16[1024,1024]{1,0:T(8,128)(2,1)}, u32[]{:S(2)}) copy-start(bf16[1024,1024]{1,0:T(8,128)(2,1)} %param.8) | copy-start | bytes 6291460
  9.4 44.7 %all-to-all-start = ((bf16[8,64,1024]{2,1,0:T(8,128)(2,1)}), bf16[8,64,1024]{2,1,0:T(8,128)(2,1)S(1)}, u32[]{:S(2)}, u32[]{:S(2)}) async-start(bf16[8,64,1024]{2,1,0:T(8,128)(2,1)} %broadcast_in_dim.6), calls=%async_computation | async-start | bytes 2097152 | tf_op jit(solution)/shard_map/all_to_all | solution.py:24
  20.3 33.9 %all-gather.5.cloned.1.call-start = ((), (), s32[]{:S(2)}) async-start(), calls=%async_computation.7 | async-start | bytes 1310720 | tf_op jit(solution)/shard_map/all_gather | solution.py:73
  21.0 75.7 %all-gather.7.cloned.1.call-start = ((), (), s32[]{:S(2)}) async-start(), calls=%async_computation.8 | async-start | bytes 1179648 | tf_op jit(solution)/shard_map/all_gather | solution.py:80
  25.4 9.9 %collective-permute-start.2 = (bf16[64,1024]{1,0:T(8,128)(2,1)}, bf16[64,1024]{1,0:T(8,128)(2,1)S(1)}, u32[]{:S(2)}, u32[]{:S(2)}) collective-permute-start(bf16[64,1024]{1,0:T(8,128)(2,1)} %get-tuple-element.17), channel_id=1, source_target_pairs={{0,6},{2,0},{4,2},{6,4},{1,7},{3,1},{5,3},{7,5},{8,14},{10,8},{12,... | collective-permute-start | bytes 393224 | tf_op jit(solution)/shard_map/ppermute | solution.py:46
  29.8 7.4 %collective-permute-start.1 = (bf16[64,1024]{1,0:T(8,128)(2,1)}, bf16[64,1024]{1,0:T(8,128)(2,1)S(1)}, u32[]{:S(2)}, u32[]{:S(2)}) collective-permute-start(bf16[64,1024]{1,0:T(8,128)(2,1)} %get-tuple-element.18), channel_id=1, source_target_pairs={{0,2},{2,4},{4,6},{6,0},{1,3},{3,5},{5,7},{7,1},{8,10},{10,12},{12... | collective-permute-start | bytes 393224 | tf_op jit(solution)/shard_map/ppermute | solution.py:46
  31.7 7.8 %collective-permute-start = (bf16[64,1024]{1,0:T(8,128)(2,1)}, bf16[64,1024]{1,0:T(8,128)(2,1)S(1)}, u32[]{:S(2)}, u32[]{:S(2)}) collective-permute-start(bf16[64,1024]{1,0:T(8,128)(2,1)} %get-tuple-element.16), channel_id=1, source_target_pairs={{0,4},{2,6},{4,0},{6,2},{1,5},{3,7},{5,1},{7,3},{8,12},{10,14},{12... | collective-permute-start | bytes 393224 | tf_op jit(solution)/shard_map/ppermute | solution.py:46
  40.5 6.1 %collective-permute-start.3 = (bf16[64,1024]{1,0:T(8,128)(2,1)S(1)}, bf16[64,1024]{1,0:T(8,128)(2,1)S(1)}, u32[]{:S(2)}, u32[]{:S(2)}) collective-permute-start(bf16[64,1024]{1,0:T(8,128)(2,1)S(1)} %fusion.12), channel_id=1, source_target_pairs={{0,1},{1,0},{2,3},{3,2},{4,5},{5,4},{6,7},{7,6},{8,9},{9,8},{10,11... | collective-permute-start | bytes 393224 | tf_op jit(solution)/shard_map/ppermute | solution.py:46
  95.2 8.8 %copy-start.1 = (f32[1024,128]{1,0:T(8,128)S(1)}, f32[1024,128]{1,0:T(8,128)}, u32[]{:S(2)}) copy-start(f32[1024,128]{1,0:T(8,128)} %param.9) | copy-start | bytes 1572868
  99.7 14.1 %all-to-all-start.2 = ((bf16[4,128,1024]{2,1,0:T(8,128)(2,1)}), bf16[4,128,1024]{2,1,0:T(8,128)(2,1)}, u32[]{:S(2)}, u32[]{:S(2)}) async-start(bf16[4,128,1024]{2,1,0:T(8,128)(2,1)} %bitcast.64), calls=%async_computation.2 | async-start | bytes 2097152 | tf_op jit(solution)/shard_map/all_to_all | solution.py:24
  183.1 12.3 %all-to-all-start.6 = ((bf16[4,32,1024]{2,1,0:T(8,128)(2,1)}), bf16[4,32,1024]{2,1,0:T(8,128)(2,1)S(1)}, u32[]{:S(2)}, u32[]{:S(2)}) async-start(bf16[4,32,1024]{2,1,0:T(8,128)(2,1)} %fusion.5), calls=%async_computation.6 | async-start | bytes 524288 | tf_op jit(solution)/shard_map/all_to_all | solution.py:24
Sparse Core Ops, SparseCore 0:
  23.2 30.9 all-gather.4
  56.8 39.8 all-gather.6

commit v7 on v4

--- a/solution.py
+++ b/solution.py
@@ -52,6 +52,16 @@
     return kept + pick(lax.all_gather(sent, axis), 1 - mine, 0).astype(wide)
 
 
+def columns_of_pair(act_half):
+    half = act_half.reshape(8, 2, act_half.shape[0] // 16, act_half.shape[1])
+    mine = lax.axis_index("yl")
+    theirs = shifted(pick(half, 1 - mine, 1), "yl", 1)
+    kept = pick(half, mine, 1)
+    pair = (lax.select_n(mine, kept, theirs), lax.select_n(mine, theirs, kept))
+    blocks = [side.reshape(-1, 4, 1, side.shape[-1] // 4) for side in pair]
+    return lax.optimization_barrier(jnp.concatenate(blocks, axis=2).reshape(-1, 2 * act_half.shape[1]))
+
+
 def ring_sum(blocks, axis):
     mine = lax.axis_index(axis)
     members = lax.axis_size(axis)
@@ -81,15 +91,17 @@
     act_wide = act_half.astype(wide)
     act_sq = (act_wide * act_wide).astype(narrow)
 
+    act_cols = columns_of_pair(act_half)
+
     summed_t = scatter_sum(contract(act_sq, grad_sq, 0, 0), "x")
     summed_t = lax.optimization_barrier(summed_t)
     spread_t = token_count * (summed_t / token_count + damping)
     scaled_t = (eigen_noise.T * lax.rsqrt(spread_t)).astype(narrow)
     scaled_t, summed_t = lax.optimization_barrier((scaled_t, summed_t))
     scales = (summed_t / token_count).T
-    widened_t = spread(scaled_t, "x")
+    widened_t = spread(scaled_t, col)
 
-    hidden = scatter_sum(contract(act_half, widened_t, 1, 0), ("tok", "yl")).astype(narrow)
+    hidden = scatter_sum(contract(act_cols, widened_t, 1, 0), "tok").astype(narrow)
     hidden = spread(hidden, col)
     halves = pair_sum(contract(hidden, grad_basis, 1, 1), "core")
     shift = scatter_sum(halves, "yh")[0].astype(narrow)

time: 215 us -> 241 us (1.12)
  waiting for transfers between devices: 26.1 us -> 50.8 us
  blocking collectives: 119 us -> 105 us
  starting transfers between devices: 33 us -> 39.3 us
  local copies, waits for them, and re-layouts: 6.98 us -> 11.8 us
  other arithmetic: 6.57 us -> 9.37 us
    ppermute x4 -> x5, waiting for transfers between devices: 7.18 us -> 29.9 us  [shifted(): lax.ppermute(block, axis, [(i, (i + step) % members) for i in range(membe...]
    all_to_all x4 -> x3, blocking collectives: 74.8 us -> 56.4 us  [exchange(): return lax.all_to_all(blocks, axes, 0, 0, tiled=True)]
    all_to_all x3 -> x4, starting transfers between devices: 18.7 us -> 22.9 us  [exchange(): return lax.all_to_all(blocks, axes, 0, 0, tiled=True)]
    all_gather x2, blocking collectives: 8.04 us -> 12 us  [pair_sum(): return kept + pick(lax.all_gather(sent, axis), 1 - mine, 0).astype(wide)]
    reshape x0 -> x2, local copies, waits for them, and re-layouts: none -> 2.48 us  [columns_of_pair(): blocks = [side.reshape(-1, 4, 1, side.shape[-1] // 4) for side in pair]]
    all_to_all x3 -> x4, waiting for transfers between devices: 17.9 us -> 20.1 us  [exchange(): return lax.all_to_all(blocks, axes, 0, 0, tiled=True)]
    ppermute x4 -> x5, starting transfers between devices: 14.2 us -> 16.4 us  [shifted(): lax.ppermute(block, axis, [(i, (i + step) % members) for i in range(membe...]
  transfers between devices with their start and end apart: 9 -> 11, of which waited for: 6 -> 7; matrix products, arithmetic and copies ran while one was open for 5% -> 8% of each run, Pallas kernels for 0% -> 0%
where the time goes in v7:
time: 241 us; the launch traced here: 240 us
  blocking collectives  105 us (44%)
  waiting for transfers between devices  50.8 us (21%)
  starting transfers between devices  39.3 us (16%)
  between operations  14.3 us (6%)
  local copies, waits for them, and re-layouts  11.8 us (5%)
  matrix products  9.9 us (4%)
  other arithmetic  9.37 us (4%)
    all_to_all x3, blocking collectives, exchange(): return lax.all_to_all(blocks, axes, 0, 0, tiled=True)  56.4 us
    ppermute x5, waiting for transfers between devices, shifted(): lax.ppermute(block, axis, [(i, (i + step) % members) for i in range(membe...  29.9 us
    all_to_all x4, starting transfers between devices, exchange(): return lax.all_to_all(blocks, axes, 0, 0, tiled=True)  22.9 us
    all_to_all x4, waiting for transfers between devices, exchange(): return lax.all_to_all(blocks, axes, 0, 0, tiled=True)  20.1 us
    all_gather x1, blocking collectives, plan(): act_half = lax.all_gather(act_proj.astype(narrow), row, axis=0, tiled=True)  18.1 us
    all_gather x1, blocking collectives, plan(): output_shift = lax.all_gather(shift, row, axis=0, tiled=True)  18.1 us
    ppermute x5, starting transfers between devices, shifted(): lax.ppermute(block, axis, [(i, (i + step) % members) for i in range(membe...  16.4 us
    all_gather x2, blocking collectives, pair_sum(): return kept + pick(lax.all_gather(sent, axis), 1 - mine, 0).astype(wide)  12 us
  transfers between devices with their start and end apart: 11, of which 7 were waited for; matrix products, arithmetic and copies ran while one was open for 8% of the time, Pallas kernels for 0%

profile of v7, /device:TPU:1, one launch (start us, length us, event | category | flops | bytes accessed | tf_op | source)
XLA Modules:
  0.0 240.2 jit_solution(16371229040725191603)
XLA Ops:
  7.2 0.0 copy-start
  7.2 0.0 all-gather.5.cloned.1.call-start
  7.2 0.7 all-gather.5.cloned.1.call-update
  7.9 0.9 constant_dynamic-slice_fusion
  8.8 1.1 broadcast_in_dim.6
  10.0 10.9 %all-to-all-start = ((bf16[8,64,1024]{2,1,0:T(8,128)(2,1)}), bf16[8,64,1024]{2,1,0:T(8,128)(2,1)S(1)}, u32[]{:S(2)}, u32[]{:S(2)}) async-start(bf16[8,64,1024]{2,1,0:T(8,128)(2,1)} %broadcast_in_dim.6), calls=%async_computation | async-start | bytes 2097152 | tf_op jit(solution)/shard_map/all_to_all | solution.py:23
  20.8 0.0 all-gather.7.cloned.1.call-start
  20.9 0.0 copy-done
  20.9 1.8 convolution_convert_fusion.2
  22.7 0.0 copy-start.1
  22.7 0.8 copy-done.1
  23.5 0.7 dynamic-slice_bitcast_fusion.5
  24.2 4.6 %collective-permute-start = (bf16[64,1024]{1,0:T(8,128)(2,1)}, bf16[64,1024]{1,0:T(8,128)(2,1)S(1)}, u32[]{:S(2)}, u32[]{:S(2)}) collective-permute-start(bf16[64,1024]{1,0:T(8,128)(2,1)} %get-tuple-element.18), channel_id=1, source_target_pairs={{0,4},{2,6},{4,0},{6,2},{1,5},{3,7},{5,1},{7,3},{8,12},{10,14},{12... | collective-permute-start | bytes 393224 | tf_op jit(solution)/shard_map/ppermute | solution.py:45
  28.9 2.8 %collective-permute-start.2 = (bf16[64,1024]{1,0:T(8,128)(2,1)}, bf16[64,1024]{1,0:T(8,128)(2,1)S(1)}, u32[]{:S(2)}, u32[]{:S(2)}) collective-permute-start(bf16[64,1024]{1,0:T(8,128)(2,1)} %get-tuple-element.19), channel_id=1, source_target_pairs={{0,6},{2,0},{4,2},{6,4},{1,7},{3,1},{5,3},{7,5},{8,14},{10,8},{12,... | collective-permute-start | bytes 393224 | tf_op jit(solution)/shard_map/ppermute | solution.py:45
  31.6 2.5 %collective-permute-start.1 = (bf16[64,1024]{1,0:T(8,128)(2,1)}, bf16[64,1024]{1,0:T(8,128)(2,1)S(1)}, u32[]{:S(2)}, u32[]{:S(2)}) collective-permute-start(bf16[64,1024]{1,0:T(8,128)(2,1)} %get-tuple-element.20), channel_id=1, source_target_pairs={{0,2},{2,4},{4,6},{6,0},{1,3},{3,5},{5,7},{7,1},{8,10},{10,12},{12... | collective-permute-start | bytes 393224 | tf_op jit(solution)/shard_map/ppermute | solution.py:45
  34.2 0.0 collective-permute-done
  34.2 4.3 %collective-permute-done.2 = bf16[64,1024]{1,0:T(8,128)(2,1)S(1)} collective-permute-done((bf16[64,1024]{1,0:T(8,128)(2,1)}, bf16[64,1024]{1,0:T(8,128)(2,1)S(1)}, u32[]{:S(2)}, u32[]{:S(2)}) %collective-permute-start.2) | collective-permute-done | bytes 131104 | tf_op jit(solution)/shard_map/ppermute | solution.py:45
  38.5 0.6 collective-permute-done.1
  39.1 1.0 fusion.11
  40.1 3.2 %collective-permute-start.3 = (bf16[64,1024]{1,0:T(8,128)(2,1)S(1)}, bf16[64,1024]{1,0:T(8,128)(2,1)S(1)}, u32[]{:S(2)}, u32[]{:S(2)}) collective-permute-start(bf16[64,1024]{1,0:T(8,128)(2,1)S(1)} %fusion.11), channel_id=1, source_target_pairs={{0,1},{1,0},{2,3},{3,2},{4,5},{5,4},{6,7},{7,6},{8,9},{9,8},{10,11... | collective-permute-start | bytes 393224 | tf_op jit(solution)/shard_map/ppermute | solution.py:45
  43.3 2.8 %collective-permute-done.3 = bf16[64,1024]{1,0:T(8,128)(2,1)S(1)} collective-permute-done((bf16[64,1024]{1,0:T(8,128)(2,1)S(1)}, bf16[64,1024]{1,0:T(8,128)(2,1)S(1)}, u32[]{:S(2)}, u32[]{:S(2)}) %collective-permute-start.3) | collective-permute-done | bytes 131104 | tf_op jit(solution)/shard_map/ppermute | solution.py:45
  46.1 1.7 multiply_convert_fusion.2
  47.7 0.0 all-gather.7.cloned.1.call-update
  47.7 0.0 all-gather.5.cloned.1.call-done
  47.8 2.2 all-to-all-done
  50.0 1.9 fusion.2
  52.0 4.8 %all-gather = bf16[8,64,512]{2,1,0:T(8,128)(2,1)S(1)} all-gather(bf16[4,64,512]{2,1,0:T(8,128)(2,1)S(1)} %fusion.7), channel_id=2, replica_groups=mesh['tok'=8,'yh'=4,'core'=2,'x'=4,'yl'=2] {'core'}, dimensions={0}, use_global_device_ids=true | all-gather | bytes 786432 | tf_op jit(solution)/shard_map/all_gather | solution.py:52
  56.9 0.1 fusion.5
  57.0 15.8 %all_to_all.49 = bf16[4,64,512]{2,1,0:T(8,128)(2,1)S(1)} all-to-all(bf16[4,64,512]{2,1,0:T(8,128)(2,1)S(1)} %fusion.5), channel_id=1, replica_groups=mesh['tok'=8,'yh'=4,'core'=2,'x'=4,'yl'=2] {'yh'}, dimensions={0} | all-to-all | bytes 524288 | tf_op jit(solution)/shard_map/all_to_all | solution.py:23
  72.8 18.1 %all_gather.27 = bf16[512,512]{1,0:T(8,128)(2,1)S(1)} all-gather(bf16[64,512]{1,0:T(8,128)(2,1)S(1)} %reduce_sum.45), channel_id=1, replica_groups=mesh['tok'=8,'yh'=4,'core'=2,'x'=4,'yl'=2] {'yh','core'}, dimensions={0}, use_global_device_ids=true | all-gather | bytes 589824 | tf_op jit(solution)/shard_map/all_gather | solution.py:90
  91.0 0.0 copy-start.2
  91.0 0.0 all-gather.7.cloned.1.call-done
  91.0 3.0 %convolution_convert_fusion = bf16[512,1024]{1,0:T(8,128)(2,1)} fusion(bf16[512,1024]{1,0:T(8,128)(2,1)} %all-gather.7.cloned.1.call-done, bf16[512,512]{1,0:T(8,128)(2,1)S(1)} %all_gather.27), kind=kOutput, calls=%fused_computation.3 | convolution fusion | flops 538181632 | bytes 2621440 | tf_op jit(solution)/shard_map/dot_general | solution.py:14
  94.0 4.3 %all-to-all-start.2 = ((bf16[4,128,1024]{2,1,0:T(8,128)(2,1)}), bf16[4,128,1024]{2,1,0:T(8,128)(2,1)}, u32[]{:S(2)}, u32[]{:S(2)}) async-start(bf16[4,128,1024]{2,1,0:T(8,128)(2,1)} %bitcast.72), calls=%async_computation.2 | async-start | bytes 2097152 | tf_op jit(solution)/shard_map/all_to_all | solution.py:23
  98.2 0.0 copy-done.2
  98.2 1.0 copy.11
  99.2 10.0 %all-to-all-done.2 = bf16[4,128,1024]{2,1,0:T(8,128)(2,1)} async-done(((bf16[4,128,1024]{2,1,0:T(8,128)(2,1)}), bf16[4,128,1024]{2,1,0:T(8,128)(2,1)}, u32[]{:S(2)}, u32[]{:S(2)}) %all-to-all-start.2) | async-done | bytes 1048608 | tf_op jit(solution)/shard_map/all_to_all | solution.py:23
  109.2 1.5 convert_reduce_fusion
  110.7 1.1 fusion.6
  111.8 1.6 broadcast_in_dim.7
  113.4 4.4 %all-to-all-start.3 = ((bf16[8,128,1024]{2,1,0:T(8,128)(2,1)}), bf16[8,128,1024]{2,1,0:T(8,128)(2,1)}, u32[]{:S(2)}, u32[]{:S(2)}) async-start(bf16[8,128,1024]{2,1,0:T(8,128)(2,1)} %broadcast_in_dim.7), calls=%async_computation.3 | async-start | bytes 4194304 | tf_op jit(solution)/shard_map/all_to_all | solution.py:23
  117.8 3.2 %collective-permute-start.4 = (bf16[8,32,512]{2,1,0:T(8,128)(2,1)S(1)}, bf16[8,32,512]{2,1,0:T(8,128)(2,1)}, u32[]{:S(2)}, u32[]{:S(2)}) collective-permute-start(bf16[8,32,512]{2,1,0:T(8,128)(2,1)S(1)} %dynamic-slice_bitcast_fusion.2), channel_id=1, source_target_pairs={{0,1},{1,0},{2,3},{3,2},{4,5},{5,4},{6,7},{7,6},{8,9},{9,8},{10,11... | collective-permute-start | bytes 786440 | tf_op jit(solution)/shard_map/ppermute | solution.py:45
  121.0 22.2 %collective-permute-done.4 = bf16[8,32,512]{2,1,0:T(8,128)(2,1)} collective-permute-done((bf16[8,32,512]{2,1,0:T(8,128)(2,1)S(1)}, bf16[8,32,512]{2,1,0:T(8,128)(2,1)}, u32[]{:S(2)}, u32[]{:S(2)}) %collective-permute-start.4) | collective-permute-done | bytes 262176 | tf_op jit(solution)/shard_map/ppermute | solution.py:45
  143.3 1.7 bitcast_select_fusion.1
  145.0 1.7 reshape.66
  146.7 0.8 reshape.67
  147.4 1.4 pad_maximum_fusion
  148.9 1.1 copy.12
  150.0 0.0 all-to-all-done.3
  150.0 2.5 %convolution_convert_fusion.1 = bf16[256,1024]{1,0:T(8,128)(2,1)S(1)} fusion(bf16[256,1024]{0,1:T(8,128)(2,1)} %bitcast.67, bf16[1024,1024]{1,0:T(8,128)(2,1)} %bitcast.19), kind=kOutput, calls=%fused_computation.4 | convolution fusion | flops 537133056 | bytes 3145728 | tf_op jit(solution)/shard_map/dot_general | solution.py:14
  152.5 29.6 %all_to_all.50 = bf16[8,32,1024]{2,1,0:T(8,128)(2,1)S(1)} all-to-all(bf16[8,32,1024]{2,1,0:T(8,128)(2,1)S(1)} %bitcast.68), channel_id=1, replica_groups=mesh['tok'=8,'yh'=4,'core'=2,'x'=4,'yl'=2] {'tok'}, dimensions={0} | all-to-all | bytes 1048576 | tf_op jit(solution)/shard_map/all_to_all | solution.py:23
  182.0 0.1 reduce_sum.47
  182.1 0.1 broadcast_in_dim.8
  182.2 11.0 %all_to_all.51 = bf16[8,32,1024]{2,1,0:T(8,128)(2,1)S(1)} all-to-all(bf16[8,32,1024]{2,1,0:T(8,128)(2,1)S(1)} %broadcast_in_dim.8), channel_id=1, replica_groups=mesh['tok'=8,'yh'=4,'core'=2,'x'=4,'yl'=2] {'x','yl'}, dimensions={0} | all-to-all | bytes 1048576 | tf_op jit(solution)/shard_map/all_to_all | solution.py:23
  193.2 0.7 fusion
  194.1 7.2 %all-gather.1 = bf16[8,32,1024]{2,1,0:T(8,128)(2,1)S(1)} all-gather(bf16[4,32,1024]{2,1,0:T(8,128)(2,1)S(1)} %fusion.8), channel_id=3, replica_groups=mesh['tok'=8,'yh'=4,'core'=2,'x'=4,'yl'=2] {'core'}, dimensions={0}, use_global_device_ids=true | all-gather | bytes 786432 | tf_op jit(solution)/shard_map/all_gather | solution.py:52
  201.2 0.8 fusion.4
  202.0 3.4 %all-to-all-start.6 = ((bf16[4,32,1024]{2,1,0:T(8,128)(2,1)}), bf16[4,32,1024]{2,1,0:T(8,128)(2,1)S(1)}, u32[]{:S(2)}, u32[]{:S(2)}) async-start(bf16[4,32,1024]{2,1,0:T(8,128)(2,1)} %fusion.4), calls=%async_computation.6 | async-start | bytes 524288 | tf_op jit(solution)/shard_map/all_to_all | solution.py:23
  205.5 1.0 copy.13
  206.5 7.9 %all-to-all-done.6 = bf16[4,32,1024]{2,1,0:T(8,128)(2,1)S(1)} async-done(((bf16[4,32,1024]{2,1,0:T(8,128)(2,1)}), bf16[4,32,1024]{2,1,0:T(8,128)(2,1)S(1)}, u32[]{:S(2)}, u32[]{:S(2)}) %all-to-all-start.6) | async-done | bytes 262176 | tf_op jit(solution)/shard_map/all_to_all | solution.py:23
  214.4 18.1 %all_gather.31 = bf16[256,1024]{1,0:T(8,128)(2,1)S(1)} all-gather(bf16[32,1024]{1,0:T(8,128)(2,1)S(1)} %reduce_sum.48), channel_id=1, replica_groups=mesh['tok'=8,'yh'=4,'core'=2,'x'=4,'yl'=2] {'yh','core'}, dimensions={0}, use_global_device_ids=true | all-gather | bytes 589824 | tf_op jit(solution)/shard_map/all_gather | solution.py:108
  232.6 0.8 copy.17
  (8 shorter events, 0.3 us)
Async XLA Ops:
  7.2 13.8 %copy-start = (bf16[1024,1024]{1,0:T(8,128)(2,1)S(1)}, bf16[1024,1024]{1,0:T(8,128)(2,1)}, u32[]{:S(2)}) copy-start(bf16[1024,1024]{1,0:T(8,128)(2,1)} %param.8) | copy-start | bytes 6291460
  7.2 40.6 %all-gather.5.cloned.1.call-start = ((), (), s32[]{:S(2)}) async-start(), calls=%async_computation.7 | async-start | bytes 1310720 | tf_op jit(solution)/shard_map/all_gather | solution.py:82
  10.0 40.0 %all-to-all-start = ((bf16[8,64,1024]{2,1,0:T(8,128)(2,1)}), bf16[8,64,1024]{2,1,0:T(8,128)(2,1)S(1)}, u32[]{:S(2)}, u32[]{:S(2)}) async-start(bf16[8,64,1024]{2,1,0:T(8,128)(2,1)} %broadcast_in_dim.6), calls=%async_computation | async-start | bytes 2097152 | tf_op jit(solution)/shard_map/all_to_all | solution.py:23
  20.8 70.1 %all-gather.7.cloned.1.call-start = ((), (), s32[]{:S(2)}) async-start(), calls=%async_computation.8 | async-start | bytes 1179648 | tf_op jit(solution)/shard_map/all_gather | solution.py:89
  22.7 0.8 copy-start.1
  24.2 9.9 %collective-permute-start = (bf16[64,1024]{1,0:T(8,128)(2,1)}, bf16[64,1024]{1,0:T(8,128)(2,1)S(1)}, u32[]{:S(2)}, u32[]{:S(2)}) collective-permute-start(bf16[64,1024]{1,0:T(8,128)(2,1)} %get-tuple-element.18), channel_id=1, source_target_pairs={{0,4},{2,6},{4,0},{6,2},{1,5},{3,7},{5,1},{7,3},{8,12},{10,14},{12... | collective-permute-start | bytes 393224 | tf_op jit(solution)/shard_map/ppermute | solution.py:45
  28.9 9.6 %collective-permute-start.2 = (bf16[64,1024]{1,0:T(8,128)(2,1)}, bf16[64,1024]{1,0:T(8,128)(2,1)S(1)}, u32[]{:S(2)}, u32[]{:S(2)}) collective-permute-start(bf16[64,1024]{1,0:T(8,128)(2,1)} %get-tuple-element.19), channel_id=1, source_target_pairs={{0,6},{2,0},{4,2},{6,4},{1,7},{3,1},{5,3},{7,5},{8,14},{10,8},{12,... | collective-permute-start | bytes 393224 | tf_op jit(solution)/shard_map/ppermute | solution.py:45
  31.6 7.4 %collective-permute-start.1 = (bf16[64,1024]{1,0:T(8,128)(2,1)}, bf16[64,1024]{1,0:T(8,128)(2,1)S(1)}, u32[]{:S(2)}, u32[]{:S(2)}) collective-permute-start(bf16[64,1024]{1,0:T(8,128)(2,1)} %get-tuple-element.20), channel_id=1, source_target_pairs={{0,2},{2,4},{4,6},{6,0},{1,3},{3,5},{5,7},{7,1},{8,10},{10,12},{12... | collective-permute-start | bytes 393224 | tf_op jit(solution)/shard_map/ppermute | solution.py:45
  40.1 6.0 %collective-permute-start.3 = (bf16[64,1024]{1,0:T(8,128)(2,1)S(1)}, bf16[64,1024]{1,0:T(8,128)(2,1)S(1)}, u32[]{:S(2)}, u32[]{:S(2)}) collective-permute-start(bf16[64,1024]{1,0:T(8,128)(2,1)S(1)} %fusion.11), channel_id=1, source_target_pairs={{0,1},{1,0},{2,3},{3,2},{4,5},{5,4},{6,7},{7,6},{8,9},{9,8},{10,11... | collective-permute-start | bytes 393224 | tf_op jit(solution)/shard_map/ppermute | solution.py:45
  91.0 7.3 %copy-start.2 = (f32[1024,128]{1,0:T(8,128)S(1)}, f32[1024,128]{1,0:T(8,128)}, u32[]{:S(2)}) copy-start(f32[1024,128]{1,0:T(8,128)} %param.9) | copy-start | bytes 1572868
  94.0 15.2 %all-to-all-start.2 = ((bf16[4,128,1024]{2,1,0:T(8,128)(2,1)}), bf16[4,128,1024]{2,1,0:T(8,128)(2,1)}, u32[]{:S(2)}, u32[]{:S(2)}) async-start(bf16[4,128,1024]{2,1,0:T(8,128)(2,1)} %bitcast.72), calls=%async_computation.2 | async-start | bytes 2097152 | tf_op jit(solution)/shard_map/all_to_all | solution.py:23
  113.4 36.6 %all-to-all-start.3 = ((bf16[8,128,1024]{2,1,0:T(8,128)(2,1)}), bf16[8,128,1024]{2,1,0:T(8,128)(2,1)}, u32[]{:S(2)}, u32[]{:S(2)}) async-start(bf16[8,128,1024]{2,1,0:T(8,128)(2,1)} %broadcast_in_dim.7), calls=%async_computation.3 | async-start | bytes 4194304 | tf_op jit(solution)/shard_map/all_to_all | solution.py:23
  117.8 25.5 %collective-permute-start.4 = (bf16[8,32,512]{2,1,0:T(8,128)(2,1)S(1)}, bf16[8,32,512]{2,1,0:T(8,128)(2,1)}, u32[]{:S(2)}, u32[]{:S(2)}) collective-permute-start(bf16[8,32,512]{2,1,0:T(8,128)(2,1)S(1)} %dynamic-slice_bitcast_fusion.2), channel_id=1, source_target_pairs={{0,1},{1,0},{2,3},{3,2},{4,5},{5,4},{6,7},{7,6},{8,9},{9,8},{10,11... | collective-permute-start | bytes 786440 | tf_op jit(solution)/shard_map/ppermute | solution.py:45
  202.0 12.4 %all-to-all-start.6 = ((bf16[4,32,1024]{2,1,0:T(8,128)(2,1)}), bf16[4,32,1024]{2,1,0:T(8,128)(2,1)S(1)}, u32[]{:S(2)}, u32[]{:S(2)}) async-start(bf16[4,32,1024]{2,1,0:T(8,128)(2,1)} %fusion.4), calls=%async_computation.6 | async-start | bytes 524288 | tf_op jit(solution)/shard_map/all_to_all | solution.py:23
Sparse Core Ops, SparseCore 0:
  10.1 37.1 all-gather.4
  49.9 39.1 all-gather.6

commit v8 on v3

--- a/solution.py
+++ b/solution.py
@@ -55,10 +55,9 @@
 def ring_sum(blocks, axis):
     mine = lax.axis_index(axis)
     members = lax.axis_size(axis)
-    sent = blocks.astype(narrow)
-    total = pick(blocks, mine, 0)
-    for step in range(1, members):
-        total = total + shifted(pick(sent, (mine + step) % members, 0), axis, step).astype(wide)
+    total = pick(blocks, mine, 0).astype(wide)
+    for step in sorted(range(1, members), key=lambda step: abs(2 * step - members)):
+        total = total + shifted(pick(blocks, (mine + step) % members, 0), axis, step).astype(wide)
     return total
 
 
@@ -68,11 +67,12 @@
 
     own_rows = lax.dynamic_slice_in_dim(activations, lax.axis_index("x") * slab, slab, 0)
     act_rows = spread(own_rows, "tok")
-    grad_part = contract(gradients, grad_basis, 1, 0)
+    grad_part = contract(gradients, grad_basis, 1, 0).astype(narrow)
     grad_part = grad_part.reshape(-1, slab, grad_part.shape[1])
     basis = lax.all_gather(act_basis, "x", axis=1, tiled=True)
     grad_half = ring_sum(grad_part, "x")
-    grad_proj = grad_half + shifted(grad_half.astype(narrow), "yl", 1).astype(wide)
+    both = lax.all_gather(grad_half.astype(narrow), "yl")
+    grad_proj = grad_half + pick(both, 1 - lax.axis_index("yl"), 0).astype(wide)
     grad_sq = (grad_proj * grad_proj).astype(narrow)
 
     act_halves = pair_sum(contract(act_rows, basis, 1, 0), "core")

time: 215 us -> 213 us (level)
  blocking collectives: 120 us -> 124 us
  waiting for transfers between devices: 26.3 us -> 23.5 us
  starting transfers between devices: 31.8 us -> 29.2 us
    ppermute x4 -> x3, waiting for transfers between devices: 9.13 us -> 4.24 us  [shifted(): lax.ppermute(block, axis, [(i, (i + step) % members) for i in range(membe...]
    all_gather x0 -> x1, blocking collectives: none -> 4.82 us  [plan(): both = lax.all_gather(grad_half.astype(narrow), 'yl')]
    ppermute x4 -> x3, starting transfers between devices: 13.9 us -> 11.1 us  [shifted(): lax.ppermute(block, axis, [(i, (i + step) % members) for i in range(membe...]
    unnamed x11 -> x13, local copies, waits for them, and re-layouts: 3.85 us -> 4.63 us
  transfers between devices with their start and end apart: 9 -> 8, of which waited for: 6 -> 5; matrix products, arithmetic and copies ran while one was open for 6% -> 6% of each run, Pallas kernels for 0% -> 0%
where the time goes in v8:
time: 213 us; the launch traced here: 212 us
  blocking collectives  124 us (58%)
  starting transfers between devices  29.2 us (14%)
  waiting for transfers between devices  23.5 us (11%)
  between operations  14.3 us (7%)
  matrix products  8.26 us (4%)
  local copies, waits for them, and re-layouts  7.78 us (4%)
  other arithmetic  5.89 us (3%)
    all_to_all x4, blocking collectives, exchange(): return lax.all_to_all(blocks, axes, 0, 0, tiled=True)  74.8 us
    all_gather x1, blocking collectives, plan(): output_shift = lax.all_gather(shift, row, axis=0, tiled=True)  18.1 us
    all_to_all x3, starting transfers between devices, exchange(): return lax.all_to_all(blocks, axes, 0, 0, tiled=True)  18 us
    all_gather x1, blocking collectives, plan(): act_half = lax.all_gather(act_proj.astype(narrow), row, axis=0, tiled=True)  17.6 us
    all_to_all x3, waiting for transfers between devices, exchange(): return lax.all_to_all(blocks, axes, 0, 0, tiled=True)  17 us
    ppermute x3, starting transfers between devices, shifted(): lax.ppermute(block, axis, [(i, (i + step) % members) for i in range(membe...  11.1 us
    dot_general x5, matrix products, contract(): lax.dot_general(former, latter, (((former_dim,), (latter_dim,)), ((), ())...  8.26 us
    all_gather x2, blocking collectives, pair_sum(): return kept + pick(lax.all_gather(sent, axis), 1 - mine, 0).astype(wide)  8.19 us
  transfers between devices with their start and end apart: 8, of which 5 were waited for; matrix products, arithmetic and copies ran while one was open for 6% of the time, Pallas kernels for 0%

profile of v8, /device:TPU:1, one launch (start us, length us, event | category | flops | bytes accessed | tf_op | source)
XLA Modules:
  0.0 212.4 jit_solution(16924007586407418382)
XLA Ops:
  7.2 0.0 copy-start
  7.2 0.0 all-gather.6.cloned.1.call-start
  7.2 0.7 all-gather.6.cloned.1.call-update
  7.9 0.9 constant_dynamic-slice_fusion
  8.8 1.1 broadcast_in_dim.6
  10.0 10.9 %all-to-all-start = ((bf16[8,64,1024]{2,1,0:T(8,128)(2,1)}), bf16[8,64,1024]{2,1,0:T(8,128)(2,1)S(1)}, u32[]{:S(2)}, u32[]{:S(2)}) async-start(bf16[8,64,1024]{2,1,0:T(8,128)(2,1)} %broadcast_in_dim.6), calls=%async_computation | async-start | bytes 2097152 | tf_op jit(solution)/shard_map/all_to_all | solution.py:23
  20.8 0.0 all-gather.8.cloned.1.call-start
  20.9 0.0 copy-done
  20.9 1.8 convolution_convert_fusion.2
  22.7 0.0 copy-start.2
  22.7 0.8 copy-done.2
  23.5 0.7 dynamic-slice_bitcast_fusion.4
  24.2 4.6 %collective-permute-start = (bf16[64,1024]{1,0:T(8,128)(2,1)}, bf16[64,1024]{1,0:T(8,128)(2,1)S(1)}, u32[]{:S(2)}, u32[]{:S(2)}) collective-permute-start(bf16[64,1024]{1,0:T(8,128)(2,1)} %get-tuple-element.14), channel_id=1, source_target_pairs={{0,4},{2,6},{4,0},{6,2},{1,5},{3,7},{5,1},{7,3},{8,12},{10,14},{12... | collective-permute-start | bytes 393224 | tf_op jit(solution)/shard_map/ppermute | solution.py:45
  28.9 2.2 %collective-permute-start.1 = (bf16[64,1024]{1,0:T(8,128)(2,1)}, bf16[64,1024]{1,0:T(8,128)(2,1)S(1)}, u32[]{:S(2)}, u32[]{:S(2)}) collective-permute-start(bf16[64,1024]{1,0:T(8,128)(2,1)} %get-tuple-element.16), channel_id=1, source_target_pairs={{0,2},{2,4},{4,6},{6,0},{1,3},{3,5},{5,7},{7,1},{8,10},{10,12},{12... | collective-permute-start | bytes 393224 | tf_op jit(solution)/shard_map/ppermute | solution.py:45
  31.1 4.3 %collective-permute-start.2 = (bf16[64,1024]{1,0:T(8,128)(2,1)}, bf16[64,1024]{1,0:T(8,128)(2,1)S(1)}, u32[]{:S(2)}, u32[]{:S(2)}) collective-permute-start(bf16[64,1024]{1,0:T(8,128)(2,1)} %get-tuple-element.15), channel_id=1, source_target_pairs={{0,6},{2,0},{4,2},{6,4},{1,7},{3,1},{5,3},{7,5},{8,14},{10,8},{12,... | collective-permute-start | bytes 393224 | tf_op jit(solution)/shard_map/ppermute | solution.py:45
  35.4 0.0 collective-permute-done
  35.4 4.2 %collective-permute-done.1 = bf16[64,1024]{1,0:T(8,128)(2,1)S(1)} collective-permute-done((bf16[64,1024]{1,0:T(8,128)(2,1)}, bf16[64,1024]{1,0:T(8,128)(2,1)S(1)}, u32[]{:S(2)}, u32[]{:S(2)}) %collective-permute-start.1) | collective-permute-done | bytes 131104 | tf_op jit(solution)/shard_map/ppermute | solution.py:45
  39.7 0.0 collective-permute-done.2
  39.7 1.0 fusion.13
  40.6 4.8 %all-gather.1 = bf16[128,1024]{1,0:T(8,128)(2,1)S(1)} all-gather(bf16[64,1024]{1,0:T(8,128)(2,1)S(1)} %fusion.13), channel_id=3, replica_groups=mesh['tok'=8,'yh'=4,'core'=2,'x'=4,'yl'=2] {'yl'}, dimensions={0}, use_global_device_ids=true | all-gather | bytes 393216 | tf_op jit(solution)/shard_map/all_gather | solution.py:74
  45.5 1.7 fusion.10
  47.1 0.0 all-gather.8.cloned.1.call-update
  47.1 1.6 all-gather.6.cloned.1.call-done
  48.7 1.3 all-to-all-done
  50.0 1.9 fusion.2
  52.1 2.8 %all-gather = bf16[8,64,512]{2,1,0:T(8,128)(2,1)S(1)} all-gather(bf16[4,64,512]{2,1,0:T(8,128)(2,1)S(1)} %fusion.7), channel_id=2, replica_groups=mesh['tok'=8,'yh'=4,'core'=2,'x'=4,'yl'=2] {'core'}, dimensions={0}, use_global_device_ids=true | all-gather | bytes 786432 | tf_op jit(solution)/shard_map/all_gather | solution.py:52
  54.9 0.1 fusion.5
  54.9 16.4 %all_to_all.49 = bf16[4,64,512]{2,1,0:T(8,128)(2,1)S(1)} all-to-all(bf16[4,64,512]{2,1,0:T(8,128)(2,1)S(1)} %fusion.5), channel_id=1, replica_groups=mesh['tok'=8,'yh'=4,'core'=2,'x'=4,'yl'=2] {'yh'}, dimensions={0} | all-to-all | bytes 524288 | tf_op jit(solution)/shard_map/all_to_all | solution.py:23
  71.3 17.6 %all_gather.33 = bf16[512,512]{1,0:T(8,128)(2,1)S(1)} all-gather(bf16[64,512]{1,0:T(8,128)(2,1)S(1)} %reduce_sum.45), channel_id=1, replica_groups=mesh['tok'=8,'yh'=4,'core'=2,'x'=4,'yl'=2] {'yh','core'}, dimensions={0}, use_global_device_ids=true | all-gather | bytes 589824 | tf_op jit(solution)/shard_map/all_gather | solution.py:81
  89.0 0.0 copy-start.3
  89.0 0.0 all-gather.8.cloned.1.call-done
  89.0 3.1 %convolution_convert_fusion.1 = bf16[512,1024]{1,0:T(8,128)(2,1)} fusion(bf16[512,1024]{1,0:T(8,128)(2,1)} %all-gather.8.cloned.1.call-done, bf16[512,512]{1,0:T(8,128)(2,1)S(1)} %all_gather.33), kind=kOutput, calls=%fused_computation.4 | convolution fusion | flops 538181632 | bytes 2621440 | tf_op jit(solution)/shard_map/dot_general | solution.py:14
  92.1 0.0 copy-done.3
  92.1 3.7 %all-to-all-start.2 = ((bf16[4,128,1024]{2,1,0:T(8,128)(2,1)}), bf16[4,128,1024]{2,1,0:T(8,128)(2,1)S(1)}, u32[]{:S(2)}, u32[]{:S(2)}) async-start(bf16[4,128,1024]{2,1,0:T(8,128)(2,1)} %bitcast.65), calls=%async_computation.2 | async-start | bytes 2097152 | tf_op jit(solution)/shard_map/all_to_all | solution.py:23
  95.8 2.0 copy.8
  97.8 7.7 %all-to-all-done.2 = bf16[4,128,1024]{2,1,0:T(8,128)(2,1)S(1)} async-done(((bf16[4,128,1024]{2,1,0:T(8,128)(2,1)}), bf16[4,128,1024]{2,1,0:T(8,128)(2,1)S(1)}, u32[]{:S(2)}, u32[]{:S(2)}) %all-to-all-start.2) | async-done | bytes 1048608 | tf_op jit(solution)/shard_map/all_to_all | solution.py:23
  105.6 0.2 convert_reduce_fusion
  105.7 1.9 fusion.6
  107.7 0.0 copy-start.4
  107.7 0.1 broadcast_in_dim.7
  107.8 12.3 %all_to_all.50 = bf16[4,128,1024]{2,1,0:T(8,128)(2,1)S(1)} all-to-all(bf16[4,128,1024]{2,1,0:T(8,128)(2,1)S(1)} %broadcast_in_dim.7), channel_id=1, replica_groups=mesh['tok'=8,'yh'=4,'core'=2,'x'=4,'yl'=2] {'x'}, dimensions={0} | all-to-all | bytes 2097152 | tf_op jit(solution)/shard_map/all_to_all | solution.py:23
  120.1 0.0 copy-done.4
  120.1 0.7 convolution_convert_fusion
  120.8 34.7 %all_to_all.51 = bf16[16,32,1024]{2,1,0:T(8,128)(2,1)S(1)} all-to-all(bf16[16,32,1024]{2,1,0:T(8,128)(2,1)S(1)} %bitcast.67), channel_id=1, replica_groups=mesh['tok'=8,'yh'=4,'core'=2,'x'=4,'yl'=2] {'tok','yl'}, dimensions={0} | all-to-all | bytes 2097152 | tf_op jit(solution)/shard_map/all_to_all | solution.py:23
  155.5 0.2 reduce_sum.47
  155.7 0.1 broadcast_in_dim.8
  155.8 11.4 %all_to_all.52 = bf16[8,32,1024]{2,1,0:T(8,128)(2,1)S(1)} all-to-all(bf16[8,32,1024]{2,1,0:T(8,128)(2,1)S(1)} %broadcast_in_dim.8), channel_id=1, replica_groups=mesh['tok'=8,'yh'=4,'core'=2,'x'=4,'yl'=2] {'x','yl'}, dimensions={0} | all-to-all | bytes 1048576 | tf_op jit(solution)/shard_map/all_to_all | solution.py:23
  167.2 0.7 fusion
  168.0 0.0 copy-start.1
  168.1 5.4 %all-gather.2 = bf16[8,32,1024]{2,1,0:T(8,128)(2,1)S(1)} all-gather(bf16[4,32,1024]{2,1,0:T(8,128)(2,1)S(1)} %fusion.8), channel_id=4, replica_groups=mesh['tok'=8,'yh'=4,'core'=2,'x'=4,'yl'=2] {'core'}, dimensions={0}, use_global_device_ids=true | all-gather | bytes 786432 | tf_op jit(solution)/shard_map/all_gather | solution.py:52
  173.5 0.8 fusion.4
  174.2 3.4 %all-to-all-start.6 = ((bf16[4,32,1024]{2,1,0:T(8,128)(2,1)}), bf16[4,32,1024]{2,1,0:T(8,128)(2,1)S(1)}, u32[]{:S(2)}, u32[]{:S(2)}) async-start(bf16[4,32,1024]{2,1,0:T(8,128)(2,1)} %fusion.4), calls=%async_computation.6 | async-start | bytes 524288 | tf_op jit(solution)/shard_map/all_to_all | solution.py:23
  177.6 0.0 copy-done.1
  177.7 1.0 copy.9
  178.7 8.0 %all-to-all-done.6 = bf16[4,32,1024]{2,1,0:T(8,128)(2,1)S(1)} async-done(((bf16[4,32,1024]{2,1,0:T(8,128)(2,1)}), bf16[4,32,1024]{2,1,0:T(8,128)(2,1)S(1)}, u32[]{:S(2)}, u32[]{:S(2)}) %all-to-all-start.6) | async-done | bytes 262176 | tf_op jit(solution)/shard_map/all_to_all | solution.py:23
  186.6 18.1 %all_gather.39 = bf16[256,1024]{1,0:T(8,128)(2,1)S(1)} all-gather(bf16[32,1024]{1,0:T(8,128)(2,1)S(1)} %reduce_sum.48), channel_id=1, replica_groups=mesh['tok'=8,'yh'=4,'core'=2,'x'=4,'yl'=2] {'yh','core'}, dimensions={0}, use_global_device_ids=true | all-gather | bytes 589824 | tf_op jit(solution)/shard_map/all_gather | solution.py:93
  204.8 0.8 copy.13
  (6 shorter events, 0.2 us)
Async XLA Ops:
  7.2 13.8 %copy-start = (bf16[1024,1024]{1,0:T(8,128)(2,1)S(1)}, bf16[1024,1024]{1,0:T(8,128)(2,1)}, u32[]{:S(2)}) copy-start(bf16[1024,1024]{1,0:T(8,128)(2,1)} %param.8) | copy-start | bytes 6291460
  7.2 41.5 %all-gather.6.cloned.1.call-start = ((), (), s32[]{:S(2)}) async-start(), calls=%async_computation.7 | async-start | bytes 1310720 | tf_op jit(solution)/shard_map/all_gather | solution.py:72
  10.0 40.0 %all-to-all-start = ((bf16[8,64,1024]{2,1,0:T(8,128)(2,1)}), bf16[8,64,1024]{2,1,0:T(8,128)(2,1)S(1)}, u32[]{:S(2)}, u32[]{:S(2)}) async-start(bf16[8,64,1024]{2,1,0:T(8,128)(2,1)} %broadcast_in_dim.6), calls=%async_computation | async-start | bytes 2097152 | tf_op jit(solution)/shard_map/all_to_all | solution.py:23
  20.8 68.1 %all-gather.8.cloned.1.call-start = ((), (), s32[]{:S(2)}) async-start(), calls=%async_computation.8 | async-start | bytes 1179648 | tf_op jit(solution)/shard_map/all_gather | solution.py:80
  22.7 0.8 copy-start.2
  24.2 11.2 %collective-permute-start = (bf16[64,1024]{1,0:T(8,128)(2,1)}, bf16[64,1024]{1,0:T(8,128)(2,1)S(1)}, u32[]{:S(2)}, u32[]{:S(2)}) collective-permute-start(bf16[64,1024]{1,0:T(8,128)(2,1)} %get-tuple-element.14), channel_id=1, source_target_pairs={{0,4},{2,6},{4,0},{6,2},{1,5},{3,7},{5,1},{7,3},{8,12},{10,14},{12... | collective-permute-start | bytes 393224 | tf_op jit(solution)/shard_map/ppermute | solution.py:45
  28.9 10.8 %collective-permute-start.1 = (bf16[64,1024]{1,0:T(8,128)(2,1)}, bf16[64,1024]{1,0:T(8,128)(2,1)S(1)}, u32[]{:S(2)}, u32[]{:S(2)}) collective-permute-start(bf16[64,1024]{1,0:T(8,128)(2,1)} %get-tuple-element.16), channel_id=1, source_target_pairs={{0,2},{2,4},{4,6},{6,0},{1,3},{3,5},{5,7},{7,1},{8,10},{10,12},{12... | collective-permute-start | bytes 393224 | tf_op jit(solution)/shard_map/ppermute | solution.py:45
  31.1 8.5 %collective-permute-start.2 = (bf16[64,1024]{1,0:T(8,128)(2,1)}, bf16[64,1024]{1,0:T(8,128)(2,1)S(1)}, u32[]{:S(2)}, u32[]{:S(2)}) collective-permute-start(bf16[64,1024]{1,0:T(8,128)(2,1)} %get-tuple-element.15), channel_id=1, source_target_pairs={{0,6},{2,0},{4,2},{6,4},{1,7},{3,1},{5,3},{7,5},{8,14},{10,8},{12,... | collective-permute-start | bytes 393224 | tf_op jit(solution)/shard_map/ppermute | solution.py:45
  89.0 3.1 %copy-start.3 = (bf16[512,512]{1,0:T(8,128)(2,1)}, bf16[512,512]{1,0:T(8,128)(2,1)S(1)}, u32[]{:S(2)}) copy-start(bf16[512,512]{1,0:T(8,128)(2,1)S(1)} %all_gather.33) | copy-start | bytes 1572868
  92.1 13.5 %all-to-all-start.2 = ((bf16[4,128,1024]{2,1,0:T(8,128)(2,1)}), bf16[4,128,1024]{2,1,0:T(8,128)(2,1)S(1)}, u32[]{:S(2)}, u32[]{:S(2)}) async-start(bf16[4,128,1024]{2,1,0:T(8,128)(2,1)} %bitcast.65), calls=%async_computation.2 | async-start | bytes 2097152 | tf_op jit(solution)/shard_map/all_to_all | solution.py:23
  107.7 12.4 %copy-start.4 = (bf16[512,512]{1,0:T(8,128)(2,1)S(1)}, bf16[512,512]{1,0:T(8,128)(2,1)}, u32[]{:S(2)}) copy-start(bf16[512,512]{1,0:T(8,128)(2,1)} %copy-done.3) | copy-start | bytes 1572868
  168.0 9.7 %copy-start.1 = (f32[1024,128]{0,1:T(8,128)S(1)}, f32[1024,128]{0,1:T(8,128)}, u32[]{:S(2)}) copy-start(f32[1024,128]{0,1:T(8,128)} %get-tuple-element.13) | copy-start | bytes 1572868
  174.2 12.4 %all-to-all-start.6 = ((bf16[4,32,1024]{2,1,0:T(8,128)(2,1)}), bf16[4,32,1024]{2,1,0:T(8,128)(2,1)S(1)}, u32[]{:S(2)}, u32[]{:S(2)}) async-start(bf16[4,32,1024]{2,1,0:T(8,128)(2,1)} %fusion.4), calls=%async_computation.6 | async-start | bytes 524288 | tf_op jit(solution)/shard_map/all_to_all | solution.py:23
Sparse Core Ops, SparseCore 0:
  10.1 38.5 all-gather.5
  50.8 37.4 all-gather.7
